TPU v7x, 256 devices: a whole 4x4x8 slice. The times are simulated.
256 devices in a mesh: dp: 64 (over x, z, core), fsdp: 4 (over y).
Axes of the slice: x: 4, y: 4, z: 8, core: 2. Of those that a mesh axis runs over, the one named last changes fastest.
Arguments:
- acts: bfloat16 [131072, 4096], P(('dp', 'fsdp')), may hold values from -6 to 6
- cotangent: bfloat16 [131072, 512], P(('dp', 'fsdp')), may hold values from -6 to 6
- weight: bfloat16 [4096, 512], P('fsdp'), may hold values from -0.09375 to 0.09375
- error_buf: float32 [64, 4096, 512], P('dp', 'fsdp'), may hold values from -100 to 100, as said below
- q_init: float32 [512, 64], replicated, may hold values from -6 to 6
- inv_scale: float32 [], replicated, may hold values from 0.011048543 to 0.022097087
Outputs:
- input_grad: bfloat16 [131072, 4096], P(('dp', 'fsdp'))
- approx: float32 [4096, 512], P('fsdp')
- new_error: float32 [64, 4096, 512], P('dp', 'fsdp')
- q_next: float32 [512, 64], replicated
Inputs may be any that keep to these rules, and one draw needn't show every extreme that they name: `error_buf`: error feedback carried from the previous step.
All inputs are finite; a program needn't handle non-finite values.
Results may differ from a plain program's by a relative error of at most 0.0033.
Values may be sent and summed in bfloat16 or wider, within the bound.
No kernel may reach another device: no remote copies, remote signals or barrier semaphores. Data moves between devices by JAX's collectives and lax.ppermute only.
A program may use at most 64 MiB of HBM per device.

v0:
```python
import jax
import jax.numpy as jnp
from jax import lax
from jax.sharding import PartitionSpec as P

ITERS = 2


def orient(lower, factor):
    return lax.linalg.triangular_solve(lower, factor, left_side=False, lower=True, transpose_a=True)


def body(acts, cotangent, weight, error_buf, q_init, inv_scale):
    part_grad = jnp.einsum(
        "tk,rk->tr",
        cotangent,
        lax.all_gather(weight, "fsdp", axis=0, tiled=True),
        preferred_element_type=jnp.float32,
    )
    input_grad = part_grad.astype(jnp.bfloat16)
    grad_shard = lax.psum_scatter(
        jnp.einsum("tr,tk->rk", acts, cotangent, preferred_element_type=jnp.float32).astype(
            jnp.bfloat16
        ),
        "fsdp",
        scatter_dimension=0,
        tiled=True,
    ).astype(jnp.float32)
    merged = error_buf[0] + inv_scale * grad_shard
    replicas = lax.axis_size("dp")
    highest = lax.Precision.HIGHEST
    factor_q = q_init
    p_hat = None
    for step in range(ITERS):
        local_p = jnp.dot(merged, factor_q, precision=highest)
        factor_p = lax.psum(local_p, "dp") / replicas
        gram = lax.psum(jnp.dot(factor_p.T, factor_p, precision=highest), "fsdp")
        lower = jnp.linalg.cholesky(gram)
        p_hat = orient(lower, factor_p)
        local_q = jnp.dot(merged.T, p_hat, precision=highest)
        factor_q = lax.psum(local_q, ("dp", "fsdp")) / replicas
    approx = jnp.dot(p_hat, factor_q.T, precision=highest)
    new_error = (merged - approx)[None]
    return (input_grad, approx, new_error, factor_q)


def solution(mesh):
    in_specs = (
        P(("dp", "fsdp"), None),
        P(("dp", "fsdp"), None),
        P("fsdp", None),
        P("dp", "fsdp", None),
        P(),
        P(),
    )
    out_specs = (P(("dp", "fsdp"), None), P("fsdp", None), P("dp", "fsdp", None), P())
    return jax.shard_map(body, mesh=mesh, in_specs=in_specs, out_specs=out_specs, check_vma=False)
```

profile of v0, /device:TPU:2, one launch (start us, length us, event | category | flops | bytes accessed | tf_op | source)
XLA Modules:
  0.0 1017.3 jit_solution(2975008801872365448)
XLA Ops:
  7.2 1.0 copy-done
  8.2 6.6 convolution_convert_fusion
  15.5 51.8 %reduce-scatter.2.cloned.1.call-done = bf16[1024,512]{1,0:T(8,128)(2,1)} async-done(((bf16[4096,512]{1,0:T(8,128)(2,1)}), bf16[1024,512]{1,0:T(8,128)(2,1)}) %reduce-scatter.2.cloned.1.call-update) | async-done | bytes 1048592 | tf_op jit(solution)/shard_map/reduce_scatter | solution.py:21
  67.3 2.2 bitcast_add_fusion
  69.5 2.9 fusion.26
  72.5 175.8 %all-reduce.5.cloned.1.call-done = f32[1024,64]{0,1:T(8,128)} async-done(((f32[1024,64]{0,1:T(8,128)}), f32[1024,64]{0,1:T(8,128)}) %all-reduce.5.cloned.1.call-update) | async-done | bytes 262160 | tf_op jit(solution)/shard_map/psum | solution.py:36
  248.3 1.4 fusion.4
  249.7 17.1 %psum.43 = f32[64,64]{0,1:T(8,128)S(1)} all-reduce(f32[64,64]{0,1:T(8,128)S(1)} %fusion.4), channel_id=1, replica_groups=mesh['dp'=64,'fsdp'=4] {'fsdp'}, use_global_device_ids=true, to_apply=%region_2.0 | all-reduce | flops 4096 | bytes 32768 | tf_op jit(solution)/shard_map/psum | solution.py:37
  266.9 5.8 cholesky.44
  272.8 0.6 compare_reduce_fusion.1
  273.4 0.7 fusion.13
  274.1 4.9 custom-call.6
  279.0 1.4 convolution_bitcast_fusion.1
  280.3 2.1 fusion.27
  282.5 243.2 %all-reduce.7.cloned.1.call-done = f32[512,64]{0,1:T(8,128)} async-done(((f32[512,64]{0,1:T(8,128)}), f32[512,64]{0,1:T(8,128)}) %all-reduce.7.cloned.1.call-update) | async-done | bytes 131088 | tf_op jit(solution)/shard_map/psum | solution.py:41
  525.7 3.8 fusion.6
  529.5 0.5 all-gather.2.cloned.1.call-update
  530.1 172.2 %all-reduce.9.cloned.1.call-done = f32[1024,64]{0,1:T(8,128)} async-done(((f32[1024,64]{0,1:T(8,128)}), f32[1024,64]{0,1:T(8,128)}) %all-reduce.9.cloned.1.call-update) | async-done | bytes 262160 | tf_op jit(solution)/shard_map/psum | solution.py:36
  702.4 1.4 fusion.1
  703.8 17.1 %psum.46 = f32[64,64]{0,1:T(8,128)S(1)} all-reduce(f32[64,64]{0,1:T(8,128)S(1)} %fusion.1), channel_id=1, replica_groups=mesh['dp'=64,'fsdp'=4] {'fsdp'}, use_global_device_ids=true, to_apply=%region_7.10 | all-reduce | flops 4096 | bytes 32768 | tf_op jit(solution)/shard_map/psum | solution.py:37
  720.9 5.8 cholesky.55
  726.8 0.6 compare_reduce_fusion
  727.5 0.7 fusion.14
  728.1 4.9 custom-call.7
  733.0 1.4 convolution_bitcast_fusion
  734.4 2.1 fusion.28
  736.6 17.1 %all-gather.2.cloned.1.call-done = bf16[4096,512]{1,0:T(8,128)(2,1)} async-done(((bf16[1024,512]{1,0:T(8,128)(2,1)}), bf16[4096,512]{1,0:T(8,128)(2,1)}) %all-gather.2.cloned.1.call-update) | async-done | bytes 4194320 | tf_op jit(solution)/shard_map/all_gather | solution.py:17
  753.6 6.6 convolution_convert_fusion.1
  760.2 245.5 %all-reduce.11.cloned.1.call-done = f32[512,64]{0,1:T(8,128)} async-done(((f32[512,64]{0,1:T(8,128)}), f32[512,64]{0,1:T(8,128)}) %all-reduce.11.cloned.1.call-update) | async-done | bytes 131088 | tf_op jit(solution)/shard_map/psum | solution.py:41
  1005.7 0.9 broadcast_multiply_fusion
  1006.6 1.8 fusion.29
  1008.5 2.0 subtract_bitcast_fusion
  (24 shorter events, 0.6 us)
Async XLA Ops:
  7.2 1.0 copy-start
  7.2 60.2 %reduce-scatter.2.cloned.1.call-start = ((), (), s32[]{:S(2)}) async-start(), calls=%async_computation.2 | async-start | bytes 5242880 | tf_op jit(solution)/shard_map/reduce_scatter | solution.py:21
  14.8 233.5 %all-reduce.5.cloned.1.call-start = ((), (), s32[]{:S(2)}) async-start(), calls=%async_computation.3 | async-start | bytes 524288 | tf_op jit(solution)/shard_map/psum | solution.py:36
  15.5 54.0 %copy-start.3 = (f32[512,64]{0,1:T(8,128)S(1)}, f32[512,64]{0,1:T(8,128)}, u32[]{:S(2)}) copy-start(f32[512,64]{0,1:T(8,128)} %param.13) | copy-start | bytes 393220
  72.4 453.3 %all-reduce.7.cloned.1.call-start = ((), (), s32[]{:S(2)}) async-start(), calls=%async_computation.4 | async-start | bytes 262144 | tf_op jit(solution)/shard_map/psum | solution.py:41
  282.5 419.9 %all-reduce.9.cloned.1.call-start = ((), (), s32[]{:S(2)}) async-start(), calls=%async_computation.5 | async-start | bytes 524288 | tf_op jit(solution)/shard_map/psum | solution.py:36
  529.5 224.2 %all-gather.2.cloned.1.call-start = ((), (), s32[]{:S(2)}) async-start(), calls=%async_computation.1 | async-start | bytes 5242880 | tf_op jit(solution)/shard_map/all_gather | solution.py:17
  530.1 475.6 %all-reduce.11.cloned.1.call-start = ((), (), s32[]{:S(2)}) async-start(), calls=%async_computation.6 | async-start | bytes 262144 | tf_op jit(solution)/shard_map/psum | solution.py:41
  1006.6 3.9 copy-start.2
  1008.5 2.0 copy-start.1
Sparse Core Ops, SparseCore 0:
  14.9 52.3 reduce-scatter.1
  72.6 175.7 all-reduce.4
  282.6 243.0 all-reduce.6
  529.6 172.7 all-reduce.8
  704.0 49.5 all-gather.1
  759.6 246.0 all-reduce.10
where the time goes:
time: 1020 us
  waiting for transfers between devices  906 us (89%)
  blocking collectives  34.1 us (3%)
  matrix products  31.4 us (3%)
  other arithmetic  29.3 us (3%)
  between operations  14.9 us (1%)
    psum x2, waiting for transfers between devices, body(): factor_q = lax.psum(local_q, ('dp', 'fsdp')) / replicas  489 us
    psum x2, waiting for transfers between devices, body(): factor_p = lax.psum(local_p, 'dp') / replicas  348 us
    reduce_scatter x1, waiting for transfers between devices, body(): lax.psum_scatter(jnp.einsum('tr,tk->rk', acts, cotangent, preferred_eleme...  51.8 us
    psum x2, blocking collectives, body(): gram = lax.psum(jnp.dot(factor_p.T, factor_p, precision=highest), 'fsdp')  34.1 us
  transfers between devices with their start and end apart: 6, of which 6 were waited for; matrix products, arithmetic and copies ran while one was open for 2% of the time, Pallas kernels for 0%

commit v1 on v0

v1 whole, which is shorter than its diff:
```python
import jax
import jax.numpy as jnp
from jax import lax
from jax.sharding import Mesh
from jax.sharding import PartitionSpec as P

ITERS = 2
NX, NZ, NC, NY = 4, 8, 2, 4
DP = ("x", "z", "core")
HI = lax.Precision.HIGHEST
f32, bf16 = jnp.float32, jnp.bfloat16
SWAP = [(0, 1), (1, 0)]


def dot(a, b, dims):
    return lax.dot_general(a, b, (dims, ((), ())), precision=HI, preferred_element_type=f32)


def gather_weight(weight, y, core):
    half = lax.dynamic_slice_in_dim(weight, core * 512, 512, 0)
    pieces = [half]
    for s in range(1, NY):
        pieces.append(lax.ppermute(half, "y", [(i, (i + s) % NY) for i in range(NY)]))
    mine = lax.concatenate([pieces[s] for s in (3, 2, 1, 0, 3, 2, 1)], 0)
    mine = lax.dynamic_slice_in_dim(mine, (NY - 1 - y) * 512, NY * 512, 0).reshape(NY, 512, 512)
    other = lax.ppermute(mine, "core", SWAP)
    low = jnp.where(core == 0, mine, other)
    high = jnp.where(core == 0, other, mine)
    return jnp.stack([low, high], axis=1).reshape(NY * 1024, 512)


def sum_y(t):
    got = lax.all_to_all(jnp.broadcast_to(t, (NY, *t.shape)), "y", 0, 0, tiled=True)
    return (got[0] + got[1]) + (got[2] + got[3])


def body(acts, cotangent, weight, error_buf, q_init, inv_scale):
    y, core = lax.axis_index("y"), lax.axis_index("core")
    part = jnp.einsum("tr,tk->rk", acts, cotangent, preferred_element_type=f32).astype(bf16)
    recv = lax.all_to_all(part.reshape(NY, 1024, 512), "y", 0, 0, tiled=True)
    recv, weight = lax.optimization_barrier((recv, weight))
    full_weight = gather_weight(weight, y, core)
    input_grad = jnp.einsum("tk,rk->tr", cotangent, full_weight, preferred_element_type=f32).astype(bf16)

    merged = error_buf[0] + inv_scale * jnp.sum(recv.astype(f32), axis=0)
    keep = lax.dynamic_slice_in_dim(merged, core * 512, 512, 0)
    give = lax.dynamic_slice_in_dim(merged, (1 - core) * 512, 512, 0).astype(bf16)
    pair = keep + lax.ppermute(give, "core", SWAP).astype(f32)
    terms = lax.all_to_all(pair.astype(bf16).reshape(NX * NZ, 16, 512), ("x", "z"), 0, 0, tiled=True)
    rows = jnp.sum(terms.astype(f32), axis=0) * (1.0 / (NX * NZ * NC))
    half = lax.all_to_all(jnp.broadcast_to(rows, (NX * NZ, 16, 512)), ("x", "z"), 0, 0, tiled=True)
    half = half.reshape(512, 512)
    other = lax.ppermute(half, "core", SWAP)
    mean = lax.concatenate([jnp.where(core == 0, half, other), jnp.where(core == 0, other, half)], 0)

    qt = q_init.T
    pt = None
    for step in range(ITERS):
        pt = dot(qt, mean, ((1,), (1,)))
        zt = dot(pt, mean, ((1,), (0,)))
        gram = dot(pt, pt, ((1,), (1,)))
        tot = sum_y(lax.concatenate([zt, jnp.pad(gram, ((0, 0), (0, 64)))], 1))
        zt, gram = tot[:, :512], tot[:, 512:576]
        lower = jnp.linalg.cholesky(gram)
        rhs = zt if step < ITERS - 1 else lax.concatenate([zt, pt], 1)
        sol = lax.linalg.triangular_solve(lower, rhs, left_side=True, lower=True)
        qt = sol[:, :512]
    pt = sol[:, 512:]
    approx = dot(pt, qt, ((0,), (0,)))
    new_error = (merged - approx)[None]
    return (input_grad, approx, new_error, qt.T)


def solution(mesh):
    fine = Mesh(mesh.devices.reshape(NX, NZ, NC, NY), ("x", "z", "core", "y"))
    every = P((*DP, "y"), None)
    in_specs = (every, every, P("y", None), P(DP, "y", None), P(), P())
    out_specs = (every, P("y", None), P(DP, "y", None), P())
    return jax.shard_map(body, mesh=fine, in_specs=in_specs, out_specs=out_specs, check_vma=False)
```

time: 1020 us -> 224 us (0.22)
  waiting for transfers between devices: 906 us -> 79.7 us
  local copies, waits for them, and re-layouts: 1.16 us -> 30 us
  starting transfers between devices: 0.24 us -> 21.8 us
  between operations: 14.9 us -> 1.6 us
    psum x4 -> x0, waiting for transfers between devices: 837 us -> none  [the longest x2 489 us: body(): factor_q = lax.psum(local_q, ('dp', 'fsdp')) / replicas]
    all_to_all x0 -> x4, waiting for transfers between devices: none -> 55.3 us  [the longest x1 48.5 us: body(): recv = lax.all_to_all(part.reshape(NY, 1024, 512), 'y', 0, 0, tiled=True)]
    reduce_scatter x1 -> x0, waiting for transfers between devices: 51.8 us -> none  [body(): lax.psum_scatter(jnp.einsum('tr,tk->rk', acts, cotangent, preferred_eleme...]
    psum x2 -> x0, blocking collectives: 34.1 us -> none  [body(): gram = lax.psum(jnp.dot(factor_p.T, factor_p, precision=highest), 'fsdp')]
    all_to_all x0 -> x1, blocking collectives: none -> 27.3 us  [body(): lax.all_to_all(pair.astype(bf16).reshape(NX * NZ, 16, 512), ('x', 'z'), 0...]
    ppermute x0 -> x6, waiting for transfers between devices: none -> 24.4 us  [the longest x3 22.3 us: gather_weight(): lax.ppermute(half, 'y', [(i, (i + s) % NY) for i in range(NY)])]
    all_to_all x0 -> x4, starting transfers between devices: none -> 18.9 us  [the longest x2 7.19 us: sum_y(): lax.all_to_all(jnp.broadcast_to(t, (NY, *t.shape)), 'y', 0, 0, tiled=True)]
    unnamed x8 -> x33, local copies, waits for them, and re-layouts: 1.01 us -> 18.6 us
  transfers between devices with their start and end apart: 6 -> 10, of which waited for: 6 -> 6; matrix products, arithmetic and copies ran while one was open for 2% -> 15% of each run, Pallas kernels for 0% -> 0%
where the time goes in v1:
time: 224 us; the launch traced here: 223 us
  waiting for transfers between devices  79.7 us (36%)
  other arithmetic  38 us (17%)
  local copies, waits for them, and re-layouts  30 us (13%)
  blocking collectives  27.3 us (12%)
  matrix products  24.6 us (11%)
  starting transfers between devices  21.8 us (10%)
    all_to_all x1, waiting for transfers between devices, body(): recv = lax.all_to_all(part.reshape(NY, 1024, 512), 'y', 0, 0, tiled=True)  48.5 us
    all_to_all x1, blocking collectives, body(): lax.all_to_all(pair.astype(bf16).reshape(NX * NZ, 16, 512), ('x', 'z'), 0...  27.3 us
    ppermute x3, waiting for transfers between devices, gather_weight(): lax.ppermute(half, 'y', [(i, (i + s) % NY) for i in range(NY)])  22.3 us
    unnamed x33, local copies, waits for them, and re-layouts  18.6 us
    another operation x6, other arithmetic, body(): lower = jnp.linalg.cholesky(gram)  13 us
    another operation x4, other arithmetic, body(): sol = lax.linalg.triangular_solve(lower, rhs, left_side=True, lower=True)  11.1 us
    dot_general x7, matrix products, dot(): lax.dot_general(a, b, (dims, ((), ())), precision=HI, preferred_element_t...  9.6 us
    all_to_all x2, starting transfers between devices, sum_y(): lax.all_to_all(jnp.broadcast_to(t, (NY, *t.shape)), 'y', 0, 0, tiled=True)  7.19 us
  transfers between devices with their start and end apart: 10, of which 6 were waited for; matrix products, arithmetic and copies ran while one was open for 15% of the time, Pallas kernels for 0%

profile of v1, /device:TPU:2, one launch (start us, length us, event | category | flops | bytes accessed | tf_op | source)
XLA Modules:
  0.0 223.0 jit_solution(686977057311700541)
XLA Ops:
  1.7 6.6 %convolution_convert_fusion.1 = bf16[4096,512]{1,0:T(8,128)(2,1)} fusion(bf16[512,4096]{1,0:T(8,128)(2,1)} %param.7, bf16[512,512]{1,0:T(8,128)(2,1)S(1)} %copy-done), kind=kOutput, calls=%fused_computation.2 | convolution fusion | flops 2149580800 | bytes 8912896 | tf_op jit(solution)/shard_map/tr,tk->rk/dot_general | solution.py:39
  8.3 4.8 %all-to-all-start = ((bf16[4,1024,512]{2,1,0:T(8,128)(2,1)}), bf16[4,1024,512]{2,1,0:T(8,128)(2,1)}, u32[]{:S(2)}, u32[]{:S(2)}) async-start(bf16[4,1024,512]{2,1,0:T(8,128)(2,1)} %bitcast.57), calls=%async_computation | async-start | bytes 8388608 | tf_op jit(solution)/shard_map/all_to_all | solution.py:40
  13.8 48.5 %all-to-all-done = bf16[4,1024,512]{2,1,0:T(8,128)(2,1)} async-done(((bf16[4,1024,512]{2,1,0:T(8,128)(2,1)}), bf16[4,1024,512]{2,1,0:T(8,128)(2,1)}, u32[]{:S(2)}, u32[]{:S(2)}) %all-to-all-start) | async-done | bytes 4194336 | tf_op jit(solution)/shard_map/all_to_all | solution.py:40
  62.2 3.3 %convert_reduce_fusion = f32[1024,512]{1,0:T(8,128)S(1)} fusion(bf16[4,1024,512]{2,1,0:T(8,128)(2,1)} %all-to-all-done), kind=kLoop, calls=%fused_computation | loop fusion | flops 3670016 | bytes 6291456 | tf_op jit(solution)/shard_map/reduce_sum | solution.py:45
  67.0 2.1 collective-permute-done.4
  69.3 27.3 %all_to_all.25 = bf16[32,16,512]{2,1,0:T(8,128)(2,1)S(1)} all-to-all(bf16[32,16,512]{2,1,0:T(8,128)(2,1)S(1)} %bitcast.58), channel_id=1, replica_groups=mesh['x'=4,'z'=8,'core'=2,'y'=4] {'x','z'}, dimensions={0} | all-to-all | bytes 1048576 | tf_op jit(solution)/shard_map/all_to_all | solution.py:49
  97.8 6.9 %all-to-all-start.2 = ((f32[32,16,512]{2,1,0:T(8,128)}), f32[32,16,512]{2,1,0:T(8,128)S(1)}, u32[]{:S(2)}, u32[]{:S(2)}) async-start(f32[32,16,512]{2,1,0:T(8,128)} %broadcast_in_dim.13), calls=%async_computation.2 | async-start | bytes 2097152 | tf_op jit(solution)/shard_map/all_to_all | solution.py:51
  106.7 1.6 collective-permute-start.1
  108.3 12.3 %collective-permute-done = bf16[512,512]{1,0:T(8,128)(2,1)S(1)} collective-permute-done((bf16[512,512]{1,0:T(8,128)(2,1)}, bf16[512,512]{1,0:T(8,128)(2,1)S(1)}, u32[]{:S(2)}, u32[]{:S(2)}) %collective-permute-start) | collective-permute-done | bytes 524320 | tf_op jit(solution)/shard_map/ppermute | solution.py:23
  121.4 1.9 collective-permute-done.1
  124.1 8.2 %collective-permute-done.2 = bf16[512,512]{1,0:T(8,128)(2,1)S(1)} collective-permute-done((bf16[512,512]{1,0:T(8,128)(2,1)}, bf16[512,512]{1,0:T(8,128)(2,1)S(1)}, u32[]{:S(2)}, u32[]{:S(2)}) %collective-permute-start.2) | collective-permute-done | bytes 524320 | tf_op jit(solution)/shard_map/ppermute | solution.py:23
  136.4 3.4 %constant_dynamic-slice_fusion = bf16[2048,512]{1,0:T(8,128)(2,1)} fusion(bf16[3584,512]{1,0:T(8,128)(2,1)} %constant_dynamic-update-slice_fusion, s32[]{:T(128)S(6)} %select_n.39), kind=kLoop, calls=%fused_computation.59 | loop fusion | bytes 4194308 | tf_op jit(solution)/shard_map/dynamic_slice | solution.py:25
  140.0 1.8 broadcast_select_fusion.1
  141.8 2.2 fusion.4
  146.6 3.5 %all-to-all-start.3 = ((f32[4,64,640]{2,1,0:T(8,128)}), f32[4,64,640]{2,1,0:T(8,128)S(1)}, u32[]{:S(2)}, u32[]{:S(2)}) async-start(f32[4,64,640]{2,1,0:T(8,128)} %broadcast_in_dim.14), calls=%async_computation.3 | async-start | bytes 1310720 | tf_op jit(solution)/shard_map/all_to_all | solution.py:33
  150.1 2.5 %select_bitcast_fusion.1 = (bf16[4,1,512,512]{3,2,1,0:T(8,128)(2,1)S(1)}, bf16[4,1,512,512]{3,2,1,0:T(8,128)(2,1)S(1)}) fusion(bf16[4,512,512]{2,1,0:T(8,128)(2,1)} %bitcast.1, bf16[4,512,512]{2,1,0:T(8,128)(2,1)} %collective-permute-done.3, pred[]{:T(512)S(6)} %eq.2), kind=kLoop, calls=%fused_computation.9 | loop fusion | flops 2097152 | bytes 8388609 | tf_op jit(solution)/shard_map/stack | solution.py:29
  152.6 2.4 %pad_maximum_fusion = bf16[4,2,512,512]{3,2,1,0:T(8,128)(2,1)} fusion(bf16[4,1,512,512]{3,2,1,0:T(8,128)(2,1)S(1)} %get-tuple-element.22, bf16[4,1,512,512]{3,2,1,0:T(8,128)(2,1)S(1)} %get-tuple-element.21), kind=kLoop, calls=%fused_computation.4 | loop fusion | flops 2097152 | bytes 8388608 | tf_op jit(solution)/shard_map/stack | solution.py:29
  155.0 6.8 %all-to-all-done.3 = f32[4,64,640]{2,1,0:T(8,128)S(1)} async-done(((f32[4,64,640]{2,1,0:T(8,128)}), f32[4,64,640]{2,1,0:T(8,128)S(1)}, u32[]{:S(2)}, u32[]{:S(2)}) %all-to-all-start.3) | async-done | bytes 655392 | tf_op jit(solution)/shard_map/all_to_all | solution.py:33
  163.7 1.8 copy.39
  165.5 1.8 copy.36
  169.5 5.8 %cholesky.44 = f32[64,64]{1,0:T(8,128)S(1)} custom-call(f32[64,64]{1,0:T(8,128)S(1)} %fusion.19), custom_call_target="Cholesky" | custom-call | tf_op jit(solution)/shard_map/jit(cholesky)/cholesky | solution.py:64
  176.7 4.9 %custom-call.8 = f32[1,64,64]{1,2,0:T(8,128)S(1)} custom-call(f32[1,64,64]{2,1,0:T(8,128)S(1)} %fusion.14), custom_call_target="InvertDiagBlocksLowerTriangular" | custom-call | tf_op jit(solution)/shard_map/triangular_solve | solution.py:66
  182.1 2.1 fusion.2
  184.6 1.4 fusion.1
  186.8 3.7 %all-to-all-start.4 = ((f32[4,64,640]{2,1,0:T(8,128)}), f32[4,64,640]{2,1,0:T(8,128)S(1)}, u32[]{:S(2)}, u32[]{:S(2)}) async-start(f32[4,64,640]{2,1,0:T(8,128)} %broadcast_in_dim.15), calls=%async_computation.4 | async-start | bytes 1310720 | tf_op jit(solution)/shard_map/all_to_all | solution.py:33
  190.6 6.5 %fusion = bf16[512,4096]{0,1:T(8,128)(2,1)} fusion(bf16[4096,512]{1,0:T(8,128)(2,1)} %bitcast.56, bf16[512,512]{1,0:T(8,128)(2,1)S(1)} %copy-done), kind=kOutput, calls=%fused_computation.3 | convolution fusion | flops 2149580800 | bytes 8912896 | tf_op jit(solution)/shard_map/tk,rk->tr/dot_general | solution.py:43
  197.1 6.3 %copy.35 = bf16[512,4096]{1,0:T(8,128)(2,1)} copy(bf16[512,4096]{0,1:T(8,128)(2,1)} %fusion) | data formatting | bytes 8388608
  205.1 5.8 %cholesky.55 = f32[64,64]{1,0:T(8,128)S(1)} custom-call(f32[64,64]{1,0:T(8,128)S(1)} %fusion.17), custom_call_target="Cholesky" | custom-call | tf_op jit(solution)/shard_map/jit(cholesky)/cholesky | solution.py:64
  212.3 4.9 %custom-call.9 = f32[1,64,64]{1,2,0:T(8,128)S(1)} custom-call(f32[1,64,64]{2,1,0:T(8,128)S(1)} %fusion.15), custom_call_target="InvertDiagBlocksLowerTriangular" | custom-call | tf_op jit(solution)/shard_map/triangular_solve | solution.py:66
  217.2 1.4 fusion.5
  218.6 1.8 fusion.9
  221.2 1.8 subtract_bitcast_fusion
  (74 shorter events, 25.2 us)
Async XLA Ops:
  0.6 1.0 copy-start
  8.3 54.0 %all-to-all-start = ((bf16[4,1024,512]{2,1,0:T(8,128)(2,1)}), bf16[4,1024,512]{2,1,0:T(8,128)(2,1)}, u32[]{:S(2)}, u32[]{:S(2)}) async-start(bf16[4,1024,512]{2,1,0:T(8,128)(2,1)} %bitcast.57), calls=%async_computation | async-start | bytes 8388608 | tf_op jit(solution)/shard_map/all_to_all | solution.py:40
  62.2 3.3 %copy-start.5 = (f32[1,1024,512]{2,1,0:T(8,128)S(1)}, f32[1,1024,512]{2,1,0:T(8,128)}, u32[]{:S(2)}) copy-start(f32[1,1024,512]{2,1,0:T(8,128)} %param.10) | copy-start | bytes 6291460
  66.0 30.5 %copy-start.1 = (f32[1024,512]{1,0:T(8,128)}, f32[1024,512]{1,0:T(8,128)S(1)}, u32[]{:S(2)}) copy-start(f32[1024,512]{1,0:T(8,128)S(1)} %bitcast_add_fusion) | copy-start | bytes 6291460
  67.0 2.1 collective-permute-start.4
  96.6 8.1 %copy-start.6 = (bf16[1024,512]{1,0:T(8,128)(2,1)S(1)}, bf16[1024,512]{1,0:T(8,128)(2,1)}, u32[]{:S(2)}) copy-start(bf16[1024,512]{1,0:T(8,128)(2,1)} %param.9) | copy-start | bytes 3145732
  97.8 38.6 %all-to-all-start.2 = ((f32[32,16,512]{2,1,0:T(8,128)}), f32[32,16,512]{2,1,0:T(8,128)S(1)}, u32[]{:S(2)}, u32[]{:S(2)}) async-start(f32[32,16,512]{2,1,0:T(8,128)} %broadcast_in_dim.13), calls=%async_computation.2 | async-start | bytes 2097152 | tf_op jit(solution)/shard_map/all_to_all | solution.py:51
  105.5 15.0 %collective-permute-start = (bf16[512,512]{1,0:T(8,128)(2,1)}, bf16[512,512]{1,0:T(8,128)(2,1)S(1)}, u32[]{:S(2)}, u32[]{:S(2)}) collective-permute-start(bf16[512,512]{1,0:T(8,128)(2,1)} %constant_dynamic-slice_fusion.1), channel_id=1, source_target_pairs={{0,3},{1,0},{2,1},{3,2},{4,7},{5,4},{6,5},{7,6},{8,11},{9,8},{10,9... | collective-permute-start | bytes 1572872 | tf_op jit(solution)/shard_map/ppermute | solution.py:23
  106.7 16.6 %collective-permute-start.1 = (bf16[512,512]{1,0:T(8,128)(2,1)}, bf16[512,512]{1,0:T(8,128)(2,1)S(1)}, u32[]{:S(2)}, u32[]{:S(2)}) collective-permute-start(bf16[512,512]{1,0:T(8,128)(2,1)} %constant_dynamic-slice_fusion.1), channel_id=1, source_target_pairs={{0,2},{1,3},{2,0},{3,1},{4,6},{5,7},{6,4},{7,5},{8,10},{9,11},{10,... | collective-permute-start | bytes 1572872 | tf_op jit(solution)/shard_map/ppermute | solution.py:23
  108.3 24.0 %collective-permute-start.2 = (bf16[512,512]{1,0:T(8,128)(2,1)}, bf16[512,512]{1,0:T(8,128)(2,1)S(1)}, u32[]{:S(2)}, u32[]{:S(2)}) collective-permute-start(bf16[512,512]{1,0:T(8,128)(2,1)} %constant_dynamic-slice_fusion.1), channel_id=1, source_target_pairs={{0,1},{1,2},{2,3},{3,0},{4,5},{5,6},{6,7},{7,4},{8,9},{9,10},{10,1... | collective-permute-start | bytes 1572872 | tf_op jit(solution)/shard_map/ppermute | solution.py:23
  108.3 24.8 %copy-start.7 = (bf16[1024,512]{1,0:T(8,128)(2,1)S(1)}, bf16[1024,512]{1,0:T(8,128)(2,1)}, u32[]{:S(2)}) copy-start(bf16[1024,512]{1,0:T(8,128)(2,1)} %param.9) | copy-start | bytes 3145732
  136.4 3.4 %copy-start.4 = (f32[32,16,512]{2,1,0:T(8,128)}, f32[32,16,512]{2,1,0:T(8,128)S(1)}, u32[]{:S(2)}) copy-start(f32[32,16,512]{2,1,0:T(8,128)S(1)} %all-to-all-done.2) | copy-start | bytes 3145732
  136.4 3.6 %collective-permute-start.5 = (f32[512,512]{1,0:T(8,128)S(1)}, f32[512,512]{1,0:T(8,128)}, u32[]{:S(2)}, u32[]{:S(2)}) collective-permute-start(f32[512,512]{1,0:T(8,128)S(1)} %bitcast.55), channel_id=1, source_target_pairs={{0,4},{4,0},{1,5},{5,1},{2,6},{6,2},{3,7},{7,3},{8,12},{12,8},{9,1... | collective-permute-start | bytes 3145736 | tf_op jit(solution)/shard_map/ppermute | solution.py:53
  139.8 10.3 %collective-permute-start.3 = (bf16[4,512,512]{2,1,0:T(8,128)(2,1)}, bf16[4,512,512]{2,1,0:T(8,128)(2,1)}, u32[]{:S(2)}, u32[]{:S(2)}) collective-permute-start(bf16[4,512,512]{2,1,0:T(8,128)(2,1)} %bitcast.1), channel_id=1, source_target_pairs={{0,4},{4,0},{1,5},{5,1},{2,6},{6,2},{3,7},{7,3},{8,12},{12,8},{9,1... | collective-permute-start | bytes 6291464 | tf_op jit(solution)/shard_map/ppermute | solution.py:26
  140.0 1.9 copy-start.8
  146.6 15.2 %all-to-all-start.3 = ((f32[4,64,640]{2,1,0:T(8,128)}), f32[4,64,640]{2,1,0:T(8,128)S(1)}, u32[]{:S(2)}, u32[]{:S(2)}) async-start(f32[4,64,640]{2,1,0:T(8,128)} %broadcast_in_dim.14), calls=%async_computation.3 | async-start | bytes 1310720 | tf_op jit(solution)/shard_map/all_to_all | solution.py:33
  186.8 16.5 %all-to-all-start.4 = ((f32[4,64,640]{2,1,0:T(8,128)}), f32[4,64,640]{2,1,0:T(8,128)S(1)}, u32[]{:S(2)}, u32[]{:S(2)}) async-start(f32[4,64,640]{2,1,0:T(8,128)} %broadcast_in_dim.15), calls=%async_computation.4 | async-start | bytes 1310720 | tf_op jit(solution)/shard_map/all_to_all | solution.py:33
  204.2 17.0 %copy-start.2 = (f32[1024,512]{1,0:T(8,128)S(1)}, f32[1024,512]{1,0:T(8,128)}, u32[]{:S(2)}) copy-start(f32[1024,512]{1,0:T(8,128)} %copy-done.1) | copy-start | bytes 6291460
  220.5 2.5 %copy-start.3 = (f32[1024,512]{1,0:T(8,128)}, f32[1024,512]{1,0:T(8,128)S(1)}, u32[]{:S(2)}) copy-start(f32[1024,512]{1,0:T(8,128)S(1)} %fusion.9) | copy-start | bytes 6291460

commit v2 on v1

v2 whole, which is shorter than its diff:
```python
import jax
import jax.numpy as jnp
from jax import lax
from jax.experimental import pallas as pl
from jax.experimental.pallas import tpu as pltpu
from jax.sharding import Mesh
from jax.sharding import PartitionSpec as P

ITERS = 2
NX, NZ, NC, NY = 4, 8, 2, 4
DP = ("x", "z", "core")
D, KVC, R, TOK = 4096, 512, 64, 512
ROWS = D // NY
HALF = ROWS // NC
COLS = KVC // 2
WIDE = KVC + 128
HI = lax.Precision.HIGHEST
f32, bf16 = jnp.float32, jnp.bfloat16
SWAP = [(0, 1), (1, 0)]
FLIP = [(i, i ^ 1) for i in range(NY)]
MIRROR = [(i, 3 - i) for i in range(NY)]
VMEM_LIMIT = 24 * 1024 * 1024


def params(**kw):
    return pltpu.CompilerParams(vmem_limit_bytes=VMEM_LIMIT, **kw)


def sds(shape, dtype=f32):
    return jax.ShapeDtypeStruct(shape, dtype)


def whole(shape):
    return pl.BlockSpec(shape, lambda *_: (0,) * len(shape))


def dot(a, b, dims):
    return lax.dot_general(a, b, (dims, ((), ())), precision=HI, preferred_element_type=f32)


NT = ((1,), (1,))
NN = ((1,), (0,))
TN = ((0,), (0,))


def inverse_lower(block):
    lane = lax.broadcasted_iota(jnp.int32, (8, 128), 1)
    sub = lax.broadcasted_iota(jnp.int32, (8, 128), 0)
    tiles = [
        jnp.where(lane < R, block[8 * i : 8 * i + 8], jnp.where(lane - R == sub + 8 * i, 1.0, 0.0))
        for i in range(8)
    ]
    for k in range(R):
        a, b = divmod(k, 8)
        row = tiles[a][b : b + 1, :]
        scale = lax.rsqrt(row[:, k : k + 1])
        row = row * scale
        for i in range(a, 8):
            col = tiles[i][:, k : k + 1] * scale
            new = tiles[i] - col * row
            if i == a:
                new = jnp.where(sub > b, new, jnp.where(sub == b, row, tiles[i]))
            tiles[i] = new
    return jnp.concatenate(tiles, axis=0)[:, R:]


def products(qt, half_ref, other_ref, p_ref, t_ref):
    z, g = [], []
    for n, ref in enumerate((half_ref, other_ref)):
        m = ref[...]
        p = dot(qt, m, NT)
        p_ref[n] = p
        z.append(dot(p, m, NN))
        g.append(dot(p, jnp.concatenate([p, jnp.zeros_like(p)], axis=0), NT))
    zt = z[0] + z[1]
    gram = g[0] + g[1]
    for s in range(NY):
        t_ref[s, :, :KVC] = zt
        t_ref[s, :, KVC:] = gram


def total(got_ref, lo, hi):
    return (got_ref[0, :, lo:hi] + got_ref[1, :, lo:hi]) + (got_ref[2, :, lo:hi] + got_ref[3, :, lo:hi])


def first_kernel(q_ref, half_ref, other_ref, t_ref, p_ref):
    products(q_ref[...], half_ref, other_ref, p_ref, t_ref)


def next_kernel(got_ref, half_ref, other_ref, t_ref, p_ref):
    inv = inverse_lower(total(got_ref, KVC, WIDE))
    qt = dot(inv, total(got_ref, 0, KVC), NN)
    products(qt, half_ref, other_ref, p_ref, t_ref)


def first(qt, half, other):
    return pl.pallas_call(
        first_kernel, name="first", out_shape=(sds((NY, R, WIDE)), sds((2, R, HALF))), compiler_params=params()
    )(qt, half, other)


def following(got, half, other):
    return pl.pallas_call(
        next_kernel, name="following", out_shape=(sds((NY, R, WIDE)), sds((2, R, HALF))), compiler_params=params()
    )(got, half, other)


def last_kernel(core_ref, got_ref, p_ref, merged_ref, approx_ref, err_ref, q_ref, ph):
    @pl.when(pl.program_id(0) == 0)
    def _():
        inv = inverse_lower(total(got_ref, KVC, WIDE))
        q_ref[...] = dot(inv, total(got_ref, 0, KVC), NN)
        for n in range(2):
            p = dot(inv, p_ref[n], NN)
            ph[2 * n] = p[:, : HALF // 2]
            ph[2 * n + 1] = p[:, HALF // 2 :]

    approx = dot(ph[pl.program_id(0)], q_ref[...], TN)
    approx_ref[...] = approx
    err_ref[...] = merged_ref[...] - approx


def last(core, got, p, merged):
    rows = HALF // 2
    place = pl.BlockSpec((rows, KVC), lambda i, c: ((i + 2 * c[0]) % 4, 0))
    return pl.pallas_call(
        last_kernel,
        name="last",
        grid_spec=pltpu.PrefetchScalarGridSpec(
            num_scalar_prefetch=1,
            grid=(4,),
            in_specs=[whole((NY, R, WIDE)), whole((2, R, HALF)), place],
            out_specs=[place, place, whole((R, KVC))],
            scratch_shapes=[pltpu.VMEM((4, R, rows), f32)],
        ),
        out_shape=(sds((ROWS, KVC)), sds((ROWS, KVC)), sds((R, KVC))),
        compiler_params=params(),
    )(core, got, p, merged)


def merge_kernel(at_ref, s_ref, pa, va, wa, pb, vb, wb, e_ref, merged_ref, give_ref):
    def add(p, v, w):
        return p[0].astype(f32) + v[...].astype(f32) + w[...].astype(f32)

    scale = s_ref[0]
    left = e_ref[:, :COLS] + scale * add(pa, va, wa)
    right = e_ref[:, COLS:] + scale * add(pb, vb, wb)
    merged_ref[:, :COLS] = left
    merged_ref[:, COLS:] = right

    @pl.when(pl.program_id(0) < 2)
    def _():
        give_ref[:, :COLS] = left.astype(bf16)
        give_ref[:, COLS:] = right.astype(bf16)


def merge(at, scale, pa, va, wa, pb, vb, wb, error):
    rows = HALF // 2

    def block(i, a):
        return (i + 2 * (1 - a[1])) % 4

    own = pl.BlockSpec((1, rows, COLS), lambda i, a, s: (a[0], block(i, a), 0))
    got = pl.BlockSpec((rows, COLS), lambda i, a, s: (block(i, a), 0))
    place = pl.BlockSpec((rows, KVC), lambda i, a, s: (block(i, a), 0))
    give = pl.BlockSpec((rows, KVC), lambda i, a, s: (jnp.minimum(i, 1), 0))
    return pl.pallas_call(
        merge_kernel,
        name="merge",
        grid_spec=pltpu.PrefetchScalarGridSpec(
            num_scalar_prefetch=2,
            grid=(4,),
            in_specs=[own, got, got, own, got, got, place],
            out_specs=[place, give],
        ),
        out_shape=(sds((ROWS, KVC)), sds((HALF, KVC), bf16)),
        compiler_params=params(),
    )(at, scale, pa, va, wa, pb, vb, wb, error)


def input_grad_kernel(at_ref, cot_ref, w0, w1, w2, w3, other_ref, out_ref):
    for g in range(2 * NY):

        @pl.when(pl.program_id(0) == g)
        def _(g=g):
            w = (w0, w1, w2, w3)[g][...] if g < NY else other_ref[g - NY]
            out_ref[...] = lax.dot_general(
                cot_ref[...], w, (NT, ((), ())), preferred_element_type=f32
            ).astype(bf16)


def input_grad_of(at, cot, pieces, other):
    piece = whole((HALF, KVC))
    return pl.pallas_call(
        input_grad_kernel,
        name="input_grad",
        grid_spec=pltpu.PrefetchScalarGridSpec(
            num_scalar_prefetch=1,
            grid=(2 * NY,),
            in_specs=[whole((TOK, KVC)), piece, piece, piece, piece, whole((NY, HALF, KVC))],
            out_specs=pl.BlockSpec((TOK, HALF), lambda i, a: (0, a[i])),
        ),
        out_shape=sds((TOK, D), bf16),
        compiler_params=params(),
        cost_estimate=pl.CostEstimate(flops=2 * TOK * D * KVC, bytes_accessed=9 << 20, transcendentals=0),
    )(at, cot, *pieces, other)


def scatter_y(acts, cot, y):
    flip, mirror = y ^ 1, 3 - y
    out = []
    parts = [
        jnp.einsum("tr,tk->rk", acts, cot[:, n * COLS : (n + 1) * COLS], preferred_element_type=f32)
        .astype(bf16)
        .reshape(NY, ROWS, COLS)
        for n in range(2)
    ]
    plans = ((FLIP, MIRROR, flip, mirror), (MIRROR, FLIP, mirror, flip))

    def take(n, index):
        return lax.dynamic_index_in_dim(parts[n], index, 0, keepdims=False)

    firsts = [lax.ppermute(take(n, 3 - (y ^ 1)), "y", plans[n][0]) for n in range(2)]
    seconds = [lax.ppermute(take(n, plans[n][2]), "y", plans[n][0]) for n in range(2)]
    for n in range(2):
        onward = (firsts[n].astype(f32) + take(n, plans[n][3]).astype(f32)).astype(bf16)
        out += [parts[n], seconds[n], lax.ppermute(onward, "y", plans[n][1])]
    return out


def everyone(t, axis, n):
    return lax.all_to_all(jnp.broadcast_to(t, (n, *t.shape)), axis, 0, 0, tiled=True)


def body(acts, cotangent, weight, error_buf, q_init, inv_scale):
    y, core = lax.axis_index("y"), lax.axis_index("core")
    terms = scatter_y(acts, cotangent, y)
    merged, give = merge(jnp.stack([y, core]), inv_scale[None], *terms, error_buf[0])

    give, weight = lax.optimization_barrier((give, weight))
    keep = lax.dynamic_slice_in_dim(merged, core * HALF, HALF, 0)
    pair = keep + lax.ppermute(give, "core", SWAP).astype(f32)
    along_x = lax.all_to_all(pair.astype(bf16).reshape(NX, 128, KVC), "x", 0, 0, tiled=True)
    row = jnp.sum(along_x.astype(f32), axis=0)
    along_z = lax.all_to_all(row.reshape(NZ, 16, KVC), "z", 0, 0, tiled=True)
    rows = jnp.sum(along_z, axis=0) * (1.0 / (NX * NZ * NC))
    block = everyone(rows, "z", NZ).reshape(128, KVC)
    half = everyone(block, "x", NX).reshape(HALF, KVC)
    other = lax.ppermute(half, "core", SWAP)

    mine = lax.dynamic_slice_in_dim(weight, core * HALF, HALF, 0)
    pieces = [mine] + [
        lax.ppermute(mine, "y", [(i, (i + s) % NY) for i in range(NY)]) for s in range(1, NY)
    ]
    others = lax.ppermute(jnp.stack(pieces), "core", SWAP)
    source = (y - jnp.arange(NY)) % NY
    at = jnp.concatenate([2 * source + core, 2 * source + 1 - core])
    input_grad = input_grad_of(at, cotangent, pieces, others)

    t, p = first(q_init.T, half, other)
    for _ in range(ITERS - 1):
        t, p = following(lax.all_to_all(t, "y", 0, 0, tiled=True), half, other)
    approx, new_error, qt = last(core[None], lax.all_to_all(t, "y", 0, 0, tiled=True), p, merged)
    return (input_grad, approx, new_error[None], qt.T)


def solution(mesh):
    fine = Mesh(mesh.devices.reshape(NX, NZ, NC, NY), ("x", "z", "core", "y"))
    every = P((*DP, "y"), None)
    in_specs = (every, every, P("y", None), P(DP, "y", None), P(), P())
    out_specs = (every, P("y", None), P(DP, "y", None), P())
    return jax.shard_map(body, mesh=fine, in_specs=in_specs, out_specs=out_specs, check_vma=False)
```

time: 224 us -> 189 us (0.84)
  Pallas kernels: 0 us -> 36.5 us
  waiting for transfers between devices: 79.7 us -> 47 us
  other arithmetic: 38 us -> 8.38 us
  blocking collectives: 27.3 us -> 46.8 us
  local copies, waits for them, and re-layouts: 30 us -> 12.8 us
  matrix products: 24.6 us -> 8.41 us
  starting transfers between devices: 21.8 us -> 25.5 us
    all_to_all x4 -> x3, waiting for transfers between devices: 55.3 us -> 5.93 us  [the longest x2 5.92 us: everyone(): lax.all_to_all(jnp.broadcast_to(t, (n, *t.shape)), axis, 0, 0, tiled=True)]
    pallas_call x0 -> x5, Pallas kernels: none -> 36.5 us  [the longest x1 10.8 us: last(): pl.pallas_call(last_kernel, name='last', grid_spec=pltpu.PrefetchScalarGr...]
    another operation x12 -> x2, other arithmetic: 29 us -> 2.89 us  [the longest x1 2.81 us: body(): others = lax.ppermute(jnp.stack(pieces), 'core', SWAP)]
    all_to_all x1 -> x3, blocking collectives: 27.3 us -> 46.8 us  [the longest x1 19 us: body(): along_z = lax.all_to_all(row.reshape(NZ, 16, KVC), 'z', 0, 0, tiled=True)]
    dot_general x9 -> x2, matrix products: 22.7 us -> 8.41 us  [scatter_y(): jnp.einsum('tr,tk->rk', acts, cot[:, n * COLS:(n + 1) * COLS], preferred_...]
    ppermute x4 -> x10, waiting for transfers between devices: 22.3 us -> 33.6 us  [the longest x2 9.83 us: scatter_y(): out += [parts[n], seconds[n], lax.ppermute(onward, 'y', plans[n][1])]]
    unnamed x33 -> x24, local copies, waits for them, and re-layouts: 18.6 us -> 7.81 us
    ppermute x4 -> x10, starting transfers between devices: 2.86 us -> 12.5 us  [the longest x3 4.39 us: body(): lax.ppermute(mine, 'y', [(i, (i + s) % NY) for i in range(NY)])]
  transfers between devices with their start and end apart: 10 -> 15, of which waited for: 6 -> 9; matrix products, arithmetic and copies ran while one was open for 15% -> 8% of each run, Pallas kernels for 0% -> 11%
where the time goes in v2:
time: 189 us; the launch traced here: 187 us
  waiting for transfers between devices  47 us (25%)
  blocking collectives  46.8 us (25%)
  Pallas kernels  36.5 us (19%)
  starting transfers between devices  25.5 us (13%)
  local copies, waits for them, and re-layouts  12.8 us (7%)
  matrix products  8.41 us (4%)
  other arithmetic  8.38 us (4%)
    all_to_all x1, blocking collectives, body(): along_z = lax.all_to_all(row.reshape(NZ, 16, KVC), 'z', 0, 0, tiled=True)  19 us
    all_to_all x1, blocking collectives, body(): t, p = following(lax.all_to_all(t, 'y', 0, 0, tiled=True), half, other)  14.9 us
    all_to_all x1, blocking collectives, body(): lax.all_to_all(pair.astype(bf16).reshape(NX, 128, KVC), 'x', 0, 0, tiled=...  12.9 us
    pallas_call x1, Pallas kernels, last(): pl.pallas_call(last_kernel, name='last', grid_spec=pltpu.PrefetchScalarGr...  10.8 us
    ppermute x2, waiting for transfers between devices, scatter_y(): out += [parts[n], seconds[n], lax.ppermute(onward, 'y', plans[n][1])]  9.83 us
    pallas_call x1, Pallas kernels, following(): pl.pallas_call(next_kernel, name='following', out_shape=(sds((NY, R, WIDE...  9.75 us
    ppermute x2, waiting for transfers between devices, scatter_y(): lax.ppermute(take(n, plans[n][2]), 'y', plans[n][0])  8.65 us
    dot_general x2, matrix products, scatter_y(): jnp.einsum('tr,tk->rk', acts, cot[:, n * COLS:(n + 1) * COLS], preferred_...  8.41 us
  transfers between devices with their start and end apart: 15, of which 9 were waited for; matrix products, arithmetic and copies ran while one was open for 8% of the time, Pallas kernels for 11%

profile of v2, /device:TPU:2, one launch (start us, length us, event | category | flops | bytes accessed | tf_op | source)
XLA Modules:
  0.0 186.9 jit_solution(45124110691143981)
XLA Ops:
  0.7 3.6 %convolution_convert_fusion.1 = bf16[4096,256]{1,0:T(8,128)(2,1)S(1)} fusion(bf16[512,4096]{1,0:T(8,128)(2,1)} %param.6, bf16[512,512]{1,0:T(8,128)(2,1)} %cot_ref.1), kind=kOutput, calls=%fused_computation.1 | convolution fusion | flops 1074790400 | bytes 6553600 | tf_op jit(solution)/shard_map/tr,tk->rk/dot_general | solution.py:213
  5.3 1.6 collective-permute-start.1
  6.9 4.8 %convolution_convert_fusion = bf16[4096,256]{1,0:T(8,128)(2,1)} fusion(bf16[512,4096]{1,0:T(8,128)(2,1)} %param.6, bf16[512,512]{1,0:T(8,128)(2,1)S(1)} %copy-done.9), kind=kOutput, calls=%fused_computation | convolution fusion | flops 1074790400 | bytes 6553600 | tf_op jit(solution)/shard_map/tr,tk->rk/dot_general | solution.py:213
  11.7 2.1 %dynamic-slice_bitcast_fusion = (bf16[1024,256]{1,0:T(8,128)(2,1)S(1)}, bf16[1024,256]{1,0:T(8,128)(2,1)}) fusion(bf16[4,1024,256]{2,1,0:T(8,128)(2,1)} %bitcast.41, s32[]{:T(128)S(6)} %select_n.26, s32[]{:T(128)S(6)} %select_n.27), kind=kLoop, calls=%fused_computation.9 | loop fusion | bytes 2097160 | tf_op jit(solution)/shard_map/jit(dynamic_index_in_dim)/squeeze | solution.py:221
  13.8 2.2 %collective-permute-start.4 = (bf16[1024,256]{1,0:T(8,128)(2,1)S(1)}, bf16[1024,256]{1,0:T(8,128)(2,1)S(1)}, u32[]{:S(2)}, u32[]{:S(2)}) collective-permute-start(bf16[1024,256]{1,0:T(8,128)(2,1)S(1)} %get-tuple-element.24), channel_id=1, source_target_pairs={{0,3},{1,2},{2,1},{3,0},{4,7},{5,6},{6,5},{7,4},{8,11},{9,10},{10,... | collective-permute-start | bytes 1572872 | tf_op jit(solution)/shard_map/ppermute | solution.py:223
  17.3 3.2 %collective-permute-done.1 = bf16[1024,256]{1,0:T(8,128)(2,1)} collective-permute-done((bf16[1024,256]{1,0:T(8,128)(2,1)}, bf16[1024,256]{1,0:T(8,128)(2,1)}, u32[]{:S(2)}, u32[]{:S(2)}) %collective-permute-start.1) | collective-permute-done | bytes 524320 | tf_op jit(solution)/shard_map/ppermute | solution.py:223
  20.4 2.0 %fusion.1 = bf16[1024,256]{1,0:T(8,128)(2,1)} fusion(bf16[1024,256]{1,0:T(8,128)(2,1)} %collective-permute-done.1, bf16[4,1024,256]{2,1,0:T(8,128)(2,1)S(1)} %bitcast.39, s32[]{:T(128)S(6)} %select_n.27), kind=kLoop, calls=%fused_computation.6 | loop fusion | flops 1048576 | bytes 1572868 | tf_op jit(solution)/shard_map/convert_element_type | solution.py:226
  22.4 3.0 %collective-permute-start.2 = (bf16[1024,256]{1,0:T(8,128)(2,1)}, bf16[1024,256]{1,0:T(8,128)(2,1)}, u32[]{:S(2)}, u32[]{:S(2)}) collective-permute-start(bf16[1024,256]{1,0:T(8,128)(2,1)} %fusion.1), channel_id=1, source_target_pairs={{0,3},{1,2},{2,1},{3,0},{4,7},{5,6},{6,5},{7,4},{8,11},{9,10},{10,... | collective-permute-start | bytes 1572872 | tf_op jit(solution)/shard_map/ppermute | solution.py:227
  25.4 4.4 %collective-permute-done.4 = bf16[1024,256]{1,0:T(8,128)(2,1)S(1)} collective-permute-done((bf16[1024,256]{1,0:T(8,128)(2,1)S(1)}, bf16[1024,256]{1,0:T(8,128)(2,1)S(1)}, u32[]{:S(2)}, u32[]{:S(2)}) %collective-permute-start.4) | collective-permute-done | bytes 524320 | tf_op jit(solution)/shard_map/ppermute | solution.py:223
  29.8 2.0 %fusion = bf16[1024,256]{1,0:T(8,128)(2,1)} fusion(bf16[1024,256]{1,0:T(8,128)(2,1)S(1)} %collective-permute-done.4, bf16[4,1024,256]{2,1,0:T(8,128)(2,1)} %bitcast.42, s32[]{:T(128)S(6)} %select_n.25), kind=kLoop, calls=%fused_computation.4 | loop fusion | flops 1048576 | bytes 1572868 | tf_op jit(solution)/shard_map/convert_element_type | solution.py:226
  32.5 8.6 %collective-permute-done.3.vb = bf16[1024,256]{1,0:T(8,128)(2,1)} collective-permute-done((bf16[1024,256]{1,0:T(8,128)(2,1)}, bf16[1024,256]{1,0:T(8,128)(2,1)}, u32[]{:S(2)}, u32[]{:S(2)}) %collective-permute-start.3) | collective-permute-done | bytes 524320 | tf_op jit(solution)/shard_map/ppermute | solution.py:224
  41.1 9.8 %collective-permute-done.2.wa = bf16[1024,256]{1,0:T(8,128)(2,1)} collective-permute-done((bf16[1024,256]{1,0:T(8,128)(2,1)}, bf16[1024,256]{1,0:T(8,128)(2,1)}, u32[]{:S(2)}, u32[]{:S(2)}) %collective-permute-start.2) | collective-permute-done | bytes 524320 | tf_op jit(solution)/shard_map/ppermute | solution.py:227
  51.0 1.6 copy-done.1
  52.6 1.6 copy-done.4
  54.2 4.4 %merge.1 = (f32[1024,512]{1,0:T(8,128)S(1)}, bf16[512,512]{1,0:T(8,128)(2,1)}) custom-call(s32[2]{0:T(128)S(1)} %pad_add_fusion.1.at_ref, f32[1]{0:T(128)} %bitcast.34.s_ref, bf16[4,1024,256]{2,1,0:T(8,128)(2,1)S(1)} %bitcast.40, bf16[1024,256]{1,0:T(8,128)(2,1)} %collective-permute-done.va, bf16[1024,256]{1,0:T(8,128)(2,1)} %collective-permute-done.2.wa, ...), custom_call_target="tpu_custom_call" | custom-call | tf_op jit(solution)/shard_map/merge/pallas_call | solution.py:167
  59.9 2.1 %collective-permute-done.10 = bf16[512,512]{1,0:T(8,128)(2,1)S(1)} collective-permute-done((bf16[512,512]{1,0:T(8,128)(2,1)}, bf16[512,512]{1,0:T(8,128)(2,1)S(1)}, u32[]{:S(2)}, u32[]{:S(2)}) %collective-permute-start.10) | collective-permute-done | bytes 524320 | tf_op jit(solution)/shard_map/ppermute | solution.py:242
  62.0 1.4 add_convert_fusion
  63.4 12.9 %all_to_all.30 = bf16[4,128,512]{2,1,0:T(8,128)(2,1)S(1)} all-to-all(bf16[4,128,512]{2,1,0:T(8,128)(2,1)S(1)} %bitcast.47), channel_id=1, replica_groups=mesh['x'=4,'z'=8,'core'=2,'y'=4] {'x'}, dimensions={0} | all-to-all | bytes 1048576 | tf_op jit(solution)/shard_map/all_to_all | solution.py:243
  76.4 19.0 %all_to_all.31 = f32[8,16,512]{2,1,0:T(8,128)S(1)} all-to-all(f32[8,16,512]{2,1,0:T(8,128)S(1)} %bitcast.49), channel_id=1, replica_groups=mesh['x'=4,'z'=8,'core'=2,'y'=4] {'z'}, dimensions={0} | all-to-all | bytes 524288 | tf_op jit(solution)/shard_map/all_to_all | solution.py:245
  96.2 3.4 %all-to-all-start.2 = ((f32[8,16,512]{2,1,0:T(8,128)}), f32[8,16,512]{2,1,0:T(8,128)S(1)}, u32[]{:S(2)}, u32[]{:S(2)}) async-start(f32[8,16,512]{2,1,0:T(8,128)} %broadcast_in_dim.14), calls=%async_computation.2 | async-start | bytes 524288 | tf_op jit(solution)/shard_map/all_to_all | solution.py:232
  99.8 3.6 %collective-permute-start.7 = (bf16[512,512]{1,0:T(8,128)(2,1)S(1)}, bf16[512,512]{1,0:T(8,128)(2,1)}, u32[]{:S(2)}, u32[]{:S(2)}) collective-permute-start(bf16[512,512]{1,0:T(8,128)(2,1)S(1)} %constant_dynamic-slice_fusion.w0), channel_id=1, source_target_pairs={{0,2},{1,3},{2,0},{3,1},{4,6},{5,7},{6,4},{7,5},{8,10},{9,11},{10,... | collective-permute-start | bytes 1572872 | tf_op jit(solution)/shard_map/ppermute | solution.py:253
  104.1 5.9 %all-to-all-done.2 = f32[8,16,512]{2,1,0:T(8,128)S(1)} async-done(((f32[8,16,512]{2,1,0:T(8,128)}), f32[8,16,512]{2,1,0:T(8,128)S(1)}, u32[]{:S(2)}, u32[]{:S(2)}) %all-to-all-start.2) | async-done | bytes 262176 | tf_op jit(solution)/shard_map/all_to_all | solution.py:232
  111.1 4.9 %all-to-all-start.3 = ((f32[4,128,512]{2,1,0:T(8,128)}), f32[4,128,512]{2,1,0:T(8,128)S(1)}, u32[]{:S(2)}, u32[]{:S(2)}) async-start(f32[4,128,512]{2,1,0:T(8,128)} %broadcast_in_dim.15), calls=%async_computation.3 | async-start | bytes 2097152 | tf_op jit(solution)/shard_map/all_to_all | solution.py:232
  116.1 7.3 %collective-permute-done.7.w2 = bf16[512,512]{1,0:T(8,128)(2,1)} collective-permute-done((bf16[512,512]{1,0:T(8,128)(2,1)S(1)}, bf16[512,512]{1,0:T(8,128)(2,1)}, u32[]{:S(2)}, u32[]{:S(2)}) %collective-permute-start.7) | collective-permute-done | bytes 524320 | tf_op jit(solution)/shard_map/ppermute | solution.py:253
  123.7 2.8 %pad_maximum_fusion = bf16[4,512,512]{2,1,0:T(8,128)(2,1)} fusion(bf16[1,512,512]{2,1,0:T(8,128)(2,1)} %bitcast.15, bf16[1,512,512]{2,1,0:T(8,128)(2,1)} %bitcast.14, bf16[1,512,512]{2,1,0:T(8,128)(2,1)S(1)} %bitcast.45, bf16[1,512,512]{2,1,0:T(8,128)(2,1)S(1)} %fusion.8), kind=kLoop, calls=%fused_computation.2 | loop fusion | flops 3145728 | bytes 4194304 | tf_op jit(solution)/shard_map/stack | solution.py:255
  127.0 5.4 %collective-permute-done.11.other_ref = f32[512,512]{1,0:T(8,128)S(1)} collective-permute-done((f32[512,512]{1,0:T(8,128)S(1)}, f32[512,512]{1,0:T(8,128)S(1)}, u32[]{:S(2)}, u32[]{:S(2)}) %collective-permute-start.11) | collective-permute-done | bytes 1048608 | tf_op jit(solution)/shard_map/ppermute | solution.py:249
  132.4 3.4 %first.1 = (f32[4,64,640]{2,1,0:T(8,128)S(1)}, f32[2,64,512]{2,1,0:T(8,128)}) custom-call(f32[64,512]{1,0:T(8,128)S(1)} %bitcast.46, f32[512,512]{1,0:T(8,128)S(1)} %bitcast.36, f32[512,512]{1,0:T(8,128)S(1)} %collective-permute-done.11.other_ref), custom_call_target="tpu_custom_call" | custom-call | tf_op jit(solution)/shard_map/first/pallas_call | solution.py:97
  135.8 14.9 %all_to_all.32.got_ref = f32[4,64,640]{2,1,0:T(8,128)S(1)} all-to-all(f32[4,64,640]{2,1,0:T(8,128)S(1)} %get-tuple-element.18), channel_id=1, replica_groups=mesh['x'=4,'z'=8,'core'=2,'y'=4] {'y'}, dimensions={0} | all-to-all | bytes 1310720 | tf_op jit(solution)/shard_map/all_to_all | solution.py:262
  150.7 9.8 %following.1 = (f32[4,64,640]{2,1,0:T(8,128)}, f32[2,64,512]{2,1,0:T(8,128)S(1)}) custom-call(f32[4,64,640]{2,1,0:T(8,128)S(1)} %all_to_all.32.got_ref, f32[512,512]{1,0:T(8,128)S(1)} %bitcast.37, f32[512,512]{1,0:T(8,128)S(1)} %collective-permute-done.11.other_ref), custom_call_target="tpu_custom_call" | custom-call | tf_op jit(solution)/shard_map/following/pallas_call | solution.py:103
  160.4 4.2 %all-to-all-start.5 = ((f32[4,64,640]{2,1,0:T(8,128)}), f32[4,64,640]{2,1,0:T(8,128)}, u32[]{:S(2)}, u32[]{:S(2)}) async-start(f32[4,64,640]{2,1,0:T(8,128)} %get-tuple-element.19), calls=%async_computation.5 | async-start | bytes 1310720 | tf_op jit(solution)/shard_map/all_to_all | solution.py:263
  167.9 8.1 %input_grad.1 = bf16[512,4096]{1,0:T(8,128)(2,1)} custom-call(s32[8]{0:T(128)S(1)} %pad_add_fusion.at_ref, bf16[512,512]{1,0:T(8,128)(2,1)S(1)} %copy-done.10, bf16[512,512]{1,0:T(8,128)(2,1)S(1)} %copy-done.6, bf16[512,512]{1,0:T(8,128)(2,1)S(1)} %copy-done.8, bf16[512,512]{1,0:T(8,128)(2,1)} %collective-permute-done.7.w2, ...), custom_call_target="tpu_custom_call" | custom-call | flops 2147483648 | bytes 9437184 | tf_op jit(solution)/shard_map/input_grad/pallas_call | solution.py:194
  176.1 10.8 %last.1 = (f32[1024,512]{1,0:T(8,128)}, f32[1024,512]{1,0:T(8,128)}, f32[64,512]{1,0:T(8,128)}) custom-call(s32[1]{0:T(128)} %bitcast.1.core_ref, f32[4,64,640]{2,1,0:T(8,128)} %all-to-all-done.5.got_ref, f32[2,64,512]{2,1,0:T(8,128)S(1)} %get-tuple-element.20.p_ref, f32[1024,512]{1,0:T(8,128)S(1)} %copy-done.3), custom_call_target="tpu_custom_call" | custom-call | tf_op jit(solution)/shard_map/last/pallas_call | solution.py:126
  (48 shorter events, 10.6 us)
Async XLA Ops:
  0.6 99.0 %copy-start = (bf16[1024,512]{1,0:T(8,128)(2,1)S(1)}, bf16[1024,512]{1,0:T(8,128)(2,1)}, u32[]{:S(2)}) copy-start(bf16[1024,512]{1,0:T(8,128)(2,1)} %param.8) | copy-start | bytes 3145732
  4.3 2.6 %copy-start.9 = (bf16[512,512]{1,0:T(8,128)(2,1)S(1)}, bf16[512,512]{1,0:T(8,128)(2,1)}, u32[]{:S(2)}) copy-start(bf16[512,512]{1,0:T(8,128)(2,1)} %cot_ref.1) | copy-start | bytes 1572868
  5.3 15.1 %collective-permute-start.1 = (bf16[1024,256]{1,0:T(8,128)(2,1)}, bf16[1024,256]{1,0:T(8,128)(2,1)}, u32[]{:S(2)}, u32[]{:S(2)}) collective-permute-start(bf16[1024,256]{1,0:T(8,128)(2,1)} %get-tuple-element.26), channel_id=1, source_target_pairs={{0,1},{1,0},{2,3},{3,2},{4,5},{5,4},{6,7},{7,6},{8,9},{9,8},{10,11... | collective-permute-start | bytes 1572872 | tf_op jit(solution)/shard_map/ppermute | solution.py:223
  13.8 16.0 %collective-permute-start.4 = (bf16[1024,256]{1,0:T(8,128)(2,1)S(1)}, bf16[1024,256]{1,0:T(8,128)(2,1)S(1)}, u32[]{:S(2)}, u32[]{:S(2)}) collective-permute-start(bf16[1024,256]{1,0:T(8,128)(2,1)S(1)} %get-tuple-element.24), channel_id=1, source_target_pairs={{0,3},{1,2},{2,1},{3,0},{4,7},{5,6},{6,5},{7,4},{8,11},{9,10},{10,... | collective-permute-start | bytes 1572872 | tf_op jit(solution)/shard_map/ppermute | solution.py:223
  16.0 16.5 %collective-permute-start = (bf16[1024,256]{1,0:T(8,128)(2,1)}, bf16[1024,256]{1,0:T(8,128)(2,1)}, u32[]{:S(2)}, u32[]{:S(2)}) collective-permute-start(bf16[1024,256]{1,0:T(8,128)(2,1)} %get-tuple-element.27), channel_id=1, source_target_pairs={{0,1},{1,0},{2,3},{3,2},{4,5},{5,4},{6,7},{7,6},{8,9},{9,8},{10,11... | collective-permute-start | bytes 1572872 | tf_op jit(solution)/shard_map/ppermute | solution.py:224
  16.7 24.5 %collective-permute-start.3 = (bf16[1024,256]{1,0:T(8,128)(2,1)}, bf16[1024,256]{1,0:T(8,128)(2,1)}, u32[]{:S(2)}, u32[]{:S(2)}) collective-permute-start(bf16[1024,256]{1,0:T(8,128)(2,1)} %get-tuple-element.25), channel_id=1, source_target_pairs={{0,3},{1,2},{2,1},{3,0},{4,7},{5,6},{6,5},{7,4},{8,11},{9,10},{10,... | collective-permute-start | bytes 1572872 | tf_op jit(solution)/shard_map/ppermute | solution.py:224
  22.4 28.6 %collective-permute-start.2 = (bf16[1024,256]{1,0:T(8,128)(2,1)}, bf16[1024,256]{1,0:T(8,128)(2,1)}, u32[]{:S(2)}, u32[]{:S(2)}) collective-permute-start(bf16[1024,256]{1,0:T(8,128)(2,1)} %fusion.1), channel_id=1, source_target_pairs={{0,3},{1,2},{2,1},{3,0},{4,7},{5,6},{6,5},{7,4},{8,11},{9,10},{10,... | collective-permute-start | bytes 1572872 | tf_op jit(solution)/shard_map/ppermute | solution.py:227
  31.8 19.2 %collective-permute-start.5 = (bf16[1024,256]{1,0:T(8,128)(2,1)}, bf16[1024,256]{1,0:T(8,128)(2,1)}, u32[]{:S(2)}, u32[]{:S(2)}) collective-permute-start(bf16[1024,256]{1,0:T(8,128)(2,1)} %fusion), channel_id=1, source_target_pairs={{0,1},{1,0},{2,3},{3,2},{4,5},{5,4},{6,7},{7,6},{8,9},{9,8},{10,11... | collective-permute-start | bytes 1572872 | tf_op jit(solution)/shard_map/ppermute | solution.py:227
  51.0 1.6 copy-start.1
  52.6 1.6 copy-start.4
  58.6 1.3 copy-start.2
  59.9 2.1 %collective-permute-start.10 = (bf16[512,512]{1,0:T(8,128)(2,1)}, bf16[512,512]{1,0:T(8,128)(2,1)S(1)}, u32[]{:S(2)}, u32[]{:S(2)}) collective-permute-start(bf16[512,512]{1,0:T(8,128)(2,1)} %get-tuple-element.17), channel_id=1, source_target_pairs={{0,4},{4,0},{1,5},{5,1},{2,6},{6,2},{3,7},{7,3},{8,12},{12,8},{9,1... | collective-permute-start | bytes 1572872 | tf_op jit(solution)/shard_map/ppermute | solution.py:242
  96.2 13.8 %all-to-all-start.2 = ((f32[8,16,512]{2,1,0:T(8,128)}), f32[8,16,512]{2,1,0:T(8,128)S(1)}, u32[]{:S(2)}, u32[]{:S(2)}) async-start(f32[8,16,512]{2,1,0:T(8,128)} %broadcast_in_dim.14), calls=%async_computation.2 | async-start | bytes 524288 | tf_op jit(solution)/shard_map/all_to_all | solution.py:232
  99.7 16.4 %copy-start.5 = (bf16[512,512]{1,0:T(8,128)(2,1)}, bf16[512,512]{1,0:T(8,128)(2,1)S(1)}, u32[]{:S(2)}) copy-start(bf16[512,512]{1,0:T(8,128)(2,1)S(1)} %constant_dynamic-slice_fusion.w0) | copy-start | bytes 1572868
  99.7 16.4 %collective-permute-start.6 = (bf16[512,512]{1,0:T(8,128)(2,1)S(1)}, bf16[512,512]{1,0:T(8,128)(2,1)S(1)}, u32[]{:S(2)}, u32[]{:S(2)}) collective-permute-start(bf16[512,512]{1,0:T(8,128)(2,1)S(1)} %constant_dynamic-slice_fusion.w0), channel_id=1, source_target_pairs={{0,1},{1,2},{2,3},{3,0},{4,5},{5,6},{6,7},{7,4},{8,9},{9,10},{10,1... | collective-permute-start | bytes 1572872 | tf_op jit(solution)/shard_map/ppermute | solution.py:253
  99.8 23.7 %collective-permute-start.7 = (bf16[512,512]{1,0:T(8,128)(2,1)S(1)}, bf16[512,512]{1,0:T(8,128)(2,1)}, u32[]{:S(2)}, u32[]{:S(2)}) collective-permute-start(bf16[512,512]{1,0:T(8,128)(2,1)S(1)} %constant_dynamic-slice_fusion.w0), channel_id=1, source_target_pairs={{0,2},{1,3},{2,0},{3,1},{4,6},{5,7},{6,4},{7,5},{8,10},{9,11},{10,... | collective-permute-start | bytes 1572872 | tf_op jit(solution)/shard_map/ppermute | solution.py:253
  103.4 20.3 %collective-permute-start.8 = (bf16[512,512]{1,0:T(8,128)(2,1)S(1)}, bf16[512,512]{1,0:T(8,128)(2,1)}, u32[]{:S(2)}, u32[]{:S(2)}) collective-permute-start(bf16[512,512]{1,0:T(8,128)(2,1)S(1)} %constant_dynamic-slice_fusion.w0), channel_id=1, source_target_pairs={{0,3},{1,0},{2,1},{3,2},{4,7},{5,4},{6,5},{7,6},{8,11},{9,8},{10,9... | collective-permute-start | bytes 1572872 | tf_op jit(solution)/shard_map/ppermute | solution.py:253
  111.1 15.4 %all-to-all-start.3 = ((f32[4,128,512]{2,1,0:T(8,128)}), f32[4,128,512]{2,1,0:T(8,128)S(1)}, u32[]{:S(2)}, u32[]{:S(2)}) async-start(f32[4,128,512]{2,1,0:T(8,128)} %broadcast_in_dim.15), calls=%async_computation.3 | async-start | bytes 2097152 | tf_op jit(solution)/shard_map/all_to_all | solution.py:232
  116.1 10.4 %copy-start.7 = (bf16[512,512]{1,0:T(8,128)(2,1)}, bf16[512,512]{1,0:T(8,128)(2,1)S(1)}, u32[]{:S(2)}) copy-start(bf16[512,512]{1,0:T(8,128)(2,1)S(1)} %collective-permute-done.6.w1) | copy-start | bytes 1572868
  123.7 8.7 %copy-start.11 = (f32[512,64]{0,1:T(8,128)S(1)}, f32[512,64]{0,1:T(8,128)}, u32[]{:S(2)}) copy-start(f32[512,64]{0,1:T(8,128)} %param.10) | copy-start | bytes 393220
  126.5 38.2 %collective-permute-start.9 = (bf16[4,512,512]{2,1,0:T(8,128)(2,1)}, bf16[4,512,512]{2,1,0:T(8,128)(2,1)}, u32[]{:S(2)}, u32[]{:S(2)}) collective-permute-start(bf16[4,512,512]{2,1,0:T(8,128)(2,1)} %pad_maximum_fusion), channel_id=1, source_target_pairs={{0,4},{4,0},{1,5},{5,1},{2,6},{6,2},{3,7},{7,3},{8,12},{12,8},{9,1... | collective-permute-start | bytes 6291464 | tf_op jit(solution)/shard_map/ppermute | solution.py:255
  126.5 5.9 %collective-permute-start.11 = (f32[512,512]{1,0:T(8,128)S(1)}, f32[512,512]{1,0:T(8,128)S(1)}, u32[]{:S(2)}, u32[]{:S(2)}) collective-permute-start(f32[512,512]{1,0:T(8,128)S(1)} %bitcast.35), channel_id=1, source_target_pairs={{0,4},{4,0},{1,5},{5,1},{2,6},{6,2},{3,7},{7,3},{8,12},{12,8},{9,1... | collective-permute-start | bytes 3145736 | tf_op jit(solution)/shard_map/ppermute | solution.py:249
  160.4 15.7 %all-to-all-start.5 = ((f32[4,64,640]{2,1,0:T(8,128)}), f32[4,64,640]{2,1,0:T(8,128)}, u32[]{:S(2)}, u32[]{:S(2)}) async-start(f32[4,64,640]{2,1,0:T(8,128)} %get-tuple-element.19), calls=%async_computation.5 | async-start | bytes 1310720 | tf_op jit(solution)/shard_map/all_to_all | solution.py:263
  164.7 11.4 %copy-start.3 = (f32[1024,512]{1,0:T(8,128)S(1)}, f32[1024,512]{1,0:T(8,128)}, u32[]{:S(2)}) copy-start(f32[1024,512]{1,0:T(8,128)} %copy-done.2) | copy-start | bytes 6291460
  164.7 1.2 copy-start.6
  165.9 1.0 copy-start.8
  166.9 1.0 copy-start.10

commit v3 on v2

v3 whole, which is shorter than its diff:
```python
import jax
import jax.numpy as jnp
from jax import lax
from jax.experimental import pallas as pl
from jax.experimental.pallas import tpu as pltpu
from jax.sharding import Mesh
from jax.sharding import PartitionSpec as P

ITERS = 2
NX, NZ, NC, NY = 4, 8, 2, 4
DP = ("x", "z", "core")
D, KVC, R, TOK = 4096, 512, 64, 512
ROWS = D // NY
HALF = ROWS // NC
WIDE = KVC + 128
HI = lax.Precision.HIGHEST
f32, bf16 = jnp.float32, jnp.bfloat16
SWAP = [(0, 1), (1, 0)]
FLIP = [(i, i ^ 1) for i in range(NY)]
MIRROR = [(i, 3 - i) for i in range(NY)]
VMEM_LIMIT = 24 * 1024 * 1024


def params(**kw):
    return pltpu.CompilerParams(vmem_limit_bytes=VMEM_LIMIT, **kw)


def sds(shape, dtype=f32):
    return jax.ShapeDtypeStruct(shape, dtype)


def whole(shape):
    return pl.BlockSpec(shape, lambda *_: (0,) * len(shape))


def dot(a, b, dims):
    return lax.dot_general(a, b, (dims, ((), ())), precision=HI, preferred_element_type=f32)


NT = ((1,), (1,))
NN = ((1,), (0,))
TN = ((0,), (0,))


def inverse_lower(block):
    lane = lax.broadcasted_iota(jnp.int32, (8, 128), 1)
    sub = lax.broadcasted_iota(jnp.int32, (8, 128), 0)
    tiles = [
        jnp.where(lane < R, block[8 * i : 8 * i + 8], jnp.where(lane - R == sub + 8 * i, 1.0, 0.0))
        for i in range(8)
    ]
    for k in range(0, R, 2):
        a, b = divmod(k, 8)
        row0, row1 = tiles[a][b : b + 1, :], tiles[a][b + 1 : b + 2, :]
        cross = row0[:, k + 1 : k + 2]
        scale0 = lax.rsqrt(row0[:, k : k + 1])
        below = cross * scale0
        scale1 = lax.rsqrt(row1[:, k + 1 : k + 2] - below * below)
        row0 = row0 * scale0
        row1 = (row1 - below * row0) * scale1
        for i in range(a, 8):
            col0 = tiles[i][:, k : k + 1] * scale0
            col1 = (tiles[i][:, k + 1 : k + 2] - col0 * below) * scale1
            new = (tiles[i] - col0 * row0) - col1 * row1
            if i == a:
                new = jnp.where(sub > b + 1, new, tiles[i])
                new = jnp.where(sub == b, row0, jnp.where(sub == b + 1, row1, new))
            tiles[i] = new
    return jnp.concatenate(tiles, axis=0)[:, R:]


def products(qt, half_ref, other_ref, p_ref, t_ref):
    z, g = [], []
    for n, ref in enumerate((half_ref, other_ref)):
        m = ref[...]
        p = dot(qt, m, NT)
        p_ref[n] = p
        z.append(dot(p, m, NN))
        g.append(dot(p, jnp.concatenate([p, jnp.zeros_like(p)], axis=0), NT))
    zt = z[0] + z[1]
    gram = g[0] + g[1]
    for s in range(NY):
        t_ref[s, :, :KVC] = zt
        t_ref[s, :, KVC:] = gram


def total(got_ref, lo, hi):
    return (got_ref[0, :, lo:hi] + got_ref[1, :, lo:hi]) + (got_ref[2, :, lo:hi] + got_ref[3, :, lo:hi])


def first_kernel(q_ref, half_ref, other_ref, t_ref, p_ref):
    products(q_ref[...], half_ref, other_ref, p_ref, t_ref)


def next_kernel(got_ref, half_ref, other_ref, t_ref, p_ref):
    inv = inverse_lower(total(got_ref, KVC, WIDE))
    qt = dot(inv, total(got_ref, 0, KVC), NN)
    products(qt, half_ref, other_ref, p_ref, t_ref)


def first(qt, half, other):
    return pl.pallas_call(
        first_kernel, name="first", out_shape=(sds((NY, R, WIDE)), sds((2, R, HALF))), compiler_params=params()
    )(qt, half, other)


def following(got, half, other):
    return pl.pallas_call(
        next_kernel, name="following", out_shape=(sds((NY, R, WIDE)), sds((2, R, HALF))), compiler_params=params()
    )(got, half, other)


def last_kernel(core_ref, got_ref, p_ref, keep_ref, rest_ref, approx_ref, err_ref, q_ref, ph):
    i = pl.program_id(0)

    @pl.when(i == 0)
    def _():
        inv = inverse_lower(total(got_ref, KVC, WIDE))
        q_ref[...] = dot(inv, total(got_ref, 0, KVC), NN)
        for n in range(2):
            p = dot(inv, p_ref[n], NN)
            ph[2 * n] = p[:, : HALF // 2]
            ph[2 * n + 1] = p[:, HALF // 2 :]

    approx = dot(ph[i], q_ref[...], TN)
    approx_ref[...] = approx

    @pl.when(i < 2)
    def _():
        err_ref[...] = keep_ref[...] - approx

    @pl.when(i >= 2)
    def _():
        err_ref[...] = rest_ref[...] - approx


def last(core, got, p, keep, rest):
    rows = HALF // 2
    place = pl.BlockSpec((rows, KVC), lambda i, c: ((i + 2 * c[0]) % 4, 0))
    return pl.pallas_call(
        last_kernel,
        name="last",
        grid_spec=pltpu.PrefetchScalarGridSpec(
            num_scalar_prefetch=1,
            grid=(4,),
            in_specs=[
                whole((NY, R, WIDE)),
                whole((2, R, HALF)),
                pl.BlockSpec((rows, KVC), lambda i, c: (jnp.minimum(i, 1), 0)),
                pl.BlockSpec((rows, KVC), lambda i, c: (jnp.maximum(i - 2, 0), 0)),
            ],
            out_specs=[place, place, whole((R, KVC))],
            scratch_shapes=[pltpu.VMEM((4, R, rows), f32)],
        ),
        out_shape=(sds((ROWS, KVC)), sds((ROWS, KVC)), sds((R, KVC))),
        compiler_params=params(),
    )(core, got, p, keep, rest)


def input_grad_kernel(at_ref, cot_ref, w0, w1, w2, w3, *refs):
    out_ref = refs[-1]
    for g, w in enumerate((w0, w1, w2, w3)):

        @pl.when(pl.program_id(0) == g)
        def _(w=w):
            out_ref[...] = lax.dot_general(
                cot_ref[...], w[...], (NT, ((), ())), preferred_element_type=f32
            ).astype(bf16)


def input_grad_of(at, cot, pieces, before=None):
    piece = whole((HALF, KVC))
    extra = [] if before is None else [before]
    return pl.pallas_call(
        input_grad_kernel,
        name="input_grad",
        grid_spec=pltpu.PrefetchScalarGridSpec(
            num_scalar_prefetch=1,
            grid=(NY,),
            in_specs=[whole((TOK, KVC))] + [piece] * NY + [pl.BlockSpec(memory_space=pl.ANY) for _ in extra],
            out_specs=pl.BlockSpec((TOK, HALF), lambda i, a: (0, a[i])),
        ),
        out_shape=sds((TOK, D), bf16),
        input_output_aliases={} if before is None else {2 + NY: 0},
        compiler_params=params(),
        cost_estimate=pl.CostEstimate(flops=TOK * D * KVC, bytes_accessed=5 << 20, transcendentals=0),
    )(at, cot, *pieces, *extra)


def scatter_y(acts, cot, error, scale, y):
    def term(block, half):
        rows = lax.dynamic_slice(acts, (0, block * ROWS + half * HALF), (TOK, HALF))
        return jnp.einsum("tr,tk->rk", rows, cot, preferred_element_type=f32)

    near = (y ^ 1, y ^ 3)
    pairs = (FLIP, MIRROR)
    firsts = [lax.ppermute(term(y ^ 2, n).astype(bf16), "y", pairs[n]) for n in range(2)]
    seconds = [lax.ppermute(term(near[n], n).astype(bf16), "y", pairs[n]) for n in range(2)]
    mids = [lax.optimization_barrier(term(near[1 - n], n)) for n in range(2)]
    owns = [lax.optimization_barrier(error[n * HALF : (n + 1) * HALF] + scale * term(y, n)) for n in range(2)]
    onward = [
        lax.ppermute((firsts[n].astype(f32) + mids[n]).astype(bf16), "y", pairs[1 - n]) for n in range(2)
    ]
    bases = [lax.optimization_barrier(owns[n] + scale * seconds[n].astype(f32)) for n in range(2)]
    return [bases[n] + scale * onward[n].astype(f32) for n in range(2)]


def everyone(t, axis, n):
    return lax.all_to_all(jnp.broadcast_to(t, (n, *t.shape)), axis, 0, 0, tiled=True)


def body(acts, cotangent, weight, error_buf, q_init, inv_scale):
    y, core = lax.axis_index("y"), lax.axis_index("core")
    low, high = scatter_y(acts, cotangent, error_buf[0], inv_scale, y)
    keep = jnp.where(core == 0, low, high)
    rest = jnp.where(core == 0, high, low)

    give, weight = lax.optimization_barrier((rest.astype(bf16), weight))
    pair = keep + lax.ppermute(give, "core", SWAP).astype(f32)
    along_x = lax.all_to_all(pair.astype(bf16).reshape(NX, 128, KVC), "x", 0, 0, tiled=True)
    row = jnp.sum(along_x.astype(f32), axis=0)
    along_z = lax.all_to_all(row.reshape(NZ, 16, KVC), "z", 0, 0, tiled=True)
    rows = jnp.sum(along_z, axis=0) * (1.0 / (NX * NZ * NC))
    block = everyone(rows, "z", NZ).reshape(128, KVC)

    mine = lax.dynamic_slice_in_dim(weight, core * HALF, HALF, 0)
    pieces = [mine] + [
        lax.ppermute(mine, "y", [(i, (i + s) % NY) for i in range(NY)]) for s in range(1, NY)
    ]
    block, *pieces = lax.optimization_barrier((block, *pieces))

    half = everyone(block, "x", NX).reshape(HALF, KVC)
    other = lax.ppermute(half, "core", SWAP)
    other, *pieces = lax.optimization_barrier((other, *pieces))
    others = [lax.ppermute(piece, "core", SWAP) for piece in pieces]
    source = (y - jnp.arange(NY)) % NY

    t, p = first(q_init.T, half, other)
    input_grad = input_grad_of(2 * source + core, cotangent, pieces)
    for _ in range(ITERS - 1):
        got = lax.all_to_all(t, "y", 0, 0, tiled=True)
        got, input_grad = lax.optimization_barrier((got, input_grad))
        t, p = following(got, half, other)
    input_grad = input_grad_of(2 * source + 1 - core, cotangent, others, input_grad)
    approx, new_error, qt = last(core[None], lax.all_to_all(t, "y", 0, 0, tiled=True), p, keep, rest)
    return (input_grad, approx, new_error[None], qt.T)


def solution(mesh):
    fine = Mesh(mesh.devices.reshape(NX, NZ, NC, NY), ("x", "z", "core", "y"))
    every = P((*DP, "y"), None)
    in_specs = (every, every, P("y", None), P(DP, "y", None), P(), P())
    out_specs = (every, P("y", None), P(DP, "y", None), P())
    return jax.shard_map(body, mesh=fine, in_specs=in_specs, out_specs=out_specs, check_vma=False)
```

time: 189 us -> 189 us (level)
  blocking collectives: 46.8 us -> 30.8 us
  matrix products: 8.41 us -> 18.6 us
  starting transfers between devices: 25.5 us -> 30.3 us
  local copies, waits for them, and re-layouts: 12.8 us -> 9.18 us
  Pallas kernels: 36.5 us -> 39.3 us
  waiting for transfers between devices: 47 us -> 49.1 us
    all_to_all x2 -> x1, blocking collectives: 33.9 us -> 17.7 us  [everyone(): lax.all_to_all(jnp.broadcast_to(t, (n, *t.shape)), axis, 0, 0, tiled=True)]
    all_to_all x0 -> x2, starting transfers between devices: none -> 12 us  [the longest x1 8.47 us: body(): along_z = lax.all_to_all(row.reshape(NZ, 16, KVC), 'z', 0, 0, tiled=True)]
    dot_general x2 -> x8, matrix products: 8.41 us -> 18.6 us  [term(): return jnp.einsum('tr,tk->rk', rows, cot, preferred_element_type=f32)]
    all_to_all x0 -> x2, waiting for transfers between devices: none -> 9.1 us  [the longest x1 6.57 us: body(): along_z = lax.all_to_all(row.reshape(NZ, 16, KVC), 'z', 0, 0, tiled=True)]
    ppermute x7 -> x10, waiting for transfers between devices: 26 us -> 19 us  [the longest x2 10.6 us: scatter_y(): lax.ppermute((firsts[n].astype(f32) + mids[n]).astype(bf16), 'y', pairs[1...]
    all_to_all x2 -> x1, waiting for transfers between devices: 5.92 us -> 0.01 us  [everyone(): lax.all_to_all(jnp.broadcast_to(t, (n, *t.shape)), axis, 0, 0, tiled=True)]
    all_to_all x1, waiting for transfers between devices: 0.01 us -> 5.13 us  [body(): lax.all_to_all(t, 'y', 0, 0, tiled=True)]
    all_to_all x2 -> x1, starting transfers between devices: 8.36 us -> 3.41 us  [everyone(): lax.all_to_all(jnp.broadcast_to(t, (n, *t.shape)), axis, 0, 0, tiled=True)]
  transfers between devices with their start and end apart: 15 -> 19, of which waited for: 9 -> 10; matrix products, arithmetic and copies ran while one was open for 8% -> 12% of each run, Pallas kernels for 11% -> 12%
where the time goes in v3:
time: 189 us; the launch traced here: 187 us
  waiting for transfers between devices  49.1 us (26%)
  Pallas kernels  39.3 us (21%)
  blocking collectives  30.8 us (16%)
  starting transfers between devices  30.3 us (16%)
  matrix products  18.6 us (10%)
  local copies, waits for them, and re-layouts  9.18 us (5%)
  other arithmetic  8.63 us (5%)
    dot_general x8, matrix products, term(): return jnp.einsum('tr,tk->rk', rows, cot, preferred_element_type=f32)  18.6 us
    all_to_all x1, blocking collectives, everyone(): lax.all_to_all(jnp.broadcast_to(t, (n, *t.shape)), axis, 0, 0, tiled=True)  17.7 us
    pallas_call x1, Pallas kernels, last(): pl.pallas_call(last_kernel, name='last', grid_spec=pltpu.PrefetchScalarGr...  13.5 us
    all_to_all x1, blocking collectives, body(): lax.all_to_all(pair.astype(bf16).reshape(NX, 128, KVC), 'x', 0, 0, tiled=...  13.1 us
    pallas_call x1, Pallas kernels, following(): pl.pallas_call(next_kernel, name='following', out_shape=(sds((NY, R, WIDE...  12.6 us
    ppermute x3, waiting for transfers between devices, body(): lax.ppermute(mine, 'y', [(i, (i + s) % NY) for i in range(NY)])  11.3 us
    ppermute x2, waiting for transfers between devices, scatter_y(): lax.ppermute((firsts[n].astype(f32) + mids[n]).astype(bf16), 'y', pairs[1...  10.6 us
    pallas_call x2, Pallas kernels, input_grad_of(): pl.pallas_call(input_grad_kernel, name='input_grad', grid_spec=pltpu.Pref...  9.79 us
  transfers between devices with their start and end apart: 19, of which 10 were waited for; matrix products, arithmetic and copies ran while one was open for 12% of the time, Pallas kernels for 12%

profile of v3, /device:TPU:2, one launch (start us, length us, event | category | flops | bytes accessed | tf_op | source)
XLA Modules:
  0.0 187.4 jit_solution(16969847940625781692)
XLA Ops:
  0.7 2.6 %convolution_convert_fusion = bf16[512,512]{1,0:T(8,128)(2,1)} fusion(bf16[512,512]{1,0:T(8,128)(2,1)} %cot_ref.3, bf16[512,4096]{1,0:T(8,128)(2,1)} %param.6, s32[]{:T(128)S(6)} %select_n.54), kind=kOutput, calls=%fused_computation.4 | convolution fusion | flops 268697600 | bytes 1572868 | tf_op jit(solution)/shard_map/tr,tk->rk/dot_general | solution.py:193
  3.2 3.0 %collective-permute-start.4 = (bf16[512,512]{1,0:T(8,128)(2,1)}, bf16[512,512]{1,0:T(8,128)(2,1)}, u32[]{:S(2)}, u32[]{:S(2)}) collective-permute-start(bf16[512,512]{1,0:T(8,128)(2,1)} %convolution_convert_fusion), channel_id=1, source_target_pairs={{0,3},{1,2},{2,1},{3,0},{4,7},{5,6},{6,5},{7,4},{8,11},{9,10},{10,... | collective-permute-start | bytes 1572872 | tf_op jit(solution)/shard_map/ppermute | solution.py:197
  6.3 2.5 %convolution_convert_fusion.3 = bf16[512,512]{1,0:T(8,128)(2,1)} fusion(bf16[512,512]{1,0:T(8,128)(2,1)} %cot_ref.3, bf16[512,4096]{1,0:T(8,128)(2,1)} %param.6, s32[]{:T(128)S(6)} %select_n.49), kind=kOutput, calls=%fused_computation.7 | convolution fusion | flops 268697600 | bytes 1572868 | tf_op jit(solution)/shard_map/tr,tk->rk/dot_general | solution.py:193
  8.9 2.5 %convolution_convert_fusion.2 = bf16[512,512]{1,0:T(8,128)(2,1)} fusion(bf16[512,512]{1,0:T(8,128)(2,1)} %cot_ref.3, bf16[512,4096]{1,0:T(8,128)(2,1)} %param.6, s32[]{:T(128)S(6)} %select_n.50), kind=kOutput, calls=%fused_computation.6 | convolution fusion | flops 268697600 | bytes 1572868 | tf_op jit(solution)/shard_map/tr,tk->rk/dot_general | solution.py:193
  11.3 1.9 %collective-permute-start.1 = (bf16[512,512]{1,0:T(8,128)(2,1)}, bf16[512,512]{1,0:T(8,128)(2,1)}, u32[]{:S(2)}, u32[]{:S(2)}) collective-permute-start(bf16[512,512]{1,0:T(8,128)(2,1)} %convolution_convert_fusion.2), channel_id=1, source_target_pairs={{0,1},{1,0},{2,3},{3,2},{4,5},{5,4},{6,7},{7,6},{8,9},{9,8},{10,11... | collective-permute-start | bytes 1572872 | tf_op jit(solution)/shard_map/ppermute | solution.py:197
  13.2 2.3 %convolution_convert_fusion.1 = bf16[512,512]{1,0:T(8,128)(2,1)} fusion(bf16[512,512]{1,0:T(8,128)(2,1)S(1)} %copy-done.1, bf16[512,4096]{1,0:T(8,128)(2,1)} %param.6, s32[]{:T(128)S(6)} %select_n.53), kind=kOutput, calls=%fused_computation.5 | convolution fusion | flops 268697600 | bytes 1572868 | tf_op jit(solution)/shard_map/tr,tk->rk/dot_general | solution.py:193
  16.4 2.8 %fusion = f32[512,512]{1,0:T(8,128)} fusion(bf16[512,512]{1,0:T(8,128)(2,1)S(1)} %copy-done.1, f32[1,1024,512]{2,1,0:T(8,128)} %param.9, bf16[512,4096]{1,0:T(8,128)(2,1)} %param.6, s32[]{:T(128)S(6)} %select_n.52, f32[]{:T(128)S(6)} %copy.12), kind=kOutput, calls=%fused_computation.1 | convolution fusion | flops 268959744 | bytes 3145736 | tf_op jit(solution)/shard_map/tr,tk->rk/dot_general | solution.py:193
  19.2 2.8 %fusion.1 = f32[512,512]{1,0:T(8,128)} fusion(bf16[512,512]{1,0:T(8,128)(2,1)S(1)} %copy-done.1, f32[1,1024,512]{2,1,0:T(8,128)} %param.9, bf16[512,4096]{1,0:T(8,128)(2,1)} %param.6, s32[]{:T(128)S(6)} %select_n.48, f32[]{:T(128)S(6)} %copy.12), kind=kOutput, calls=%fused_computation.3 | convolution fusion | flops 268959744 | bytes 3145736 | tf_op jit(solution)/shard_map/tr,tk->rk/dot_general | solution.py:193
  22.1 1.5 fusion.9
  23.6 1.6 fusion.4
  25.3 8.4 %collective-permute-done.1 = bf16[512,512]{1,0:T(8,128)(2,1)} collective-permute-done((bf16[512,512]{1,0:T(8,128)(2,1)}, bf16[512,512]{1,0:T(8,128)(2,1)}, u32[]{:S(2)}, u32[]{:S(2)}) %collective-permute-start.1) | collective-permute-done | bytes 524320 | tf_op jit(solution)/shard_map/ppermute | solution.py:197
  38.2 10.4 %collective-permute-done.2 = bf16[512,512]{1,0:T(8,128)(2,1)S(1)} collective-permute-done((bf16[512,512]{1,0:T(8,128)(2,1)S(1)}, bf16[512,512]{1,0:T(8,128)(2,1)S(1)}, u32[]{:S(2)}, u32[]{:S(2)}) %collective-permute-start.2) | collective-permute-done | bytes 524320 | tf_op jit(solution)/shard_map/ppermute | solution.py:202
  50.1 1.9 %collective-permute-done.6 = bf16[512,512]{1,0:T(8,128)(2,1)S(1)} collective-permute-done((bf16[512,512]{1,0:T(8,128)(2,1)S(1)}, bf16[512,512]{1,0:T(8,128)(2,1)S(1)}, u32[]{:S(2)}, u32[]{:S(2)}) %collective-permute-start.6) | collective-permute-done | bytes 524320 | tf_op jit(solution)/shard_map/ppermute | solution.py:219
  52.0 1.4 add_convert_fusion
  53.4 13.1 %all_to_all.30 = bf16[4,128,512]{2,1,0:T(8,128)(2,1)S(1)} all-to-all(bf16[4,128,512]{2,1,0:T(8,128)(2,1)S(1)} %bitcast.24), channel_id=1, replica_groups=mesh['x'=4,'z'=8,'core'=2,'y'=4] {'x'}, dimensions={0} | all-to-all | bytes 1048576 | tf_op jit(solution)/shard_map/all_to_all | solution.py:220
  67.3 8.5 %all-to-all-start.1 = ((f32[8,16,512]{2,1,0:T(8,128)}), f32[8,16,512]{2,1,0:T(8,128)S(1)}, u32[]{:S(2)}, u32[]{:S(2)}) async-start(f32[8,16,512]{2,1,0:T(8,128)} %bitcast.3), calls=%async_computation.1 | async-start | bytes 524288 | tf_op jit(solution)/shard_map/all_to_all | solution.py:222
  75.8 3.0 %collective-permute-start.9 = (bf16[512,512]{1,0:T(8,128)(2,1)S(1)}, bf16[512,512]{1,0:T(8,128)(2,1)S(1)}, u32[]{:S(2)}, u32[]{:S(2)}) collective-permute-start(bf16[512,512]{1,0:T(8,128)(2,1)S(1)} %constant_dynamic-slice_fusion.w0), channel_id=1, source_target_pairs={{0,3},{1,0},{2,1},{3,2},{4,7},{5,4},{6,5},{7,6},{8,11},{9,8},{10,9... | collective-permute-start | bytes 1572872 | tf_op jit(solution)/shard_map/ppermute | solution.py:228
  79.9 6.6 %all-to-all-done.1 = f32[8,16,512]{2,1,0:T(8,128)S(1)} async-done(((f32[8,16,512]{2,1,0:T(8,128)}), f32[8,16,512]{2,1,0:T(8,128)S(1)}, u32[]{:S(2)}, u32[]{:S(2)}) %all-to-all-start.1) | async-done | bytes 262176 | tf_op jit(solution)/shard_map/all_to_all | solution.py:222
  88.6 3.4 %all-to-all-start.2 = ((f32[8,16,512]{2,1,0:T(8,128)}), f32[8,16,512]{2,1,0:T(8,128)S(1)}, u32[]{:S(2)}, u32[]{:S(2)}) async-start(f32[8,16,512]{2,1,0:T(8,128)} %broadcast_in_dim.12), calls=%async_computation.2 | async-start | bytes 524288 | tf_op jit(solution)/shard_map/all_to_all | solution.py:209
  92.0 7.7 %collective-permute-done.9.w3 = bf16[512,512]{1,0:T(8,128)(2,1)S(1)} collective-permute-done((bf16[512,512]{1,0:T(8,128)(2,1)S(1)}, bf16[512,512]{1,0:T(8,128)(2,1)S(1)}, u32[]{:S(2)}, u32[]{:S(2)}) %collective-permute-start.9) | collective-permute-done | bytes 524320 | tf_op jit(solution)/shard_map/ppermute | solution.py:228
  99.8 3.5 %collective-permute-done.7.w1 = bf16[512,512]{1,0:T(8,128)(2,1)} collective-permute-done((bf16[512,512]{1,0:T(8,128)(2,1)S(1)}, bf16[512,512]{1,0:T(8,128)(2,1)}, u32[]{:S(2)}, u32[]{:S(2)}) %collective-permute-start.7) | collective-permute-done | bytes 524320 | tf_op jit(solution)/shard_map/ppermute | solution.py:228
  103.4 17.7 %all_to_all.31 = f32[4,128,512]{2,1,0:T(8,128)S(1)} all-to-all(f32[4,128,512]{2,1,0:T(8,128)S(1)} %broadcast_in_dim.13), channel_id=1, replica_groups=mesh['x'=4,'z'=8,'core'=2,'y'=4] {'x'}, dimensions={0} | all-to-all | bytes 2097152 | tf_op jit(solution)/shard_map/all_to_all | solution.py:209
  121.1 2.7 %collective-permute-done.10.other_ref = f32[512,512]{1,0:T(8,128)S(1)} collective-permute-done((f32[512,512]{1,0:T(8,128)S(1)}, f32[512,512]{1,0:T(8,128)S(1)}, u32[]{:S(2)}, u32[]{:S(2)}) %collective-permute-start.10) | collective-permute-done | bytes 1048608 | tf_op jit(solution)/shard_map/ppermute | solution.py:233
  123.8 3.4 %first.1 = (f32[4,64,640]{2,1,0:T(8,128)S(1)}, f32[2,64,512]{2,1,0:T(8,128)}) custom-call(f32[64,512]{1,0:T(8,128)S(1)} %bitcast.23, f32[512,512]{1,0:T(8,128)S(1)} %bitcast.21, f32[512,512]{1,0:T(8,128)S(1)} %collective-permute-done.10.other_ref), custom_call_target="tpu_custom_call" | custom-call | tf_op jit(solution)/shard_map/first/pallas_call | solution.py:102
  129.0 3.5 %all-to-all-start.4 = ((f32[4,64,640]{2,1,0:T(8,128)}), f32[4,64,640]{2,1,0:T(8,128)S(1)}, u32[]{:S(2)}, u32[]{:S(2)}) async-start(f32[4,64,640]{2,1,0:T(8,128)} %copy-done.9), calls=%async_computation.4 | async-start | bytes 1310720 | tf_op jit(solution)/shard_map/all_to_all | solution.py:241
  136.7 4.6 %input_grad.2.refs_0_ = bf16[512,4096]{1,0:T(8,128)(2,1)} custom-call(s32[4]{0:T(128)S(1)} %broadcast_add_fusion.at_ref, bf16[512,512]{1,0:T(8,128)(2,1)S(1)} %copy-done.1, bf16[512,512]{1,0:T(8,128)(2,1)S(1)} %copy-done.7, bf16[512,512]{1,0:T(8,128)(2,1)} %collective-permute-done.7.w1, bf16[512,512]{1,0:T(8,128)(2,1)S(1)} %copy-done.13, ...), custom_call_target="tpu_custom_call" | custom-call | flops 1073741824 | bytes 5242880 | tf_op jit(solution)/shard_map/input_grad/pallas_call | solution.py:174
  141.4 2.5 %all-to-all-done.4.got_ref = f32[4,64,640]{2,1,0:T(8,128)S(1)} async-done(((f32[4,64,640]{2,1,0:T(8,128)}), f32[4,64,640]{2,1,0:T(8,128)S(1)}, u32[]{:S(2)}, u32[]{:S(2)}) %all-to-all-start.4) | async-done | bytes 655392 | tf_op jit(solution)/shard_map/all_to_all | solution.py:241
  145.1 12.6 %following.1 = (f32[4,64,640]{2,1,0:T(8,128)S(1)}, f32[2,64,512]{2,1,0:T(8,128)S(1)}) custom-call(f32[4,64,640]{2,1,0:T(8,128)S(1)} %all-to-all-done.4.got_ref, f32[512,512]{1,0:T(8,128)S(1)} %bitcast.22, f32[512,512]{1,0:T(8,128)S(1)} %copy-done.5), custom_call_target="tpu_custom_call" | custom-call | tf_op jit(solution)/shard_map/following/pallas_call | solution.py:108
  158.6 3.7 %all-to-all-start.5 = ((f32[4,64,640]{2,1,0:T(8,128)}), f32[4,64,640]{2,1,0:T(8,128)S(1)}, u32[]{:S(2)}, u32[]{:S(2)}) async-start(f32[4,64,640]{2,1,0:T(8,128)} %copy-done.8), calls=%async_computation.5 | async-start | bytes 1310720 | tf_op jit(solution)/shard_map/all_to_all | solution.py:245
  162.4 5.1 %input_grad.3 = bf16[512,4096]{1,0:T(8,128)(2,1)} custom-call(s32[4]{0:T(128)S(1)} %add_subtract_fusion.at_ref, bf16[512,512]{1,0:T(8,128)(2,1)S(1)} %copy-done.1, bf16[512,512]{1,0:T(8,128)(2,1)} %collective-permute-done.11.w0, bf16[512,512]{1,0:T(8,128)(2,1)} %collective-permute-done.12.w1, ...), custom_call_target="tpu_custom_call", output_to_operand_aliasing={{}: (6, {})} | custom-call | flops 1073741824 | bytes 5242880 | tf_op jit(solution)/shard_map/input_grad/pallas_call | solution.py:174
  167.5 5.1 %all-to-all-done.5.got_ref = f32[4,64,640]{2,1,0:T(8,128)S(1)} async-done(((f32[4,64,640]{2,1,0:T(8,128)}), f32[4,64,640]{2,1,0:T(8,128)S(1)}, u32[]{:S(2)}, u32[]{:S(2)}) %all-to-all-start.5) | async-done | bytes 655392 | tf_op jit(solution)/shard_map/all_to_all | solution.py:245
  173.9 13.5 %last.1 = (f32[1024,512]{1,0:T(8,128)}, f32[1024,512]{1,0:T(8,128)}, f32[64,512]{1,0:T(8,128)}) custom-call(s32[1]{0:T(128)} %bitcast.7.core_ref, f32[4,64,640]{2,1,0:T(8,128)S(1)} %all-to-all-done.5.got_ref, f32[2,64,512]{2,1,0:T(8,128)S(1)} %get-tuple-element.40.p_ref, f32[512,512]{1,0:T(8,128)S(1)} %copy-done.3, f32[512,512]{1,0:T(8,128)S(1)} %copy-done.2), custom_call_target="tpu_custom_call" | custom-call | tf_op jit(solution)/shard_map/last/pallas_call | solution.py:140
  (69 shorter events, 20.0 us)
Async XLA Ops:
  0.6 75.1 %copy-start = (bf16[1024,512]{1,0:T(8,128)(2,1)S(1)}, bf16[1024,512]{1,0:T(8,128)(2,1)}, u32[]{:S(2)}) copy-start(bf16[1024,512]{1,0:T(8,128)(2,1)} %param.8) | copy-start | bytes 3145732
  0.6 12.6 %copy-start.1 = (bf16[512,512]{1,0:T(8,128)(2,1)S(1)}, bf16[512,512]{1,0:T(8,128)(2,1)}, u32[]{:S(2)}) copy-start(bf16[512,512]{1,0:T(8,128)(2,1)} %cot_ref.3) | copy-start | bytes 1572868
  3.2 32.0 %collective-permute-start.4 = (bf16[512,512]{1,0:T(8,128)(2,1)}, bf16[512,512]{1,0:T(8,128)(2,1)}, u32[]{:S(2)}, u32[]{:S(2)}) collective-permute-start(bf16[512,512]{1,0:T(8,128)(2,1)} %convolution_convert_fusion), channel_id=1, source_target_pairs={{0,3},{1,2},{2,1},{3,0},{4,7},{5,6},{6,5},{7,4},{8,11},{9,10},{10,... | collective-permute-start | bytes 1572872 | tf_op jit(solution)/shard_map/ppermute | solution.py:197
  8.7 29.3 %collective-permute-start = (bf16[512,512]{1,0:T(8,128)(2,1)}, bf16[512,512]{1,0:T(8,128)(2,1)S(1)}, u32[]{:S(2)}, u32[]{:S(2)}) collective-permute-start(bf16[512,512]{1,0:T(8,128)(2,1)} %convolution_convert_fusion.3), channel_id=1, source_target_pairs={{0,1},{1,0},{2,3},{3,2},{4,5},{5,4},{6,7},{7,6},{8,9},{9,8},{10,11... | collective-permute-start | bytes 1572872 | tf_op jit(solution)/shard_map/ppermute | solution.py:198
  11.3 22.3 %collective-permute-start.1 = (bf16[512,512]{1,0:T(8,128)(2,1)}, bf16[512,512]{1,0:T(8,128)(2,1)}, u32[]{:S(2)}, u32[]{:S(2)}) collective-permute-start(bf16[512,512]{1,0:T(8,128)(2,1)} %convolution_convert_fusion.2), channel_id=1, source_target_pairs={{0,1},{1,0},{2,3},{3,2},{4,5},{5,4},{6,7},{7,6},{8,9},{9,8},{10,11... | collective-permute-start | bytes 1572872 | tf_op jit(solution)/shard_map/ppermute | solution.py:197
  15.5 21.3 %collective-permute-start.3 = (bf16[512,512]{1,0:T(8,128)(2,1)}, bf16[512,512]{1,0:T(8,128)(2,1)}, u32[]{:S(2)}, u32[]{:S(2)}) collective-permute-start(bf16[512,512]{1,0:T(8,128)(2,1)} %convolution_convert_fusion.1), channel_id=1, source_target_pairs={{0,3},{1,2},{2,1},{3,0},{4,7},{5,6},{6,5},{7,4},{8,11},{9,10},{10,... | collective-permute-start | bytes 1572872 | tf_op jit(solution)/shard_map/ppermute | solution.py:198
  23.6 13.3 %copy-start.16 = (f32[512,512]{1,0:T(8,128)S(1)}, f32[512,512]{1,0:T(8,128)}, u32[]{:S(2)}) copy-start(f32[512,512]{1,0:T(8,128)} %fusion) | copy-start | bytes 3145732
  23.6 14.5 %copy-start.15 = (f32[512,512]{1,0:T(8,128)S(1)}, f32[512,512]{1,0:T(8,128)}, u32[]{:S(2)}) copy-start(f32[512,512]{1,0:T(8,128)} %fusion.1) | copy-start | bytes 3145732
  34.9 13.8 %collective-permute-start.2 = (bf16[512,512]{1,0:T(8,128)(2,1)S(1)}, bf16[512,512]{1,0:T(8,128)(2,1)S(1)}, u32[]{:S(2)}, u32[]{:S(2)}) collective-permute-start(bf16[512,512]{1,0:T(8,128)(2,1)S(1)} %add_convert_fusion.2), channel_id=1, source_target_pairs={{0,3},{1,2},{2,1},{3,0},{4,7},{5,6},{6,5},{7,4},{8,11},{9,10},{10,... | collective-permute-start | bytes 1572872 | tf_op jit(solution)/shard_map/ppermute | solution.py:202
  36.4 12.4 %collective-permute-start.5 = (bf16[512,512]{1,0:T(8,128)(2,1)S(1)}, bf16[512,512]{1,0:T(8,128)(2,1)S(1)}, u32[]{:S(2)}, u32[]{:S(2)}) collective-permute-start(bf16[512,512]{1,0:T(8,128)(2,1)S(1)} %add_convert_fusion.1), channel_id=1, source_target_pairs={{0,1},{1,0},{2,3},{3,2},{4,5},{5,4},{6,7},{7,6},{8,9},{9,8},{10,11... | collective-permute-start | bytes 1572872 | tf_op jit(solution)/shard_map/ppermute | solution.py:202
  50.1 1.9 %collective-permute-start.6 = (bf16[512,512]{1,0:T(8,128)(2,1)S(1)}, bf16[512,512]{1,0:T(8,128)(2,1)S(1)}, u32[]{:S(2)}, u32[]{:S(2)}) collective-permute-start(bf16[512,512]{1,0:T(8,128)(2,1)S(1)} %get-tuple-element.24), channel_id=1, source_target_pairs={{0,4},{4,0},{1,5},{5,1},{2,6},{6,2},{3,7},{7,3},{8,12},{12,8},{9,1... | collective-permute-start | bytes 1572872 | tf_op jit(solution)/shard_map/ppermute | solution.py:219
  53.4 70.4 %copy-start.14 = (f32[512,64]{0,1:T(8,128)S(1)}, f32[512,64]{0,1:T(8,128)}, u32[]{:S(2)}) copy-start(f32[512,64]{0,1:T(8,128)} %param.10) | copy-start | bytes 393220
  67.3 19.2 %all-to-all-start.1 = ((f32[8,16,512]{2,1,0:T(8,128)}), f32[8,16,512]{2,1,0:T(8,128)S(1)}, u32[]{:S(2)}, u32[]{:S(2)}) async-start(f32[8,16,512]{2,1,0:T(8,128)} %bitcast.3), calls=%async_computation.1 | async-start | bytes 524288 | tf_op jit(solution)/shard_map/all_to_all | solution.py:222
  75.8 27.5 %copy-start.6 = (bf16[512,512]{1,0:T(8,128)(2,1)}, bf16[512,512]{1,0:T(8,128)(2,1)S(1)}, u32[]{:S(2)}) copy-start(bf16[512,512]{1,0:T(8,128)(2,1)S(1)} %constant_dynamic-slice_fusion.w0) | copy-start | bytes 1572868
  75.8 24.0 %collective-permute-start.9 = (bf16[512,512]{1,0:T(8,128)(2,1)S(1)}, bf16[512,512]{1,0:T(8,128)(2,1)S(1)}, u32[]{:S(2)}, u32[]{:S(2)}) collective-permute-start(bf16[512,512]{1,0:T(8,128)(2,1)S(1)} %constant_dynamic-slice_fusion.w0), channel_id=1, source_target_pairs={{0,3},{1,0},{2,1},{3,2},{4,7},{5,4},{6,5},{7,6},{8,11},{9,8},{10,9... | collective-permute-start | bytes 1572872 | tf_op jit(solution)/shard_map/ppermute | solution.py:228
  78.8 21.0 %collective-permute-start.8 = (bf16[512,512]{1,0:T(8,128)(2,1)S(1)}, bf16[512,512]{1,0:T(8,128)(2,1)S(1)}, u32[]{:S(2)}, u32[]{:S(2)}) collective-permute-start(bf16[512,512]{1,0:T(8,128)(2,1)S(1)} %constant_dynamic-slice_fusion.w0), channel_id=1, source_target_pairs={{0,2},{1,3},{2,0},{3,1},{4,6},{5,7},{6,4},{7,5},{8,10},{9,11},{10,... | collective-permute-start | bytes 1572872 | tf_op jit(solution)/shard_map/ppermute | solution.py:228
  78.8 24.5 %collective-permute-start.7 = (bf16[512,512]{1,0:T(8,128)(2,1)S(1)}, bf16[512,512]{1,0:T(8,128)(2,1)}, u32[]{:S(2)}, u32[]{:S(2)}) collective-permute-start(bf16[512,512]{1,0:T(8,128)(2,1)S(1)} %constant_dynamic-slice_fusion.w0), channel_id=1, source_target_pairs={{0,1},{1,2},{2,3},{3,0},{4,5},{5,6},{6,7},{7,4},{8,9},{9,10},{10,1... | collective-permute-start | bytes 1572872 | tf_op jit(solution)/shard_map/ppermute | solution.py:228
  88.6 14.7 %all-to-all-start.2 = ((f32[8,16,512]{2,1,0:T(8,128)}), f32[8,16,512]{2,1,0:T(8,128)S(1)}, u32[]{:S(2)}, u32[]{:S(2)}) async-start(f32[8,16,512]{2,1,0:T(8,128)} %broadcast_in_dim.12), calls=%async_computation.2 | async-start | bytes 524288 | tf_op jit(solution)/shard_map/all_to_all | solution.py:209
  99.8 3.5 %copy-start.10 = (bf16[512,512]{1,0:T(8,128)(2,1)}, bf16[512,512]{1,0:T(8,128)(2,1)S(1)}, u32[]{:S(2)}) copy-start(bf16[512,512]{1,0:T(8,128)(2,1)S(1)} %collective-permute-done.9.w3) | copy-start | bytes 1572868
  99.8 29.2 %copy-start.12 = (bf16[512,512]{1,0:T(8,128)(2,1)}, bf16[512,512]{1,0:T(8,128)(2,1)S(1)}, u32[]{:S(2)}) copy-start(bf16[512,512]{1,0:T(8,128)(2,1)S(1)} %collective-permute-done.8.w2) | copy-start | bytes 1572868
  121.1 2.7 %collective-permute-start.10 = (f32[512,512]{1,0:T(8,128)S(1)}, f32[512,512]{1,0:T(8,128)S(1)}, u32[]{:S(2)}, u32[]{:S(2)}) collective-permute-start(f32[512,512]{1,0:T(8,128)S(1)} %bitcast.20), channel_id=1, source_target_pairs={{0,4},{4,0},{1,5},{5,1},{2,6},{6,2},{3,7},{7,3},{8,12},{12,8},{9,1... | collective-permute-start | bytes 3145736 | tf_op jit(solution)/shard_map/ppermute | solution.py:233
  129.0 14.9 %all-to-all-start.4 = ((f32[4,64,640]{2,1,0:T(8,128)}), f32[4,64,640]{2,1,0:T(8,128)S(1)}, u32[]{:S(2)}, u32[]{:S(2)}) async-start(f32[4,64,640]{2,1,0:T(8,128)} %copy-done.9), calls=%async_computation.4 | async-start | bytes 1310720 | tf_op jit(solution)/shard_map/all_to_all | solution.py:241
  132.5 29.8 %collective-permute-start.11 = (bf16[512,512]{1,0:T(8,128)(2,1)}, bf16[512,512]{1,0:T(8,128)(2,1)}, u32[]{:S(2)}, u32[]{:S(2)}) collective-permute-start(bf16[512,512]{1,0:T(8,128)(2,1)} %copy-done.6), channel_id=1, source_target_pairs={{0,4},{4,0},{1,5},{5,1},{2,6},{6,2},{3,7},{7,3},{8,12},{12,8},{9,1... | collective-permute-start | bytes 1572872 | tf_op jit(solution)/shard_map/ppermute | solution.py:235
  132.7 29.6 %collective-permute-start.12 = (bf16[512,512]{1,0:T(8,128)(2,1)}, bf16[512,512]{1,0:T(8,128)(2,1)}, u32[]{:S(2)}, u32[]{:S(2)}) collective-permute-start(bf16[512,512]{1,0:T(8,128)(2,1)} %collective-permute-done.7.w1), channel_id=1, source_target_pairs={{0,4},{4,0},{1,5},{5,1},{2,6},{6,2},{3,7},{7,3},{8,12},{12,8},{9,1... | collective-permute-start | bytes 1572872 | tf_op jit(solution)/shard_map/ppermute | solution.py:235
  133.1 29.3 %collective-permute-start.13 = (bf16[512,512]{1,0:T(8,128)(2,1)}, bf16[512,512]{1,0:T(8,128)(2,1)}, u32[]{:S(2)}, u32[]{:S(2)}) collective-permute-start(bf16[512,512]{1,0:T(8,128)(2,1)} %copy-done.12), channel_id=1, source_target_pairs={{0,4},{4,0},{1,5},{5,1},{2,6},{6,2},{3,7},{7,3},{8,12},{12,8},{9,1... | collective-permute-start | bytes 1572872 | tf_op jit(solution)/shard_map/ppermute | solution.py:235
  133.2 29.1 %collective-permute-start.14 = (bf16[512,512]{1,0:T(8,128)(2,1)}, bf16[512,512]{1,0:T(8,128)(2,1)}, u32[]{:S(2)}, u32[]{:S(2)}) collective-permute-start(bf16[512,512]{1,0:T(8,128)(2,1)} %copy-done.10), channel_id=1, source_target_pairs={{0,4},{4,0},{1,5},{5,1},{2,6},{6,2},{3,7},{7,3},{8,12},{12,8},{9,1... | collective-permute-start | bytes 1572872 | tf_op jit(solution)/shard_map/ppermute | solution.py:235
  133.6 1.0 copy-start.7
  134.7 1.0 copy-start.11
  143.9 1.2 copy-start.5
  158.6 14.1 %all-to-all-start.5 = ((f32[4,64,640]{2,1,0:T(8,128)}), f32[4,64,640]{2,1,0:T(8,128)S(1)}, u32[]{:S(2)}, u32[]{:S(2)}) async-start(f32[4,64,640]{2,1,0:T(8,128)} %copy-done.8), calls=%async_computation.5 | async-start | bytes 1310720 | tf_op jit(solution)/shard_map/all_to_all | solution.py:245
  162.3 10.3 %copy-start.2 = (f32[512,512]{1,0:T(8,128)S(1)}, f32[512,512]{1,0:T(8,128)}, u32[]{:S(2)}) copy-start(f32[512,512]{1,0:T(8,128)} %get-tuple-element.47.rest_ref) | copy-start | bytes 3145732
  172.7 1.2 copy-start.3
  (4 other events, 3.7 us)

commit v4 on v3

v4 whole, which is shorter than its diff:
```python
import jax
import jax.numpy as jnp
from jax import lax
from jax.experimental import pallas as pl
from jax.experimental.pallas import tpu as pltpu
from jax.sharding import Mesh
from jax.sharding import PartitionSpec as P

ITERS = 2
NX, NZ, NC, NY = 4, 8, 2, 4
DP = ("x", "z", "core")
D, KVC, R, TOK = 4096, 512, 64, 512
ROWS = D // NY
HALF = ROWS // NC
WIDE = KVC + 128
HI = lax.Precision.HIGHEST
f32, bf16 = jnp.float32, jnp.bfloat16
SWAP = [(0, 1), (1, 0)]
FLIP = [(i, i ^ 1) for i in range(NY)]
MIRROR = [(i, 3 - i) for i in range(NY)]


def params(room):
    return pltpu.CompilerParams(vmem_limit_bytes=64 * 1024 * 1024 - room)


def sds(shape, dtype=f32):
    return jax.ShapeDtypeStruct(shape, dtype)


def whole(shape):
    return pl.BlockSpec(shape, lambda *_: (0,) * len(shape))


def dot(a, b, dims):
    return lax.dot_general(a, b, (dims, ((), ())), precision=HI, preferred_element_type=f32)


NT = ((1,), (1,))
NN = ((1,), (0,))
TN = ((0,), (0,))


def inverse_lower(block):
    lane = lax.broadcasted_iota(jnp.int32, (8, 128), 1)
    sub = lax.broadcasted_iota(jnp.int32, (8, 128), 0)
    tiles = [
        jnp.where(lane < R, block[8 * i : 8 * i + 8], jnp.where(lane - R == sub + 8 * i, 1.0, 0.0))
        for i in range(8)
    ]

    def spread_row(t, r):
        return jnp.broadcast_to(t[r : r + 1, :], (8, 128))

    for a in range(8):
        cols = {
            i: [jnp.broadcast_to(tiles[i][:, 8 * a + j : 8 * a + j + 1], (8, 128)) for j in range(8)]
            for i in range(a, 8)
        }
        for j in range(8):
            scale = lax.rsqrt(spread_row(cols[a][j], j))
            row = spread_row(tiles[a], j) * scale
            heads = [spread_row(cols[a][m], j) * scale for m in range(j + 1, 8)]
            for i in range(a, 8):
                c = cols[i][j] * scale
                if i == a:
                    tiles[i] = jnp.where(sub == j, row, tiles[i] - jnp.where(sub > j, c, 0.0) * row)
                else:
                    tiles[i] = tiles[i] - c * row
                for n, m in enumerate(range(j + 1, 8)):
                    cols[i][m] = cols[i][m] - c * heads[n]
    return jnp.concatenate(tiles, axis=0)[:, R:]


def products(qt, mean_refs, p_ref, t_hbm, t_ref, sems):
    z, g = [], []
    for n, ref in enumerate(mean_refs):
        m = ref[...]
        p = dot(qt, m, NT)
        p_ref[n] = p
        z.append(dot(p, m, NN))
        g.append(dot(p, jnp.concatenate([p, jnp.zeros_like(p)], axis=0), NT))
    t_ref[:, :KVC] = z[0] + z[1]
    t_ref[:, KVC:] = g[0] + g[1]
    copies = [pltpu.make_async_copy(t_ref, t_hbm.at[s], sems.at[s]) for s in range(NY)]
    for copy in copies:
        copy.start()
    for copy in copies:
        copy.wait()


def total(got_ref, lo, hi):
    return (got_ref[0, :, lo:hi] + got_ref[1, :, lo:hi]) + (got_ref[2, :, lo:hi] + got_ref[3, :, lo:hi])


def first_kernel(q_ref, half_ref, other_ref, t_hbm, p_ref, t_ref, sems):
    products(q_ref[...], (half_ref, other_ref), p_ref, t_hbm, t_ref, sems)


def next_kernel(got_ref, half_hbm, other_hbm, t_hbm, p_ref, half_ref, other_ref, t_ref, sems, in_sems):
    copies = [
        pltpu.make_async_copy(half_hbm, half_ref, in_sems.at[0]),
        pltpu.make_async_copy(other_hbm, other_ref, in_sems.at[1]),
    ]
    for copy in copies:
        copy.start()
    inv = inverse_lower(total(got_ref, KVC, WIDE))
    qt = dot(inv, total(got_ref, 0, KVC), NN)
    for copy in copies:
        copy.wait()
    products(qt, (half_ref, other_ref), p_ref, t_hbm, t_ref, sems)


IN_HBM = pl.BlockSpec(memory_space=pltpu.HBM)
IN_VMEM = pl.BlockSpec(memory_space=pltpu.VMEM)


def first(qt, half, other):
    return pl.pallas_call(
        first_kernel,
        name="first",
        in_specs=[IN_VMEM, IN_VMEM, IN_VMEM],
        out_specs=[IN_HBM, IN_VMEM],
        out_shape=(sds((NY, R, WIDE)), sds((2, R, HALF))),
        scratch_shapes=[pltpu.VMEM((R, WIDE), f32), pltpu.SemaphoreType.DMA((NY,))],
        compiler_params=params(3400 << 10),
    )(qt, half, other)


def following(got, half, other):
    return pl.pallas_call(
        next_kernel,
        name="following",
        in_specs=[IN_VMEM, IN_HBM, IN_HBM],
        out_specs=[IN_HBM, IN_VMEM],
        out_shape=(sds((NY, R, WIDE)), sds((2, R, HALF))),
        scratch_shapes=[
            pltpu.VMEM((HALF, KVC), f32),
            pltpu.VMEM((HALF, KVC), f32),
            pltpu.VMEM((R, WIDE), f32),
            pltpu.SemaphoreType.DMA((NY,)),
            pltpu.SemaphoreType.DMA((2,)),
        ],
        compiler_params=params(1300 << 10),
    )(got, half, other)


def last_kernel(core_ref, got_ref, p_ref, keep_hbm, rest_hbm, approx_ref, err_ref, q_ref, ph, merged, sems):
    i = pl.program_id(0)
    copies = [
        pltpu.make_async_copy(keep_hbm, merged.at[0], sems.at[0]),
        pltpu.make_async_copy(rest_hbm, merged.at[1], sems.at[1]),
    ]

    @pl.when(i == 0)
    def _():
        for copy in copies:
            copy.start()
        inv = inverse_lower(total(got_ref, KVC, WIDE))
        q_ref[...] = dot(inv, total(got_ref, 0, KVC), NN)
        for n in range(2):
            p = dot(inv, p_ref[n], NN)
            ph[2 * n] = p[:, : HALF // 2]
            ph[2 * n + 1] = p[:, HALF // 2 :]
        for copy in copies:
            copy.wait()

    rows = HALF // 2
    approx = dot(ph[i], q_ref[...], TN)
    approx_ref[...] = approx
    err_ref[...] = merged[i // 2, pl.ds(pl.multiple_of((i % 2) * rows, rows), rows), :] - approx


def last(core, got, p, keep, rest):
    rows = HALF // 2
    place = pl.BlockSpec((rows, KVC), lambda i, c: ((i + 2 * c[0]) % 4, 0))
    return pl.pallas_call(
        last_kernel,
        name="last",
        grid_spec=pltpu.PrefetchScalarGridSpec(
            num_scalar_prefetch=1,
            grid=(4,),
            in_specs=[whole((NY, R, WIDE)), whole((2, R, HALF)), IN_HBM, IN_HBM],
            out_specs=[place, place, whole((R, KVC))],
            scratch_shapes=[
                pltpu.VMEM((4, R, rows), f32),
                pltpu.VMEM((2, HALF, KVC), f32),
                pltpu.SemaphoreType.DMA((2,)),
            ],
        ),
        out_shape=(sds((ROWS, KVC)), sds((ROWS, KVC)), sds((R, KVC))),
        compiler_params=params(1300 << 10),
    )(core, got, p, keep, rest)


def input_grad_kernel(at_ref, cot_ref, w0, w1, w2, w3, *refs):
    out_ref = refs[-1]
    for g, w in enumerate((w0, w1, w2, w3)):

        @pl.when(pl.program_id(0) == g)
        def _(w=w):
            out_ref[...] = lax.dot_general(
                cot_ref[...], w[...], (NT, ((), ())), preferred_element_type=f32
            ).astype(bf16)


def input_grad_of(at, cot, pieces, before=None):
    piece = whole((HALF, KVC))
    extra = [] if before is None else [before]
    return pl.pallas_call(
        input_grad_kernel,
        name="input_grad",
        grid_spec=pltpu.PrefetchScalarGridSpec(
            num_scalar_prefetch=1,
            grid=(NY,),
            in_specs=[whole((TOK, KVC))] + [piece] * NY + [pl.BlockSpec(memory_space=pl.ANY) for _ in extra],
            out_specs=pl.BlockSpec((TOK, HALF), lambda i, a: (0, a[i])),
        ),
        out_shape=sds((TOK, D), bf16),
        input_output_aliases={} if before is None else {2 + NY: 0},
        compiler_params=params(4 << 20),
        cost_estimate=pl.CostEstimate(flops=TOK * D * KVC, bytes_accessed=5 << 20, transcendentals=0),
    )(at, cot, *pieces, *extra)


def scatter_y(acts, cot, error, scale, y):
    def term(rows):
        return jnp.einsum("tr,tk->rk", rows, cot, preferred_element_type=f32).astype(bf16)

    near = (y ^ 1, y ^ 3)
    pairs = (FLIP, MIRROR)
    across = term(lax.dynamic_slice(acts, (0, (y ^ 2) * ROWS), (TOK, ROWS)))
    across, acts = lax.optimization_barrier((across, acts))
    firsts = [lax.ppermute(across[n * HALF : (n + 1) * HALF], "y", pairs[n]) for n in range(2)]
    terms = lax.optimization_barrier(term(acts)).reshape(NY, 2, HALF, KVC)

    def take(block, n):
        return lax.dynamic_slice(terms, (block, n, 0, 0), (1, 1, HALF, KVC)).reshape(HALF, KVC)

    seconds = [lax.ppermute(take(near[n], n), "y", pairs[n]) for n in range(2)]
    onward = [
        lax.ppermute((firsts[n].astype(f32) + take(near[1 - n], n).astype(f32)).astype(bf16), "y", pairs[1 - n])
        for n in range(2)
    ]
    owns = [error[n * HALF : (n + 1) * HALF] + scale * take(y, n).astype(f32) for n in range(2)]
    bases = [lax.optimization_barrier(owns[n] + scale * seconds[n].astype(f32)) for n in range(2)]
    return [bases[n] + scale * onward[n].astype(f32) for n in range(2)]


def everyone(t, axis, n):
    return lax.all_to_all(jnp.broadcast_to(t, (n, *t.shape)), axis, 0, 0, tiled=True)


def body(acts, cotangent, weight, error_buf, q_init, inv_scale):
    y, core = lax.axis_index("y"), lax.axis_index("core")
    low, high = scatter_y(acts, cotangent, error_buf[0], inv_scale, y)
    keep = jnp.where(core == 0, low, high)
    rest = jnp.where(core == 0, high, low)

    give, weight = lax.optimization_barrier((rest.astype(bf16), weight))
    pair = (keep + lax.ppermute(give, "core", SWAP).astype(f32)) * (1.0 / (NX * NZ * NC))
    along_x = lax.all_to_all(pair.astype(bf16).reshape(NX, 128, KVC), "x", 0, 0, tiled=True)
    mine = lax.dynamic_slice_in_dim(weight, core * HALF, HALF, 0)
    pieces = [mine] + [
        lax.ppermute(mine, "y", [(i, (i + s) % NY) for i in range(NY)]) for s in range(1, NY)
    ]
    along_x, pieces[1], pieces[3] = lax.optimization_barrier((along_x, pieces[1], pieces[3]))
    row = jnp.sum(along_x.astype(f32), axis=0).astype(bf16)
    along_z = lax.all_to_all(row.reshape(NZ, 16, KVC), "z", 0, 0, tiled=True)
    along_z, pieces[2] = lax.optimization_barrier((along_z, pieces[2]))
    rows = jnp.sum(along_z.astype(f32), axis=0)
    block = everyone(rows, "z", NZ).reshape(128, KVC)
    half = everyone(block, "x", NX).reshape(HALF, KVC)
    other = lax.ppermute(half, "core", SWAP)
    others = [lax.ppermute(piece, "core", SWAP) for piece in pieces]
    source = (y - jnp.arange(NY)) % NY

    t, p = first(q_init.T, half, other)
    input_grad = input_grad_of(2 * source + core, cotangent, pieces)
    for _ in range(ITERS - 1):
        got = lax.all_to_all(t, "y", 0, 0, tiled=True)
        got, input_grad = lax.optimization_barrier((got, input_grad))
        t, p = following(got, half, other)
    input_grad = input_grad_of(2 * source + 1 - core, cotangent, others, input_grad)
    approx, new_error, qt = last(core[None], lax.all_to_all(t, "y", 0, 0, tiled=True), p, keep, rest)
    return (input_grad, approx, new_error[None], qt.T)


def solution(mesh):
    fine = Mesh(mesh.devices.reshape(NX, NZ, NC, NY), ("x", "z", "core", "y"))
    every = P((*DP, "y"), None)
    in_specs = (every, every, P("y", None), P(DP, "y", None), P(), P())
    out_specs = (every, P("y", None), P(DP, "y", None), P())
    return jax.shard_map(body, mesh=fine, in_specs=in_specs, out_specs=out_specs, check_vma=False)
```

time: 189 us -> 188 us (level)
  waiting for transfers between devices: 49.1 us -> 64.5 us
  matrix products: 18.6 us -> 8.8 us
  local copies, waits for them, and re-layouts: 9.18 us -> 3.3 us
  Pallas kernels: 39.3 us -> 34.6 us
  other arithmetic: 8.63 us -> 11.9 us
  starting transfers between devices: 30.3 us -> 33.5 us
  blocking collectives: 30.8 us -> 28.3 us
    all_to_all x1 -> x0, blocking collectives: 13.1 us -> none  [body(): lax.all_to_all(pair.astype(bf16).reshape(NX, 128, KVC), 'x', 0, 0, tiled=...]
    all_to_all x1 -> x2, blocking collectives: 17.7 us -> 28.3 us  [everyone(): lax.all_to_all(jnp.broadcast_to(t, (n, *t.shape)), axis, 0, 0, tiled=True)]
    dot_general x8 -> x2, matrix products: 18.6 us -> 8.8 us  [term(): jnp.einsum('tr,tk->rk', rows, cot, preferred_element_type=f32).astype(bf16)]
    unnamed x34 -> x10, local copies, waits for them, and re-layouts: 8.29 us -> 0.99 us
    ppermute x3, waiting for transfers between devices: 11.3 us -> 17.2 us  [body(): lax.ppermute(mine, 'y', [(i, (i + s) % NY) for i in range(NY)])]
    ppermute x7, waiting for transfers between devices: 20.9 us -> 26.6 us  [the longest x2 12.6 us: scatter_y(): lax.ppermute((firsts[n].astype(f32) + take(near[1 - n], n).astype(f32)).a...]
    pallas_call x1, Pallas kernels: 13.5 us -> 8.26 us  [last(): pl.pallas_call(last_kernel, name='last', grid_spec=pltpu.PrefetchScalarGr...]
    all_to_all x1, waiting for transfers between devices: 6.57 us -> 9.06 us  [body(): along_z = lax.all_to_all(row.reshape(NZ, 16, KVC), 'z', 0, 0, tiled=True)]
  transfers between devices with their start and end apart: 19 -> 19, of which waited for: 10 -> 12; matrix products, arithmetic and copies ran while one was open for 12% -> 7% of each run, Pallas kernels for 12% -> 11%
where the time goes in v4:
time: 188 us; the launch traced here: 186 us
  waiting for transfers between devices  64.5 us (34%)
  Pallas kernels  34.6 us (18%)
  starting transfers between devices  33.5 us (18%)
  blocking collectives  28.3 us (15%)
  other arithmetic  11.9 us (6%)
  matrix products  8.8 us (5%)
  local copies, waits for them, and re-layouts  3.3 us (2%)
    all_to_all x2, blocking collectives, everyone(): lax.all_to_all(jnp.broadcast_to(t, (n, *t.shape)), axis, 0, 0, tiled=True)  28.3 us
    ppermute x3, waiting for transfers between devices, body(): lax.ppermute(mine, 'y', [(i, (i + s) % NY) for i in range(NY)])  17.2 us
    ppermute x2, waiting for transfers between devices, scatter_y(): lax.ppermute((firsts[n].astype(f32) + take(near[1 - n], n).astype(f32)).a...  12.6 us
    pallas_call x2, Pallas kernels, input_grad_of(): pl.pallas_call(input_grad_kernel, name='input_grad', grid_spec=pltpu.Pref...  10.8 us
    ppermute x2, waiting for transfers between devices, scatter_y(): seconds = [lax.ppermute(take(near[n], n), 'y', pairs[n]) for n in range(2)]  9.82 us
    all_to_all x1, waiting for transfers between devices, body(): along_z = lax.all_to_all(row.reshape(NZ, 16, KVC), 'z', 0, 0, tiled=True)  9.06 us
    pallas_call x1, Pallas kernels, following(): pl.pallas_call(next_kernel, name='following', in_specs=[IN_VMEM, IN_HBM,...  8.94 us
    dot_general x2, matrix products, term(): jnp.einsum('tr,tk->rk', rows, cot, preferred_element_type=f32).astype(bf16)  8.8 us
  transfers between devices with their start and end apart: 19, of which 12 were waited for; matrix products, arithmetic and copies ran while one was open for 7% of the time, Pallas kernels for 11%

profile of v4, /device:TPU:2, one launch (start us, length us, event | category | flops | bytes accessed | tf_op | source)
XLA Modules:
  0.0 186.5 jit_solution(4936582124680735614)
XLA Ops:
  0.7 2.2 %convolution_convert_fusion.1 = bf16[1024,512]{1,0:T(8,128)(2,1)S(1)} fusion(bf16[512,512]{1,0:T(8,128)(2,1)} %cot_ref.3, bf16[512,4096]{1,0:T(8,128)(2,1)} %param.6, s32[]{:T(128)S(6)} %select_n.39), kind=kOutput, calls=%fused_computation.1 | convolution fusion | flops 537395200 | bytes 2621444 | tf_op jit(solution)/shard_map/tr,tk->rk/dot_general | solution.py:228
  3.0 3.1 %collective-permute-start.1 = (bf16[512,512]{1,0:T(8,128)(2,1)S(1)}, bf16[512,512]{1,0:T(8,128)(2,1)}, u32[]{:S(2)}, u32[]{:S(2)}) collective-permute-start(bf16[512,512]{1,0:T(8,128)(2,1)S(1)} %get-tuple-element.50), channel_id=1, source_target_pairs={{0,3},{1,2},{2,1},{3,0},{4,7},{5,6},{6,5},{7,4},{8,11},{9,10},{10,... | collective-permute-start | bytes 1572872 | tf_op jit(solution)/shard_map/ppermute | solution.py:234
  6.2 6.6 %convolution_convert_fusion = bf16[4096,512]{1,0:T(8,128)(2,1)} fusion(bf16[512,4096]{1,0:T(8,128)(2,1)} %param.6, bf16[512,512]{1,0:T(8,128)(2,1)S(1)} %copy-done.3), kind=kOutput, calls=%fused_computation | convolution fusion | flops 2149580800 | bytes 8912896 | tf_op jit(solution)/shard_map/tr,tk->rk/dot_general | solution.py:228
  16.8 1.9 %collective-permute-done.1 = bf16[512,512]{1,0:T(8,128)(2,1)} collective-permute-done((bf16[512,512]{1,0:T(8,128)(2,1)S(1)}, bf16[512,512]{1,0:T(8,128)(2,1)}, u32[]{:S(2)}, u32[]{:S(2)}) %collective-permute-start.1) | collective-permute-done | bytes 524320 | tf_op jit(solution)/shard_map/ppermute | solution.py:234
  18.7 2.3 %collective-permute-done.4 = bf16[512,512]{1,0:T(8,128)(2,1)} collective-permute-done((bf16[512,512]{1,0:T(8,128)(2,1)S(1)}, bf16[512,512]{1,0:T(8,128)(2,1)}, u32[]{:S(2)}, u32[]{:S(2)}) %collective-permute-start.4) | collective-permute-done | bytes 524320 | tf_op jit(solution)/shard_map/ppermute | solution.py:234
  21.0 8.4 %collective-permute-done = bf16[512,512]{1,0:T(8,128)(2,1)} collective-permute-done((bf16[512,512]{1,0:T(8,128)(2,1)S(1)}, bf16[512,512]{1,0:T(8,128)(2,1)}, u32[]{:S(2)}, u32[]{:S(2)}) %collective-permute-start) | collective-permute-done | bytes 524320 | tf_op jit(solution)/shard_map/ppermute | solution.py:240
  29.3 1.5 collective-permute-done.3
  30.8 4.5 %fusion.1 = (bf16[512,512]{1,0:T(8,128)(2,1)}, bf16[512,512]{1,0:T(8,128)(2,1)}, f32[512,512]{1,0:T(8,128)S(1)}, f32[512,512]{1,0:T(8,128)S(1)}) fusion(bf16[512,512]{1,0:T(8,128)(2,1)} %collective-permute-done.1, bf16[4,2,512,512]{3,2,1,0:T(8,128)(2,1)} %bitcast.38, s32[]{:T(128)S(6)} %select_n.42, s32[]{:T(128)S(6)} %select_n.41, ...), kind=kLoop, calls=%fused_computation.5 | loop fusion | flops 5242880 | bytes 9439744 | tf_op jit(solution)/shard_map/convert_element_type | solution.py:242
  35.6 1.3 collective-permute-start.5
  36.9 11.3 %collective-permute-done.2 = bf16[512,512]{1,0:T(8,128)(2,1)} collective-permute-done((bf16[512,512]{1,0:T(8,128)(2,1)}, bf16[512,512]{1,0:T(8,128)(2,1)}, u32[]{:S(2)}, u32[]{:S(2)}) %collective-permute-start.2) | collective-permute-done | bytes 524320 | tf_op jit(solution)/shard_map/ppermute | solution.py:242
  48.2 1.4 collective-permute-done.5
  49.5 2.7 %fusion.11 = (bf16[512,512]{1,0:T(8,128)(2,1)}, f32[512,512]{1,0:T(8,128)}) fusion(f32[512,512]{1,0:T(8,128)S(1)} %get-tuple-element.46, bf16[512,512]{1,0:T(8,128)(2,1)} %collective-permute-done.5, f32[512,512]{1,0:T(8,128)S(1)} %get-tuple-element.47, bf16[512,512]{1,0:T(8,128)(2,1)} %collective-permute-done.2, f32[]{:T(128)S(6)} %copy.12, pred[]{:T(512)S(6)} %eq.6), kind=kLoop, calls=%fused_computation.28 | loop fusion | flops 2097152 | bytes 4718597 | tf_op jit(solution)/shard_map/convert_element_type | solution.py:260
  53.0 1.7 collective-permute-start.9
  55.1 2.9 %multiply_convert_fusion = (bf16[512,512]{1,0:T(8,128)(2,1)}, f32[512,512]{1,0:T(8,128)}) fusion(bf16[512,512]{1,0:T(8,128)(2,1)} %collective-permute-done.7, f32[512,512]{1,0:T(8,128)S(1)} %get-tuple-element.47, bf16[512,512]{1,0:T(8,128)(2,1)} %collective-permute-done.2, f32[512,512]{1,0:T(8,128)S(1)} %get-tuple-element.46, ...), kind=kLoop, calls=%fused_computation.10 | loop fusion | flops 2883584 | bytes 5242885 | tf_op jit(solution)/shard_map/convert_element_type | solution.py:262
  58.0 4.8 %all-to-all-start = ((bf16[4,128,512]{2,1,0:T(8,128)(2,1)}), bf16[4,128,512]{2,1,0:T(8,128)(2,1)S(1)}, u32[]{:S(2)}, u32[]{:S(2)}) async-start(bf16[4,128,512]{2,1,0:T(8,128)(2,1)} %bitcast.39), calls=%async_computation | async-start | bytes 1048576 | tf_op jit(solution)/shard_map/all_to_all | solution.py:262
  62.8 1.6 collective-permute-start.11
  64.4 3.8 %collective-permute-done.9.w3 = bf16[512,512]{1,0:T(8,128)(2,1)} collective-permute-done((bf16[512,512]{1,0:T(8,128)(2,1)}, bf16[512,512]{1,0:T(8,128)(2,1)}, u32[]{:S(2)}, u32[]{:S(2)}) %collective-permute-start.9) | collective-permute-done | bytes 524320 | tf_op jit(solution)/shard_map/ppermute | solution.py:265
  68.1 13.4 %collective-permute-done.8.w1 = bf16[512,512]{1,0:T(8,128)(2,1)} collective-permute-done((bf16[512,512]{1,0:T(8,128)(2,1)}, bf16[512,512]{1,0:T(8,128)(2,1)}, u32[]{:S(2)}, u32[]{:S(2)}) %collective-permute-start.8) | collective-permute-done | bytes 524320 | tf_op jit(solution)/shard_map/ppermute | solution.py:265
  82.3 8.5 %all-to-all-start.1 = ((bf16[8,16,512]{2,1,0:T(8,128)(2,1)}), bf16[8,16,512]{2,1,0:T(8,128)(2,1)S(1)}, u32[]{:S(2)}, u32[]{:S(2)}) async-start(bf16[8,16,512]{2,1,0:T(8,128)(2,1)} %bitcast.10), calls=%async_computation.1 | async-start | bytes 262144 | tf_op jit(solution)/shard_map/all_to_all | solution.py:269
  90.8 9.1 %all-to-all-done.1 = bf16[8,16,512]{2,1,0:T(8,128)(2,1)S(1)} async-done(((bf16[8,16,512]{2,1,0:T(8,128)(2,1)}), bf16[8,16,512]{2,1,0:T(8,128)(2,1)S(1)}, u32[]{:S(2)}, u32[]{:S(2)}) %all-to-all-start.1) | async-done | bytes 131104 | tf_op jit(solution)/shard_map/all_to_all | solution.py:269
  99.9 12.9 %all_to_all.30 = f32[8,16,512]{2,1,0:T(8,128)S(1)} all-to-all(f32[8,16,512]{2,1,0:T(8,128)S(1)} %broadcast_in_dim.12), channel_id=1, replica_groups=mesh['x'=4,'z'=8,'core'=2,'y'=4] {'z'}, dimensions={0} | all-to-all | bytes 524288 | tf_op jit(solution)/shard_map/all_to_all | solution.py:251
  112.9 15.4 %all_to_all.31 = f32[4,128,512]{2,1,0:T(8,128)S(1)} all-to-all(f32[4,128,512]{2,1,0:T(8,128)S(1)} %broadcast_in_dim.13), channel_id=1, replica_groups=mesh['x'=4,'z'=8,'core'=2,'y'=4] {'x'}, dimensions={0} | all-to-all | bytes 2097152 | tf_op jit(solution)/shard_map/all_to_all | solution.py:251
  128.4 2.7 %collective-permute-done.14.other_ref.other_hbm = f32[512,512]{1,0:T(8,128)S(1)} collective-permute-done((f32[512,512]{1,0:T(8,128)S(1)}, f32[512,512]{1,0:T(8,128)S(1)}, u32[]{:S(2)}, u32[]{:S(2)}) %collective-permute-start.14) | collective-permute-done | bytes 1048608 | tf_op jit(solution)/shard_map/ppermute | solution.py:274
  132.0 6.5 %first.1 = (f32[4,64,640]{2,1,0:T(8,128)}, f32[2,64,512]{2,1,0:T(8,128)}) custom-call(f32[64,512]{1,0:T(8,128)} %bitcast.41, f32[512,512]{1,0:T(8,128)} %bitcast.35, f32[512,512]{1,0:T(8,128)} %copy-done.2), custom_call_target="tpu_custom_call" | custom-call | tf_op jit(solution)/shard_map/first/pallas_call | solution.py:119
  138.5 4.2 %all-to-all-start.4 = ((f32[4,64,640]{2,1,0:T(8,128)}), f32[4,64,640]{2,1,0:T(8,128)}, u32[]{:S(2)}, u32[]{:S(2)}) async-start(f32[4,64,640]{2,1,0:T(8,128)} %get-tuple-element.30), calls=%async_computation.4 | async-start | bytes 1310720 | tf_op jit(solution)/shard_map/all_to_all | solution.py:281
  144.3 5.4 %input_grad.2.refs_0_ = bf16[512,4096]{1,0:T(8,128)(2,1)} custom-call(s32[4]{0:T(128)} %broadcast_add_fusion.at_ref, bf16[512,512]{1,0:T(8,128)(2,1)} %cot_ref.3, bf16[512,512]{1,0:T(8,128)(2,1)} %constant_dynamic-slice_fusion.w0, bf16[512,512]{1,0:T(8,128)(2,1)} %collective-permute-done.8.w1, bf16[512,512]{1,0:T(8,128)(2,1)} %copy-done.4, ...), custom_call_target="tpu_custom_call" | custom-call | flops 1073741824 | bytes 5242880 | tf_op jit(solution)/shard_map/input_grad/pallas_call | solution.py:210
  149.8 4.5 %all-to-all-done.4.got_ref = f32[4,64,640]{2,1,0:T(8,128)} async-done(((f32[4,64,640]{2,1,0:T(8,128)}), f32[4,64,640]{2,1,0:T(8,128)}, u32[]{:S(2)}, u32[]{:S(2)}) %all-to-all-start.4) | async-done | bytes 655392 | tf_op jit(solution)/shard_map/all_to_all | solution.py:281
  154.2 8.9 %following.1 = (f32[4,64,640]{2,1,0:T(8,128)}, f32[2,64,512]{2,1,0:T(8,128)}) custom-call(f32[4,64,640]{2,1,0:T(8,128)} %all-to-all-done.4.got_ref, f32[512,512]{1,0:T(8,128)} %bitcast.36, f32[512,512]{1,0:T(8,128)} %copy-done.2), custom_call_target="tpu_custom_call" | custom-call | tf_op jit(solution)/shard_map/following/pallas_call | solution.py:131
  163.2 4.4 %all-to-all-start.5 = ((f32[4,64,640]{2,1,0:T(8,128)}), f32[4,64,640]{2,1,0:T(8,128)}, u32[]{:S(2)}, u32[]{:S(2)}) async-start(f32[4,64,640]{2,1,0:T(8,128)} %get-tuple-element.33), calls=%async_computation.5 | async-start | bytes 1310720 | tf_op jit(solution)/shard_map/all_to_all | solution.py:285
  168.1 5.4 %input_grad.3 = bf16[512,4096]{1,0:T(8,128)(2,1)} custom-call(s32[4]{0:T(128)} %add_subtract_fusion.at_ref, bf16[512,512]{1,0:T(8,128)(2,1)} %cot_ref.3, bf16[512,512]{1,0:T(8,128)(2,1)} %collective-permute-done.6.w0, bf16[512,512]{1,0:T(8,128)(2,1)} %collective-permute-done.10.w1, ...), custom_call_target="tpu_custom_call", output_to_operand_aliasing={{}: (6, {})} | custom-call | flops 1073741824 | bytes 5242880 | tf_op jit(solution)/shard_map/input_grad/pallas_call | solution.py:210
  173.6 4.5 %all-to-all-done.5.got_ref = f32[4,64,640]{2,1,0:T(8,128)} async-done(((f32[4,64,640]{2,1,0:T(8,128)}), f32[4,64,640]{2,1,0:T(8,128)}, u32[]{:S(2)}, u32[]{:S(2)}) %all-to-all-start.5) | async-done | bytes 655392 | tf_op jit(solution)/shard_map/all_to_all | solution.py:285
  178.0 8.3 %last.1 = (f32[1024,512]{1,0:T(8,128)}, f32[1024,512]{1,0:T(8,128)}, f32[64,512]{1,0:T(8,128)}) custom-call(s32[1]{0:T(128)} %bitcast.14.core_ref, f32[4,64,640]{2,1,0:T(8,128)} %all-to-all-done.5.got_ref, f32[2,64,512]{2,1,0:T(8,128)} %get-tuple-element.34.p_ref, f32[512,512]{1,0:T(8,128)} %get-tuple-element.39.keep_hbm, f32[512,512]{1,0:T(8,128)} %get-tuple-element.41.rest_hbm), custom_call_target="tpu_custom_call" | custom-call | tf_op jit(solution)/shard_map/last/pallas_call | solution.py:177
  (37 shorter events, 9.1 us)
Async XLA Ops:
  0.6 51.6 %copy-start = (bf16[1024,512]{1,0:T(8,128)(2,1)S(1)}, bf16[1024,512]{1,0:T(8,128)(2,1)}, u32[]{:S(2)}) copy-start(bf16[1024,512]{1,0:T(8,128)(2,1)} %param.8) | copy-start | bytes 3145732
  0.6 5.6 %copy-start.3 = (bf16[512,512]{1,0:T(8,128)(2,1)S(1)}, bf16[512,512]{1,0:T(8,128)(2,1)}, u32[]{:S(2)}) copy-start(bf16[512,512]{1,0:T(8,128)(2,1)} %cot_ref.3) | copy-start | bytes 1572868
  3.0 15.7 %collective-permute-start.1 = (bf16[512,512]{1,0:T(8,128)(2,1)S(1)}, bf16[512,512]{1,0:T(8,128)(2,1)}, u32[]{:S(2)}, u32[]{:S(2)}) collective-permute-start(bf16[512,512]{1,0:T(8,128)(2,1)S(1)} %get-tuple-element.50), channel_id=1, source_target_pairs={{0,3},{1,2},{2,1},{3,0},{4,7},{5,6},{6,5},{7,4},{8,11},{9,10},{10,... | collective-permute-start | bytes 1572872 | tf_op jit(solution)/shard_map/ppermute | solution.py:234
  6.1 14.9 %collective-permute-start.4 = (bf16[512,512]{1,0:T(8,128)(2,1)S(1)}, bf16[512,512]{1,0:T(8,128)(2,1)}, u32[]{:S(2)}, u32[]{:S(2)}) collective-permute-start(bf16[512,512]{1,0:T(8,128)(2,1)S(1)} %get-tuple-element.51), channel_id=1, source_target_pairs={{0,1},{1,0},{2,3},{3,2},{4,5},{5,4},{6,7},{7,6},{8,9},{9,8},{10,11... | collective-permute-start | bytes 1572872 | tf_op jit(solution)/shard_map/ppermute | solution.py:234
  14.1 15.3 %collective-permute-start = (bf16[512,512]{1,0:T(8,128)(2,1)S(1)}, bf16[512,512]{1,0:T(8,128)(2,1)}, u32[]{:S(2)}, u32[]{:S(2)}) collective-permute-start(bf16[512,512]{1,0:T(8,128)(2,1)S(1)} %get-tuple-element.48), channel_id=1, source_target_pairs={{0,3},{1,2},{2,1},{3,0},{4,7},{5,6},{6,5},{7,4},{8,11},{9,10},{10,... | collective-permute-start | bytes 1572872 | tf_op jit(solution)/shard_map/ppermute | solution.py:240
  15.2 15.6 %collective-permute-start.3 = (bf16[512,512]{1,0:T(8,128)(2,1)S(1)}, bf16[512,512]{1,0:T(8,128)(2,1)}, u32[]{:S(2)}, u32[]{:S(2)}) collective-permute-start(bf16[512,512]{1,0:T(8,128)(2,1)S(1)} %get-tuple-element.49), channel_id=1, source_target_pairs={{0,1},{1,0},{2,3},{3,2},{4,5},{5,4},{6,7},{7,6},{8,9},{9,8},{10,11... | collective-permute-start | bytes 1572872 | tf_op jit(solution)/shard_map/ppermute | solution.py:240
  35.3 12.8 %collective-permute-start.2 = (bf16[512,512]{1,0:T(8,128)(2,1)}, bf16[512,512]{1,0:T(8,128)(2,1)}, u32[]{:S(2)}, u32[]{:S(2)}) collective-permute-start(bf16[512,512]{1,0:T(8,128)(2,1)} %get-tuple-element.44), channel_id=1, source_target_pairs={{0,1},{1,0},{2,3},{3,2},{4,5},{5,4},{6,7},{7,6},{8,9},{9,8},{10,11... | collective-permute-start | bytes 1572872 | tf_op jit(solution)/shard_map/ppermute | solution.py:242
  35.6 13.9 %collective-permute-start.5 = (bf16[512,512]{1,0:T(8,128)(2,1)}, bf16[512,512]{1,0:T(8,128)(2,1)}, u32[]{:S(2)}, u32[]{:S(2)}) collective-permute-start(bf16[512,512]{1,0:T(8,128)(2,1)} %get-tuple-element.45), channel_id=1, source_target_pairs={{0,3},{1,2},{2,1},{3,0},{4,7},{5,6},{6,5},{7,4},{8,11},{9,10},{10,... | collective-permute-start | bytes 1572872 | tf_op jit(solution)/shard_map/ppermute | solution.py:242
  52.2 2.9 %collective-permute-start.7 = (bf16[512,512]{1,0:T(8,128)(2,1)}, bf16[512,512]{1,0:T(8,128)(2,1)}, u32[]{:S(2)}, u32[]{:S(2)}) collective-permute-start(bf16[512,512]{1,0:T(8,128)(2,1)} %get-tuple-element.24), channel_id=1, source_target_pairs={{0,4},{4,0},{1,5},{5,1},{2,6},{6,2},{3,7},{7,3},{8,12},{12,8},{9,1... | collective-permute-start | bytes 1572872 | tf_op jit(solution)/shard_map/ppermute | solution.py:261
  53.0 15.1 %collective-permute-start.9 = (bf16[512,512]{1,0:T(8,128)(2,1)}, bf16[512,512]{1,0:T(8,128)(2,1)}, u32[]{:S(2)}, u32[]{:S(2)}) collective-permute-start(bf16[512,512]{1,0:T(8,128)(2,1)} %constant_dynamic-slice_fusion.w0), channel_id=1, source_target_pairs={{0,3},{1,0},{2,1},{3,2},{4,7},{5,4},{6,5},{7,6},{8,11},{9,8},{10,9... | collective-permute-start | bytes 1572872 | tf_op jit(solution)/shard_map/ppermute | solution.py:265
  54.7 26.8 %collective-permute-start.8 = (bf16[512,512]{1,0:T(8,128)(2,1)}, bf16[512,512]{1,0:T(8,128)(2,1)}, u32[]{:S(2)}, u32[]{:S(2)}) collective-permute-start(bf16[512,512]{1,0:T(8,128)(2,1)} %constant_dynamic-slice_fusion.w0), channel_id=1, source_target_pairs={{0,1},{1,2},{2,3},{3,0},{4,5},{5,6},{6,7},{7,4},{8,9},{9,10},{10,1... | collective-permute-start | bytes 1572872 | tf_op jit(solution)/shard_map/ppermute | solution.py:265
  58.0 23.6 %all-to-all-start = ((bf16[4,128,512]{2,1,0:T(8,128)(2,1)}), bf16[4,128,512]{2,1,0:T(8,128)(2,1)S(1)}, u32[]{:S(2)}, u32[]{:S(2)}) async-start(bf16[4,128,512]{2,1,0:T(8,128)(2,1)} %bitcast.39), calls=%async_computation | async-start | bytes 1048576 | tf_op jit(solution)/shard_map/all_to_all | solution.py:262
  62.8 28.0 %collective-permute-start.11 = (bf16[512,512]{1,0:T(8,128)(2,1)}, bf16[512,512]{1,0:T(8,128)(2,1)S(1)}, u32[]{:S(2)}, u32[]{:S(2)}) collective-permute-start(bf16[512,512]{1,0:T(8,128)(2,1)} %constant_dynamic-slice_fusion.w0), channel_id=1, source_target_pairs={{0,2},{1,3},{2,0},{3,1},{4,6},{5,7},{6,4},{7,5},{8,10},{9,11},{10,... | collective-permute-start | bytes 1572872 | tf_op jit(solution)/shard_map/ppermute | solution.py:265
  82.3 17.5 %all-to-all-start.1 = ((bf16[8,16,512]{2,1,0:T(8,128)(2,1)}), bf16[8,16,512]{2,1,0:T(8,128)(2,1)S(1)}, u32[]{:S(2)}, u32[]{:S(2)}) async-start(bf16[8,16,512]{2,1,0:T(8,128)(2,1)} %bitcast.10), calls=%async_computation.1 | async-start | bytes 262144 | tf_op jit(solution)/shard_map/all_to_all | solution.py:269
  90.8 22.0 %copy-start.4 = (bf16[512,512]{1,0:T(8,128)(2,1)}, bf16[512,512]{1,0:T(8,128)(2,1)S(1)}, u32[]{:S(2)}) copy-start(bf16[512,512]{1,0:T(8,128)(2,1)S(1)} %collective-permute-done.11.w2) | copy-start | bytes 1572868
  128.4 2.7 %copy-start.1 = (f32[4,128,512]{2,1,0:T(8,128)}, f32[4,128,512]{2,1,0:T(8,128)S(1)}, u32[]{:S(2)}) copy-start(f32[4,128,512]{2,1,0:T(8,128)S(1)} %all_to_all.31) | copy-start | bytes 3145732
  128.4 2.7 %collective-permute-start.14 = (f32[512,512]{1,0:T(8,128)S(1)}, f32[512,512]{1,0:T(8,128)S(1)}, u32[]{:S(2)}, u32[]{:S(2)}) collective-permute-start(f32[512,512]{1,0:T(8,128)S(1)} %bitcast.34), channel_id=1, source_target_pairs={{0,4},{4,0},{1,5},{5,1},{2,6},{6,2},{3,7},{7,3},{8,12},{12,8},{9,1... | collective-permute-start | bytes 3145736 | tf_op jit(solution)/shard_map/ppermute | solution.py:274
  131.0 1.0 copy-start.2
  138.5 15.7 %all-to-all-start.4 = ((f32[4,64,640]{2,1,0:T(8,128)}), f32[4,64,640]{2,1,0:T(8,128)}, u32[]{:S(2)}, u32[]{:S(2)}) async-start(f32[4,64,640]{2,1,0:T(8,128)} %get-tuple-element.30), calls=%async_computation.4 | async-start | bytes 1310720 | tf_op jit(solution)/shard_map/all_to_all | solution.py:281
  142.7 25.4 %collective-permute-start.6 = (bf16[512,512]{1,0:T(8,128)(2,1)}, bf16[512,512]{1,0:T(8,128)(2,1)}, u32[]{:S(2)}, u32[]{:S(2)}) collective-permute-start(bf16[512,512]{1,0:T(8,128)(2,1)} %constant_dynamic-slice_fusion.w0), channel_id=1, source_target_pairs={{0,4},{4,0},{1,5},{5,1},{2,6},{6,2},{3,7},{7,3},{8,12},{12,8},{9,1... | collective-permute-start | bytes 1572872 | tf_op jit(solution)/shard_map/ppermute | solution.py:275
  142.9 25.2 %collective-permute-start.10 = (bf16[512,512]{1,0:T(8,128)(2,1)}, bf16[512,512]{1,0:T(8,128)(2,1)}, u32[]{:S(2)}, u32[]{:S(2)}) collective-permute-start(bf16[512,512]{1,0:T(8,128)(2,1)} %collective-permute-done.8.w1), channel_id=1, source_target_pairs={{0,4},{4,0},{1,5},{5,1},{2,6},{6,2},{3,7},{7,3},{8,12},{12,8},{9,1... | collective-permute-start | bytes 1572872 | tf_op jit(solution)/shard_map/ppermute | solution.py:275
  143.3 24.8 %collective-permute-start.13 = (bf16[512,512]{1,0:T(8,128)(2,1)}, bf16[512,512]{1,0:T(8,128)(2,1)}, u32[]{:S(2)}, u32[]{:S(2)}) collective-permute-start(bf16[512,512]{1,0:T(8,128)(2,1)} %collective-permute-done.9.w3), channel_id=1, source_target_pairs={{0,4},{4,0},{1,5},{5,1},{2,6},{6,2},{3,7},{7,3},{8,12},{12,8},{9,1... | collective-permute-start | bytes 1572872 | tf_op jit(solution)/shard_map/ppermute | solution.py:275
  143.4 24.7 %collective-permute-start.12 = (bf16[512,512]{1,0:T(8,128)(2,1)}, bf16[512,512]{1,0:T(8,128)(2,1)}, u32[]{:S(2)}, u32[]{:S(2)}) collective-permute-start(bf16[512,512]{1,0:T(8,128)(2,1)} %copy-done.4), channel_id=1, source_target_pairs={{0,4},{4,0},{1,5},{5,1},{2,6},{6,2},{3,7},{7,3},{8,12},{12,8},{9,1... | collective-permute-start | bytes 1572872 | tf_op jit(solution)/shard_map/ppermute | solution.py:275
  163.2 14.8 %all-to-all-start.5 = ((f32[4,64,640]{2,1,0:T(8,128)}), f32[4,64,640]{2,1,0:T(8,128)}, u32[]{:S(2)}, u32[]{:S(2)}) async-start(f32[4,64,640]{2,1,0:T(8,128)} %get-tuple-element.33), calls=%async_computation.5 | async-start | bytes 1310720 | tf_op jit(solution)/shard_map/all_to_all | solution.py:285

commit v5 on v4

--- a/solution.py
+++ b/solution.py
@@ -123,7 +123,7 @@
         out_specs=[IN_HBM, IN_VMEM],
         out_shape=(sds((NY, R, WIDE)), sds((2, R, HALF))),
         scratch_shapes=[pltpu.VMEM((R, WIDE), f32), pltpu.SemaphoreType.DMA((NY,))],
-        compiler_params=params(3400 << 10),
+        compiler_params=params(40 << 20),
     )(qt, half, other)
 
 
@@ -238,12 +238,18 @@
         return lax.dynamic_slice(terms, (block, n, 0, 0), (1, 1, HALF, KVC)).reshape(HALF, KVC)
 
     seconds = [lax.ppermute(take(near[n], n), "y", pairs[n]) for n in range(2)]
-    onward = [
-        lax.ppermute((firsts[n].astype(f32) + take(near[1 - n], n).astype(f32)).astype(bf16), "y", pairs[1 - n])
+    sent = []
+    for n in range(2):
+        sent.append((firsts[n].astype(f32) + take(near[1 - n], n).astype(f32)).astype(bf16))
+        if n == 0:
+            firsts[1], _ = lax.optimization_barrier((firsts[1], sent[0]))
+    onward = [lax.ppermute(sent[n], "y", pairs[1 - n]) for n in range(2)]
+    terms, error, _ = lax.optimization_barrier((terms, error, sent[1]))
+    bases = [
+        error[n * HALF : (n + 1) * HALF] + scale * (take(y, n).astype(f32) + seconds[n].astype(f32))
         for n in range(2)
     ]
-    owns = [error[n * HALF : (n + 1) * HALF] + scale * take(y, n).astype(f32) for n in range(2)]
-    bases = [lax.optimization_barrier(owns[n] + scale * seconds[n].astype(f32)) for n in range(2)]
+    bases = [lax.optimization_barrier(base) for base in bases]
     return [bases[n] + scale * onward[n].astype(f32) for n in range(2)]
 
 
@@ -257,20 +263,25 @@
     keep = jnp.where(core == 0, low, high)
     rest = jnp.where(core == 0, high, low)
 
-    give, weight = lax.optimization_barrier((rest.astype(bf16), weight))
-    pair = (keep + lax.ppermute(give, "core", SWAP).astype(f32)) * (1.0 / (NX * NZ * NC))
+    pair = (keep + lax.ppermute(rest.astype(bf16), "core", SWAP).astype(f32)) * (1.0 / (NX * NZ * NC))
     along_x = lax.all_to_all(pair.astype(bf16).reshape(NX, 128, KVC), "x", 0, 0, tiled=True)
+    row = jnp.sum(along_x.astype(f32), axis=0).astype(bf16)
     mine = lax.dynamic_slice_in_dim(weight, core * HALF, HALF, 0)
-    pieces = [mine] + [
-        lax.ppermute(mine, "y", [(i, (i + s) % NY) for i in range(NY)]) for s in range(1, NY)
-    ]
-    along_x, pieces[1], pieces[3] = lax.optimization_barrier((along_x, pieces[1], pieces[3]))
-    row = jnp.sum(along_x.astype(f32), axis=0).astype(bf16)
+    row, mine = lax.optimization_barrier((row, mine))
+
+    def turn(rows, s):
+        return lax.ppermute(rows, "y", [(i, (i + s) % NY) for i in range(NY)])
+
+    after, before = turn(mine, 1), turn(mine, 3)
     along_z = lax.all_to_all(row.reshape(NZ, 16, KVC), "z", 0, 0, tiled=True)
-    along_z, pieces[2] = lax.optimization_barrier((along_z, pieces[2]))
+    along_z, after, before = lax.optimization_barrier((along_z, after, before))
     rows = jnp.sum(along_z.astype(f32), axis=0)
+    rows, mine = lax.optimization_barrier((rows, mine))
+    facing = turn(mine, 2)
     block = everyone(rows, "z", NZ).reshape(128, KVC)
     half = everyone(block, "x", NX).reshape(HALF, KVC)
+    half, facing = lax.optimization_barrier((half, facing))
+    pieces = [mine, after, facing, before]
     other = lax.ppermute(half, "core", SWAP)
     others = [lax.ppermute(piece, "core", SWAP) for piece in pieces]
     source = (y - jnp.arange(NY)) % NY

time: 188 us -> 174 us (0.926)
  waiting for transfers between devices: 64.5 us -> 50.2 us
  blocking collectives: 28.3 us -> 32.8 us
  starting transfers between devices: 33.5 us -> 29.8 us
  local copies, waits for them, and re-layouts: 3.3 us -> 6.38 us
  matrix products: 8.8 us -> 6.66 us
    all_to_all x0 -> x1, blocking collectives: none -> 17.3 us  [body(): along_z = lax.all_to_all(row.reshape(NZ, 16, KVC), 'z', 0, 0, tiled=True)]
    all_to_all x2 -> x1, blocking collectives: 28.3 us -> 15.5 us  [everyone(): lax.all_to_all(jnp.broadcast_to(t, (n, *t.shape)), axis, 0, 0, tiled=True)]
    all_to_all x1, waiting for transfers between devices: 9.06 us -> 0.01 us  [everyone(): lax.all_to_all(jnp.broadcast_to(t, (n, *t.shape)), axis, 0, 0, tiled=True)]
    ppermute x6, waiting for transfers between devices: 29.8 us -> 21.6 us  [the longest x3 11.8 us: turn(): return lax.ppermute(rows, 'y', [(i, (i + s) % NY) for i in range(NY)])]
    all_to_all x1, waiting for transfers between devices: 0.01 us -> 7.48 us  [body(): lax.all_to_all(pair.astype(bf16).reshape(NX, 128, KVC), 'x', 0, 0, tiled=...]
    ppermute x2, waiting for transfers between devices: 9.82 us -> 5.33 us  [scatter_y(): seconds = [lax.ppermute(take(near[n], n), 'y', pairs[n]) for n in range(2)]]
    all_to_all x1, starting transfers between devices: 8.47 us -> 4.95 us  [everyone(): lax.all_to_all(jnp.broadcast_to(t, (n, *t.shape)), axis, 0, 0, tiled=True)]
    dot_general x2, matrix products: 8.8 us -> 6.66 us  [term(): jnp.einsum('tr,tk->rk', rows, cot, preferred_element_type=f32).astype(bf16)]
  transfers between devices with their start and end apart: 19 -> 19, of which waited for: 12 -> 11; matrix products, arithmetic and copies ran while one was open for 7% -> 9% of each run, Pallas kernels for 11% -> 11%
where the time goes in v5:
time: 174 us; the launch traced here: 173 us
  waiting for transfers between devices  50.2 us (29%)
  Pallas kernels  33 us (19%)
  blocking collectives  32.8 us (19%)
  starting transfers between devices  29.8 us (17%)
  other arithmetic  12.6 us (7%)
  matrix products  6.66 us (4%)
  local copies, waits for them, and re-layouts  6.38 us (4%)
    all_to_all x1, blocking collectives, body(): along_z = lax.all_to_all(row.reshape(NZ, 16, KVC), 'z', 0, 0, tiled=True)  17.3 us
    all_to_all x1, blocking collectives, everyone(): lax.all_to_all(jnp.broadcast_to(t, (n, *t.shape)), axis, 0, 0, tiled=True)  15.5 us
    ppermute x3, waiting for transfers between devices, turn(): return lax.ppermute(rows, 'y', [(i, (i + s) % NY) for i in range(NY)])  11.8 us
    pallas_call x2, Pallas kernels, input_grad_of(): pl.pallas_call(input_grad_kernel, name='input_grad', grid_spec=pltpu.Pref...  10.8 us
    pallas_call x1, Pallas kernels, following(): pl.pallas_call(next_kernel, name='following', in_specs=[IN_VMEM, IN_HBM,...  8.94 us
    pallas_call x1, Pallas kernels, last(): pl.pallas_call(last_kernel, name='last', grid_spec=pltpu.PrefetchScalarGr...  8.27 us
    ppermute x2, waiting for transfers between devices, scatter_y(): onward = [lax.ppermute(sent[n], 'y', pairs[1 - n]) for n in range(2)]  7.87 us
    all_to_all x1, waiting for transfers between devices, body(): lax.all_to_all(pair.astype(bf16).reshape(NX, 128, KVC), 'x', 0, 0, tiled=...  7.48 us
  transfers between devices with their start and end apart: 19, of which 11 were waited for; matrix products, arithmetic and copies ran while one was open for 9% of the time, Pallas kernels for 11%

profile of v5, /device:TPU:2, one launch (start us, length us, event | category | flops | bytes accessed | tf_op | source)
XLA Modules:
  0.0 173.0 jit_solution(16199213673794214572)
XLA Ops:
  0.7 2.3 %convolution_convert_fusion.1 = bf16[1024,512]{1,0:T(8,128)(2,1)S(1)} fusion(bf16[512,512]{1,0:T(8,128)(2,1)} %cot_ref.3, bf16[512,4096]{1,0:T(8,128)(2,1)} %param.6, s32[]{:T(128)S(6)} %select_n.39), kind=kOutput, calls=%fused_computation.1 | convolution fusion | flops 537395200 | bytes 2621444 | tf_op jit(solution)/shard_map/tr,tk->rk/dot_general | solution.py:228
  5.6 2.2 %collective-permute-start = (bf16[512,512]{1,0:T(8,128)(2,1)}, bf16[512,512]{1,0:T(8,128)(2,1)}, u32[]{:S(2)}, u32[]{:S(2)}) collective-permute-start(bf16[512,512]{1,0:T(8,128)(2,1)} %get-tuple-element.57), channel_id=1, source_target_pairs={{0,3},{1,2},{2,1},{3,0},{4,7},{5,6},{6,5},{7,4},{8,11},{9,10},{10,... | collective-permute-start | bytes 1572872 | tf_op jit(solution)/shard_map/ppermute | solution.py:234
  7.8 4.4 %convolution_convert_fusion = bf16[4096,512]{1,0:T(8,128)(2,1)} fusion(bf16[512,4096]{1,0:T(8,128)(2,1)S(1)} %copy-done.6, bf16[512,512]{1,0:T(8,128)(2,1)S(1)} %copy-done.5), kind=kOutput, calls=%fused_computation | convolution fusion | flops 2149580800 | bytes 8912896 | tf_op jit(solution)/shard_map/tr,tk->rk/dot_general | solution.py:228
  12.2 2.4 %dynamic-slice_bitcast_fusion = (bf16[512,512]{1,0:T(8,128)(2,1)}, bf16[512,512]{1,0:T(8,128)(2,1)}) fusion(bf16[4,2,512,512]{3,2,1,0:T(8,128)(2,1)} %bitcast.33, s32[]{:T(128)S(6)} %select_n.40, s32[]{:T(128)S(6)} %select_n.41), kind=kLoop, calls=%fused_computation.18 | loop fusion | bytes 2097160 | tf_op jit(solution)/shard_map/reshape | solution.py:238
  15.6 2.8 %collective-permute-done.1 = bf16[512,512]{1,0:T(8,128)(2,1)} collective-permute-done((bf16[512,512]{1,0:T(8,128)(2,1)}, bf16[512,512]{1,0:T(8,128)(2,1)}, u32[]{:S(2)}, u32[]{:S(2)}) %collective-permute-start.1) | collective-permute-done | bytes 524320 | tf_op jit(solution)/shard_map/ppermute | solution.py:234
  18.4 2.1 %fusion.5 = bf16[512,512]{1,0:T(8,128)(2,1)} fusion(bf16[512,512]{1,0:T(8,128)(2,1)} %collective-permute-done.1, bf16[4,2,512,512]{3,2,1,0:T(8,128)(2,1)} %bitcast.34, s32[]{:T(128)S(6)} %select_n.40), kind=kLoop, calls=%fused_computation.11 | loop fusion | flops 1048576 | bytes 1572868 | tf_op jit(solution)/shard_map/convert_element_type | solution.py:243
  21.9 2.1 %fusion.4 = bf16[512,512]{1,0:T(8,128)(2,1)} fusion(bf16[512,512]{1,0:T(8,128)(2,1)} %collective-permute-done, bf16[4,2,512,512]{3,2,1,0:T(8,128)(2,1)} %bitcast.35, s32[]{:T(128)S(6)} %select_n.41), kind=kLoop, calls=%fused_computation.9 | loop fusion | flops 1048576 | bytes 1572868 | tf_op jit(solution)/shard_map/convert_element_type | solution.py:243
  24.9 2.2 %collective-permute-start.3 = (bf16[512,512]{1,0:T(8,128)(2,1)}, bf16[512,512]{1,0:T(8,128)(2,1)}, u32[]{:S(2)}, u32[]{:S(2)}) collective-permute-start(bf16[512,512]{1,0:T(8,128)(2,1)} %fusion.5), channel_id=1, source_target_pairs={{0,3},{1,2},{2,1},{3,0},{4,7},{5,6},{6,5},{7,4},{8,11},{9,10},{10,... | collective-permute-start | bytes 1572872 | tf_op jit(solution)/shard_map/ppermute | solution.py:246
  27.8 5.3 %collective-permute-done.4 = bf16[512,512]{1,0:T(8,128)(2,1)} collective-permute-done((bf16[512,512]{1,0:T(8,128)(2,1)}, bf16[512,512]{1,0:T(8,128)(2,1)}, u32[]{:S(2)}, u32[]{:S(2)}) %collective-permute-start.4) | collective-permute-done | bytes 524320 | tf_op jit(solution)/shard_map/ppermute | solution.py:240
  33.1 1.9 %fusion.1 = (f32[512,512]{1,0:T(8,128)S(1)}, f32[512,512]{1,0:T(8,128)S(1)}) fusion(bf16[512,512]{1,0:T(8,128)(2,1)} %collective-permute-done.4, f32[1024,512]{1,0:T(8,128)S(1)} %bitcast.37, bf16[4,2,512,512]{3,2,1,0:T(8,128)(2,1)} %bitcast.36, s32[]{:T(128)S(6)} %select_n.42, f32[]{:T(128)S(6)} %copy.12, bf16[512,512]{1,0:T(8,128)(2,1)} %collective-permute-done.2), kind=kLoop, calls=%fused_computation.4 | loop fusion | flops 2621440 | bytes 6291464 | tf_op jit(solution)/shard_map/add | solution.py:249
  35.1 5.4 %collective-permute-done.5 = bf16[512,512]{1,0:T(8,128)(2,1)} collective-permute-done((bf16[512,512]{1,0:T(8,128)(2,1)}, bf16[512,512]{1,0:T(8,128)(2,1)}, u32[]{:S(2)}, u32[]{:S(2)}) %collective-permute-start.5) | collective-permute-done | bytes 524320 | tf_op jit(solution)/shard_map/ppermute | solution.py:246
  40.4 2.5 %collective-permute-done.3 = bf16[512,512]{1,0:T(8,128)(2,1)} collective-permute-done((bf16[512,512]{1,0:T(8,128)(2,1)}, bf16[512,512]{1,0:T(8,128)(2,1)}, u32[]{:S(2)}, u32[]{:S(2)}) %collective-permute-start.3) | collective-permute-done | bytes 524320 | tf_op jit(solution)/shard_map/ppermute | solution.py:246
  43.0 2.5 %fusion.13 = (bf16[512,512]{1,0:T(8,128)(2,1)S(1)}, f32[512,512]{1,0:T(8,128)}) fusion(f32[512,512]{1,0:T(8,128)S(1)} %get-tuple-element.53, bf16[512,512]{1,0:T(8,128)(2,1)} %collective-permute-done.3, f32[512,512]{1,0:T(8,128)S(1)} %get-tuple-element.52, bf16[512,512]{1,0:T(8,128)(2,1)} %collective-permute-done.5, f32[]{:T(128)S(6)} %copy.12, pred[]{:T(512)S(6)} %eq.6), kind=kLoop, calls=%fused_computation.30 | loop fusion | flops 2097152 | bytes 4718597 | tf_op jit(solution)/shard_map/convert_element_type | solution.py:266
  45.5 1.9 %collective-permute-done.6 = bf16[512,512]{1,0:T(8,128)(2,1)S(1)} collective-permute-done((bf16[512,512]{1,0:T(8,128)(2,1)S(1)}, bf16[512,512]{1,0:T(8,128)(2,1)S(1)}, u32[]{:S(2)}, u32[]{:S(2)}) %collective-permute-start.6) | collective-permute-done | bytes 524320 | tf_op jit(solution)/shard_map/ppermute | solution.py:266
  47.4 2.8 %multiply_convert_fusion = (bf16[512,512]{1,0:T(8,128)(2,1)}, f32[512,512]{1,0:T(8,128)}) fusion(bf16[512,512]{1,0:T(8,128)(2,1)S(1)} %collective-permute-done.6, f32[512,512]{1,0:T(8,128)S(1)} %get-tuple-element.52, bf16[512,512]{1,0:T(8,128)(2,1)} %collective-permute-done.5, f32[512,512]{1,0:T(8,128)S(1)} %get-tuple-element.53, ...), kind=kLoop, calls=%fused_computation.12 | loop fusion | flops 2883584 | bytes 5242885 | tf_op jit(solution)/shard_map/convert_element_type | solution.py:267
  50.1 4.9 %all-to-all-start = ((bf16[4,128,512]{2,1,0:T(8,128)(2,1)}), bf16[4,128,512]{2,1,0:T(8,128)(2,1)S(1)}, u32[]{:S(2)}, u32[]{:S(2)}) async-start(bf16[4,128,512]{2,1,0:T(8,128)(2,1)} %bitcast.8), calls=%async_computation | async-start | bytes 1048576 | tf_op jit(solution)/shard_map/all_to_all | solution.py:267
  55.9 7.5 %all-to-all-done = bf16[4,128,512]{2,1,0:T(8,128)(2,1)S(1)} async-done(((bf16[4,128,512]{2,1,0:T(8,128)(2,1)}), bf16[4,128,512]{2,1,0:T(8,128)(2,1)S(1)}, u32[]{:S(2)}, u32[]{:S(2)}) %all-to-all-start) | async-done | bytes 524320 | tf_op jit(solution)/shard_map/all_to_all | solution.py:267
  63.5 2.3 %collective-permute-start.8 = (bf16[512,512]{1,0:T(8,128)(2,1)}, bf16[512,512]{1,0:T(8,128)(2,1)}, u32[]{:S(2)}, u32[]{:S(2)}) collective-permute-start(bf16[512,512]{1,0:T(8,128)(2,1)} %constant_dynamic-slice_fusion.w0), channel_id=1, source_target_pairs={{0,3},{1,0},{2,1},{3,2},{4,7},{5,4},{6,5},{7,6},{8,11},{9,8},{10,9... | collective-permute-start | bytes 1572872 | tf_op jit(solution)/shard_map/ppermute | solution.py:273
  65.7 17.3 %all_to_all.30 = bf16[8,16,512]{2,1,0:T(8,128)(2,1)S(1)} all-to-all(bf16[8,16,512]{2,1,0:T(8,128)(2,1)S(1)} %bitcast.39), channel_id=1, replica_groups=mesh['x'=4,'z'=8,'core'=2,'y'=4] {'z'}, dimensions={0} | all-to-all | bytes 262144 | tf_op jit(solution)/shard_map/all_to_all | solution.py:276
  83.1 15.5 %all_to_all.31 = f32[8,16,512]{2,1,0:T(8,128)S(1)} all-to-all(f32[8,16,512]{2,1,0:T(8,128)S(1)} %broadcast_in_dim.12), channel_id=1, replica_groups=mesh['x'=4,'z'=8,'core'=2,'y'=4] {'z'}, dimensions={0} | all-to-all | bytes 524288 | tf_op jit(solution)/shard_map/all_to_all | solution.py:257
  99.7 4.9 %all-to-all-start.3 = ((f32[4,128,512]{2,1,0:T(8,128)}), f32[4,128,512]{2,1,0:T(8,128)S(1)}, u32[]{:S(2)}, u32[]{:S(2)}) async-start(f32[4,128,512]{2,1,0:T(8,128)} %broadcast_in_dim.13), calls=%async_computation.3 | async-start | bytes 2097152 | tf_op jit(solution)/shard_map/all_to_all | solution.py:257
  104.7 11.8 %collective-permute-done.11.w2 = bf16[512,512]{1,0:T(8,128)(2,1)} collective-permute-done((bf16[512,512]{1,0:T(8,128)(2,1)}, bf16[512,512]{1,0:T(8,128)(2,1)}, u32[]{:S(2)}, u32[]{:S(2)}) %collective-permute-start.11) | collective-permute-done | bytes 524320 | tf_op jit(solution)/shard_map/ppermute | solution.py:273
  116.5 2.7 %collective-permute-done.14.other_ref.other_hbm = f32[512,512]{1,0:T(8,128)S(1)} collective-permute-done((f32[512,512]{1,0:T(8,128)S(1)}, f32[512,512]{1,0:T(8,128)S(1)}, u32[]{:S(2)}, u32[]{:S(2)}) %collective-permute-start.14) | collective-permute-done | bytes 1048608 | tf_op jit(solution)/shard_map/ppermute | solution.py:285
  119.2 5.0 %first.1 = (f32[4,64,640]{2,1,0:T(8,128)}, f32[2,64,512]{2,1,0:T(8,128)}) custom-call(f32[64,512]{1,0:T(8,128)S(1)} %bitcast.32, f32[512,512]{1,0:T(8,128)S(1)} %bitcast.30, f32[512,512]{1,0:T(8,128)S(1)} %collective-permute-done.14.other_ref.other_hbm), custom_call_target="tpu_custom_call" | custom-call | tf_op jit(solution)/shard_map/first/pallas_call | solution.py:119
  125.1 4.2 %all-to-all-start.4 = ((f32[4,64,640]{2,1,0:T(8,128)}), f32[4,64,640]{2,1,0:T(8,128)}, u32[]{:S(2)}, u32[]{:S(2)}) async-start(f32[4,64,640]{2,1,0:T(8,128)} %get-tuple-element.40), calls=%async_computation.4 | async-start | bytes 1310720 | tf_op jit(solution)/shard_map/all_to_all | solution.py:292
  130.9 5.4 %input_grad.2.refs_0_ = bf16[512,4096]{1,0:T(8,128)(2,1)} custom-call(s32[4]{0:T(128)} %broadcast_add_fusion.at_ref, bf16[512,512]{1,0:T(8,128)(2,1)} %cot_ref.3, bf16[512,512]{1,0:T(8,128)(2,1)} %constant_dynamic-slice_fusion.w0, bf16[512,512]{1,0:T(8,128)(2,1)} %collective-permute-done.7.w1, bf16[512,512]{1,0:T(8,128)(2,1)} %collective-permute-done.11.w2, ...), custom_call_target="tpu_custom_call" | custom-call | flops 1073741824 | bytes 5242880 | tf_op jit(solution)/shard_map/input_grad/pallas_call | solution.py:210
  136.3 4.5 %all-to-all-done.4.got_ref = f32[4,64,640]{2,1,0:T(8,128)} async-done(((f32[4,64,640]{2,1,0:T(8,128)}), f32[4,64,640]{2,1,0:T(8,128)}, u32[]{:S(2)}, u32[]{:S(2)}) %all-to-all-start.4) | async-done | bytes 655392 | tf_op jit(solution)/shard_map/all_to_all | solution.py:292
  140.8 8.9 %following.1 = (f32[4,64,640]{2,1,0:T(8,128)}, f32[2,64,512]{2,1,0:T(8,128)}) custom-call(f32[4,64,640]{2,1,0:T(8,128)} %all-to-all-done.4.got_ref, f32[512,512]{1,0:T(8,128)} %bitcast.31, f32[512,512]{1,0:T(8,128)} %copy-done.2), custom_call_target="tpu_custom_call" | custom-call | tf_op jit(solution)/shard_map/following/pallas_call | solution.py:131
  149.7 4.4 %all-to-all-start.5 = ((f32[4,64,640]{2,1,0:T(8,128)}), f32[4,64,640]{2,1,0:T(8,128)}, u32[]{:S(2)}, u32[]{:S(2)}) async-start(f32[4,64,640]{2,1,0:T(8,128)} %get-tuple-element.43), calls=%async_computation.5 | async-start | bytes 1310720 | tf_op jit(solution)/shard_map/all_to_all | solution.py:296
  154.7 5.4 %input_grad.3 = bf16[512,4096]{1,0:T(8,128)(2,1)} custom-call(s32[4]{0:T(128)} %add_subtract_fusion.at_ref, bf16[512,512]{1,0:T(8,128)(2,1)} %cot_ref.3, bf16[512,512]{1,0:T(8,128)(2,1)} %collective-permute-done.9.w0, bf16[512,512]{1,0:T(8,128)(2,1)} %collective-permute-done.10.w1, ...), custom_call_target="tpu_custom_call", output_to_operand_aliasing={{}: (6, {})} | custom-call | flops 1073741824 | bytes 5242880 | tf_op jit(solution)/shard_map/input_grad/pallas_call | solution.py:210
  160.1 4.5 %all-to-all-done.5.got_ref = f32[4,64,640]{2,1,0:T(8,128)} async-done(((f32[4,64,640]{2,1,0:T(8,128)}), f32[4,64,640]{2,1,0:T(8,128)}, u32[]{:S(2)}, u32[]{:S(2)}) %all-to-all-start.5) | async-done | bytes 655392 | tf_op jit(solution)/shard_map/all_to_all | solution.py:296
  164.6 8.3 %last.1 = (f32[1024,512]{1,0:T(8,128)}, f32[1024,512]{1,0:T(8,128)}, f32[64,512]{1,0:T(8,128)}) custom-call(s32[1]{0:T(128)} %bitcast.13.core_ref, f32[4,64,640]{2,1,0:T(8,128)} %all-to-all-done.5.got_ref, f32[2,64,512]{2,1,0:T(8,128)} %get-tuple-element.44.p_ref, f32[512,512]{1,0:T(8,128)} %get-tuple-element.49.keep_hbm, f32[512,512]{1,0:T(8,128)} %get-tuple-element.51.rest_hbm), custom_call_target="tpu_custom_call" | custom-call | tf_op jit(solution)/shard_map/last/pallas_call | solution.py:177
  (43 shorter events, 11.2 us)
Async XLA Ops:
  0.6 54.4 %copy-start = (bf16[1024,512]{1,0:T(8,128)(2,1)S(1)}, bf16[1024,512]{1,0:T(8,128)(2,1)}, u32[]{:S(2)}) copy-start(bf16[1024,512]{1,0:T(8,128)(2,1)} %param.8) | copy-start | bytes 3145732
  0.6 7.1 %copy-start.5 = (bf16[512,512]{1,0:T(8,128)(2,1)S(1)}, bf16[512,512]{1,0:T(8,128)(2,1)}, u32[]{:S(2)}) copy-start(bf16[512,512]{1,0:T(8,128)(2,1)} %cot_ref.3) | copy-start | bytes 1572868
  0.7 7.1 %copy-start.6 = (bf16[512,4096]{1,0:T(8,128)(2,1)S(1)}, bf16[512,4096]{1,0:T(8,128)(2,1)}, u32[]{:S(2)}) copy-start(bf16[512,4096]{1,0:T(8,128)(2,1)} %param.6) | copy-start | bytes 12582916
  4.0 14.4 %collective-permute-start.1 = (bf16[512,512]{1,0:T(8,128)(2,1)}, bf16[512,512]{1,0:T(8,128)(2,1)}, u32[]{:S(2)}, u32[]{:S(2)}) collective-permute-start(bf16[512,512]{1,0:T(8,128)(2,1)} %get-tuple-element.56), channel_id=1, source_target_pairs={{0,1},{1,0},{2,3},{3,2},{4,5},{5,4},{6,7},{7,6},{8,9},{9,8},{10,11... | collective-permute-start | bytes 1572872 | tf_op jit(solution)/shard_map/ppermute | solution.py:234
  5.6 16.3 %collective-permute-start = (bf16[512,512]{1,0:T(8,128)(2,1)}, bf16[512,512]{1,0:T(8,128)(2,1)}, u32[]{:S(2)}, u32[]{:S(2)}) collective-permute-start(bf16[512,512]{1,0:T(8,128)(2,1)} %get-tuple-element.57), channel_id=1, source_target_pairs={{0,3},{1,2},{2,1},{3,0},{4,7},{5,6},{6,5},{7,4},{8,11},{9,10},{10,... | collective-permute-start | bytes 1572872 | tf_op jit(solution)/shard_map/ppermute | solution.py:234
  12.2 21.0 %copy-start.4 = (f32[1,1024,512]{2,1,0:T(8,128)S(1)}, f32[1,1024,512]{2,1,0:T(8,128)}, u32[]{:S(2)}) copy-start(f32[1,1024,512]{2,1,0:T(8,128)} %param.9) | copy-start | bytes 6291460
  14.5 18.6 %collective-permute-start.4 = (bf16[512,512]{1,0:T(8,128)(2,1)}, bf16[512,512]{1,0:T(8,128)(2,1)}, u32[]{:S(2)}, u32[]{:S(2)}) collective-permute-start(bf16[512,512]{1,0:T(8,128)(2,1)} %get-tuple-element.54), channel_id=1, source_target_pairs={{0,3},{1,2},{2,1},{3,0},{4,7},{5,6},{6,5},{7,4},{8,11},{9,10},{10,... | collective-permute-start | bytes 1572872 | tf_op jit(solution)/shard_map/ppermute | solution.py:240
  15.6 17.5 %collective-permute-start.2 = (bf16[512,512]{1,0:T(8,128)(2,1)}, bf16[512,512]{1,0:T(8,128)(2,1)}, u32[]{:S(2)}, u32[]{:S(2)}) collective-permute-start(bf16[512,512]{1,0:T(8,128)(2,1)} %get-tuple-element.55), channel_id=1, source_target_pairs={{0,1},{1,0},{2,3},{3,2},{4,5},{5,4},{6,7},{7,6},{8,9},{9,8},{10,11... | collective-permute-start | bytes 1572872 | tf_op jit(solution)/shard_map/ppermute | solution.py:240
  24.0 16.4 %collective-permute-start.5 = (bf16[512,512]{1,0:T(8,128)(2,1)}, bf16[512,512]{1,0:T(8,128)(2,1)}, u32[]{:S(2)}, u32[]{:S(2)}) collective-permute-start(bf16[512,512]{1,0:T(8,128)(2,1)} %fusion.4), channel_id=1, source_target_pairs={{0,1},{1,0},{2,3},{3,2},{4,5},{5,4},{6,7},{7,6},{8,9},{9,8},{10,11... | collective-permute-start | bytes 1572872 | tf_op jit(solution)/shard_map/ppermute | solution.py:246
  24.9 18.0 %collective-permute-start.3 = (bf16[512,512]{1,0:T(8,128)(2,1)}, bf16[512,512]{1,0:T(8,128)(2,1)}, u32[]{:S(2)}, u32[]{:S(2)}) collective-permute-start(bf16[512,512]{1,0:T(8,128)(2,1)} %fusion.5), channel_id=1, source_target_pairs={{0,3},{1,2},{2,1},{3,0},{4,7},{5,6},{6,5},{7,4},{8,11},{9,10},{10,... | collective-permute-start | bytes 1572872 | tf_op jit(solution)/shard_map/ppermute | solution.py:246
  45.5 1.9 %collective-permute-start.6 = (bf16[512,512]{1,0:T(8,128)(2,1)S(1)}, bf16[512,512]{1,0:T(8,128)(2,1)S(1)}, u32[]{:S(2)}, u32[]{:S(2)}) collective-permute-start(bf16[512,512]{1,0:T(8,128)(2,1)S(1)} %get-tuple-element.50), channel_id=1, source_target_pairs={{0,4},{4,0},{1,5},{5,1},{2,6},{6,2},{3,7},{7,3},{8,12},{12,8},{9,1... | collective-permute-start | bytes 1572872 | tf_op jit(solution)/shard_map/ppermute | solution.py:266
  50.1 69.0 %copy-start.3 = (f32[512,64]{0,1:T(8,128)S(1)}, f32[512,64]{0,1:T(8,128)}, u32[]{:S(2)}) copy-start(f32[512,64]{0,1:T(8,128)} %param.10) | copy-start | bytes 393220
  50.1 13.3 %all-to-all-start = ((bf16[4,128,512]{2,1,0:T(8,128)(2,1)}), bf16[4,128,512]{2,1,0:T(8,128)(2,1)S(1)}, u32[]{:S(2)}, u32[]{:S(2)}) async-start(bf16[4,128,512]{2,1,0:T(8,128)(2,1)} %bitcast.8), calls=%async_computation | async-start | bytes 1048576 | tf_op jit(solution)/shard_map/all_to_all | solution.py:267
  63.5 19.6 %collective-permute-start.8 = (bf16[512,512]{1,0:T(8,128)(2,1)}, bf16[512,512]{1,0:T(8,128)(2,1)}, u32[]{:S(2)}, u32[]{:S(2)}) collective-permute-start(bf16[512,512]{1,0:T(8,128)(2,1)} %constant_dynamic-slice_fusion.w0), channel_id=1, source_target_pairs={{0,3},{1,0},{2,1},{3,2},{4,7},{5,4},{6,5},{7,6},{8,11},{9,8},{10,9... | collective-permute-start | bytes 1572872 | tf_op jit(solution)/shard_map/ppermute | solution.py:273
  65.7 17.3 %collective-permute-start.7 = (bf16[512,512]{1,0:T(8,128)(2,1)}, bf16[512,512]{1,0:T(8,128)(2,1)}, u32[]{:S(2)}, u32[]{:S(2)}) collective-permute-start(bf16[512,512]{1,0:T(8,128)(2,1)} %constant_dynamic-slice_fusion.w0), channel_id=1, source_target_pairs={{0,1},{1,2},{2,3},{3,0},{4,5},{5,6},{6,7},{7,4},{8,9},{9,10},{10,1... | collective-permute-start | bytes 1572872 | tf_op jit(solution)/shard_map/ppermute | solution.py:273
  99.7 16.8 %all-to-all-start.3 = ((f32[4,128,512]{2,1,0:T(8,128)}), f32[4,128,512]{2,1,0:T(8,128)S(1)}, u32[]{:S(2)}, u32[]{:S(2)}) async-start(f32[4,128,512]{2,1,0:T(8,128)} %broadcast_in_dim.13), calls=%async_computation.3 | async-start | bytes 2097152 | tf_op jit(solution)/shard_map/all_to_all | solution.py:257
  104.7 11.8 %collective-permute-start.11 = (bf16[512,512]{1,0:T(8,128)(2,1)}, bf16[512,512]{1,0:T(8,128)(2,1)}, u32[]{:S(2)}, u32[]{:S(2)}) collective-permute-start(bf16[512,512]{1,0:T(8,128)(2,1)} %constant_dynamic-slice_fusion.w0), channel_id=1, source_target_pairs={{0,2},{1,3},{2,0},{3,1},{4,6},{5,7},{6,4},{7,5},{8,10},{9,11},{10,... | collective-permute-start | bytes 1572872 | tf_op jit(solution)/shard_map/ppermute | solution.py:273
  116.5 19.8 %copy-start.1 = (f32[4,128,512]{2,1,0:T(8,128)}, f32[4,128,512]{2,1,0:T(8,128)S(1)}, u32[]{:S(2)}) copy-start(f32[4,128,512]{2,1,0:T(8,128)S(1)} %all-to-all-done.3) | copy-start | bytes 3145732
  116.5 2.7 %collective-permute-start.14 = (f32[512,512]{1,0:T(8,128)S(1)}, f32[512,512]{1,0:T(8,128)S(1)}, u32[]{:S(2)}, u32[]{:S(2)}) collective-permute-start(f32[512,512]{1,0:T(8,128)S(1)} %bitcast.29), channel_id=1, source_target_pairs={{0,4},{4,0},{1,5},{5,1},{2,6},{6,2},{3,7},{7,3},{8,12},{12,8},{9,1... | collective-permute-start | bytes 3145736 | tf_op jit(solution)/shard_map/ppermute | solution.py:285
  124.1 1.0 copy-start.2
  125.1 15.7 %all-to-all-start.4 = ((f32[4,64,640]{2,1,0:T(8,128)}), f32[4,64,640]{2,1,0:T(8,128)}, u32[]{:S(2)}, u32[]{:S(2)}) async-start(f32[4,64,640]{2,1,0:T(8,128)} %get-tuple-element.40), calls=%async_computation.4 | async-start | bytes 1310720 | tf_op jit(solution)/shard_map/all_to_all | solution.py:292
  129.3 25.4 %collective-permute-start.9 = (bf16[512,512]{1,0:T(8,128)(2,1)}, bf16[512,512]{1,0:T(8,128)(2,1)}, u32[]{:S(2)}, u32[]{:S(2)}) collective-permute-start(bf16[512,512]{1,0:T(8,128)(2,1)} %constant_dynamic-slice_fusion.w0), channel_id=1, source_target_pairs={{0,4},{4,0},{1,5},{5,1},{2,6},{6,2},{3,7},{7,3},{8,12},{12,8},{9,1... | collective-permute-start | bytes 1572872 | tf_op jit(solution)/shard_map/ppermute | solution.py:286
  129.5 25.2 %collective-permute-start.10 = (bf16[512,512]{1,0:T(8,128)(2,1)}, bf16[512,512]{1,0:T(8,128)(2,1)}, u32[]{:S(2)}, u32[]{:S(2)}) collective-permute-start(bf16[512,512]{1,0:T(8,128)(2,1)} %collective-permute-done.7.w1), channel_id=1, source_target_pairs={{0,4},{4,0},{1,5},{5,1},{2,6},{6,2},{3,7},{7,3},{8,12},{12,8},{9,1... | collective-permute-start | bytes 1572872 | tf_op jit(solution)/shard_map/ppermute | solution.py:286
  129.9 24.8 %collective-permute-start.13 = (bf16[512,512]{1,0:T(8,128)(2,1)}, bf16[512,512]{1,0:T(8,128)(2,1)}, u32[]{:S(2)}, u32[]{:S(2)}) collective-permute-start(bf16[512,512]{1,0:T(8,128)(2,1)} %collective-permute-done.8.w3), channel_id=1, source_target_pairs={{0,4},{4,0},{1,5},{5,1},{2,6},{6,2},{3,7},{7,3},{8,12},{12,8},{9,1... | collective-permute-start | bytes 1572872 | tf_op jit(solution)/shard_map/ppermute | solution.py:286
  130.0 24.7 %collective-permute-start.12 = (bf16[512,512]{1,0:T(8,128)(2,1)}, bf16[512,512]{1,0:T(8,128)(2,1)}, u32[]{:S(2)}, u32[]{:S(2)}) collective-permute-start(bf16[512,512]{1,0:T(8,128)(2,1)} %collective-permute-done.11.w2), channel_id=1, source_target_pairs={{0,4},{4,0},{1,5},{5,1},{2,6},{6,2},{3,7},{7,3},{8,12},{12,8},{9,1... | collective-permute-start | bytes 1572872 | tf_op jit(solution)/shard_map/ppermute | solution.py:286
  149.7 14.9 %all-to-all-start.5 = ((f32[4,64,640]{2,1,0:T(8,128)}), f32[4,64,640]{2,1,0:T(8,128)}, u32[]{:S(2)}, u32[]{:S(2)}) async-start(f32[4,64,640]{2,1,0:T(8,128)} %get-tuple-element.43), calls=%async_computation.5 | async-start | bytes 1310720 | tf_op jit(solution)/shard_map/all_to_all | solution.py:296
